TPU v7x, 128 devices: a whole 4x4x4 slice. The times are simulated.
128 devices in a mesh: pairs: 128 (over x, z, y, core).
Axes of the slice: x: 4, y: 4, z: 4, core: 2. Of those that a mesh axis runs over, the one named last changes fastest.
Arguments:
- blocks: bfloat16 [2048, 512, 512], P('pairs'), may hold values from -6 to 6
- pair_orbitals: int32 [4096, 2], replicated, may hold values from 0 to 2047, as said below
- block_sizes: int32 [2048], replicated, may hold values from 256 to 512, as said below
- pno_maps: bfloat16 [4096, 512, 128], P('pairs'), may hold values from -0.25 to 0.25
- pno_sizes: int32 [4096], P('pairs'), may hold values from 32 to 128, as said below
- pno_energy: float32 [4096, 128], P('pairs'), may hold values from 0.3 to 3
- pair_shift: float32 [4096], P('pairs'), may hold values from 0.5 to 2
- neighbours: int32 [4096, 8], P('pairs'), may hold values from 0 to 4095, as said below
- intersections: bfloat16 [4096, 8, 128, 128], P('pairs'), may hold values from -0.5 to 0.5
Outputs:
- amplitudes: float32 [4096, 128, 128], P('pairs')
- pair_energy: float32 [4096], P('pairs')
Inputs may be any that keep to these rules, and one draw needn't show every extreme that they name: `pair_orbitals`: pair p is owned by device p // 32; its first orbital is one of the 16 orbitals that this device holds (orbital o is held by device o // 16), and its second orbital is held by the owner or by one of the two devices next to it. On every device but the first, its first owned pair takes its second orbital from the device on the left; on every device but the last, its second owned pair takes it from the device on the right. `neighbours`: every listed coupled pair is owned by the pair's owner or by one of the two devices next to it. `block_sizes`: some orbital has all 512 rows live in every draw. `pno_sizes`: some pair has all 128 natural orbitals live in every draw.
All inputs are finite; a program needn't handle non-finite values.
Results may differ from a plain program's by a relative error of at most 0.0038.
Values may be sent and summed in bfloat16 or wider, within the bound.
No kernel may reach another device: no remote copies, remote signals or barrier semaphores. Data moves between devices by JAX's collectives and lax.ppermute only.
A program may use at most 192 MiB of HBM per device.

v0:
```python
import math

import jax
import jax.numpy as jnp
from jax import lax
from jax.sharding import PartitionSpec as P

ITERS = 2


coupling_weight = 0.35


def extended_2(block, sides, width):
    for axis, dim in sides:
        count = lax.axis_size(axis)
        forward = [(i, i + 1) for i in range(count - 1)]
        backward = [(target, source) for source, target in forward]
        low = lax.ppermute(
            lax.slice_in_dim(block, block.shape[dim] - width, None, axis=dim), axis, forward
        )
        high = lax.ppermute(lax.slice_in_dim(block, 0, width, axis=dim), axis, backward)
        block = jnp.concatenate([low, block, high], axis=dim)
    return block


def shards(
    blocks,
    pair_orbitals,
    block_sizes,
    pno_maps,
    pno_sizes,
    pno_energy,
    pair_shift,
    neighbours,
    intersections,
):
    largest_value = lax.Precision.HIGHEST
    pair_count = pno_maps.shape[0]
    orbital_count = blocks.shape[0]
    aux_count = blocks.shape[1]
    pno_count = pno_maps.shape[2]
    device = lax.axis_index("pairs")
    first_pair = device * pair_count
    first_orbital = device * orbital_count
    owned = lax.dynamic_slice_in_dim(pair_orbitals, first_pair, pair_count, 0)
    orbital_one = owned[:, 0]
    orbital_two = owned[:, 1]
    aux_rows = jnp.arange(aux_count, dtype=jnp.int32)
    local_pno_sizes = lax.dynamic_slice_in_dim(block_sizes, first_orbital, orbital_count, 0)
    keep_rows = aux_rows[None, :] < local_pno_sizes[:, None]
    masked = jnp.where(keep_rows[:, :, None], blocks, jnp.zeros((), jnp.bfloat16))
    left_half_slice = jnp.einsum(
        "zde,zen->zdn",
        masked[orbital_one - first_orbital],
        pno_maps,
        preferred_element_type=jnp.float32,
    ).astype(jnp.bfloat16)
    extended = extended_2(masked, (("pairs", 0),), orbital_count)
    right_half_slice = jnp.einsum(
        "zde,zen->zdn",
        extended[orbital_two - first_orbital + orbital_count],
        pno_maps,
        preferred_element_type=jnp.float32,
    ).astype(jnp.bfloat16)
    integrals = jnp.einsum(
        "pqa,pqb->pab", left_half_slice, right_half_slice, preferred_element_type=jnp.float32
    ) * (1.0 / math.sqrt(aux_count))
    pno_index = jnp.arange(pno_count, dtype=jnp.int32)
    live = pno_index[None, :] < pno_sizes[:, None]
    pno_mask = live[:, :, None] & live[:, None, :]
    denominator = pno_energy[:, :, None] + pno_energy[:, None, :] + pair_shift[:, None, None]
    amplitudes = jnp.where(pno_mask, -integrals / denominator, jnp.zeros((), jnp.float32))
    local_index = neighbours - first_pair + pair_count
    intersection_factor = intersections.astype(jnp.float32)
    for iteration in range(ITERS):
        extended_amps = extended_2(amplitudes, (("pairs", 0),), pair_count)
        nearby = extended_amps[local_index]
        mixed = jnp.einsum("pnac,pncd->pnad", intersection_factor, nearby, precision=largest_value)
        coupling = jnp.einsum("pnad,pnbd->pab", mixed, intersection_factor, precision=largest_value)
        amplitudes = jnp.where(
            pno_mask,
            -(integrals + coupling_weight * coupling) / denominator,
            jnp.zeros((), jnp.float32),
        )
    pair_energy = jnp.sum(integrals * amplitudes, axis=(1, 2)) / (pno_count * pno_count)
    return (amplitudes, pair_energy)


def solution(mesh):
    in_specs = (
        P("pairs", None, None),
        P(),
        P(),
        P("pairs", None, None),
        P("pairs"),
        P("pairs", None),
        P("pairs"),
        P("pairs", None),
        P("pairs", None, None, None),
    )
    out_specs = (P("pairs", None, None), P("pairs"))
    return jax.shard_map(shards, mesh=mesh, in_specs=in_specs, out_specs=out_specs, check_vma=False)
```

profile of v0, /device:TPU:6, one launch (start us, length us, event | category | flops | bytes accessed | tf_op | source)
XLA Modules:
  0.0 334.5 jit_solution(1990087227682212177)
XLA Ops:
  0.6 0.0 copy-start
  0.7 0.8 dynamic_slice.6
  1.4 0.1 iota_compare_fusion
  1.5 7.4 %broadcast_select_fusion = bf16[16,512,512]{2,1,0:T(8,128)(2,1)} fusion(bf16[16,512,512]{2,1,0:T(8,128)(2,1)} %param.9, pred[16,512]{1,0:T(8,128)(4,1)S(1)} %iota_compare_fusion), kind=kLoop, calls=%fused_computation.9 | loop fusion | flops 4194304 | bytes 16785408 | tf_op jit(solution)/shard_map/jit(_where)/select_n | solution.py:52
  8.9 1.9 collective-permute-start
  10.8 8.1 %collective-permute-start.1 = (bf16[16,512,512]{2,1,0:T(8,128)(2,1)}, bf16[16,512,512]{2,1,0:T(8,128)(2,1)}, u32[]{:S(2)}, u32[]{:S(2)}) collective-permute-start(bf16[16,512,512]{2,1,0:T(8,128)(2,1)} %broadcast_select_fusion), channel_id=1, source_target_pairs={{1,0},{2,1},{3,2},{4,3},{5,4},{6,5},{7,6},{8,7},{9,8},{10,9},{11,1... | collective-permute-start | bytes 25165832 | tf_op jit(solution)/shard_map/ppermute | solution.py:22
  18.9 0.0 copy-done
  18.9 0.1 constant_dynamic-slice_fusion
  19.0 0.0 copy-start.5
  19.0 10.6 %gather_fusion = bf16[32,512,512]{2,1,0:T(8,128)(2,1)} fusion(bf16[16,512,512]{2,1,0:T(8,128)(2,1)} %broadcast_select_fusion, s32[1024]{0:T(1024)S(1)} %get-tuple-element.9), kind=kCustom, calls=%fused_computation | custom fusion | bytes 33554560 | tf_op jit(solution)/shard_map/gather | solution.py:55
  29.6 0.0 copy-done.5
  29.6 0.1 iota_compare_fusion.1
  29.7 78.7 %collective-permute-done = bf16[16,512,512]{2,1,0:T(8,128)(2,1)} collective-permute-done((bf16[16,512,512]{2,1,0:T(8,128)(2,1)}, bf16[16,512,512]{2,1,0:T(8,128)(2,1)}, u32[]{:S(2)}, u32[]{:S(2)}) %collective-permute-start) | collective-permute-done | bytes 8388640 | tf_op jit(solution)/shard_map/ppermute | solution.py:19
  108.4 1.8 collective-permute-done.1
  110.2 17.5 %pad_maximum_fusion = bf16[48,512,512]{2,1,0:T(8,128)(2,1)} fusion(bf16[16,512,512]{2,1,0:T(8,128)(2,1)} %collective-permute-done.1, bf16[16,512,512]{2,1,0:T(8,128)(2,1)} %broadcast_select_fusion, bf16[16,512,512]{2,1,0:T(8,128)(2,1)} %collective-permute-done), kind=kLoop, calls=%fused_computation.4 | loop fusion | flops 25165824 | bytes 50331648 | tf_op jit(solution)/shard_map/concatenate | solution.py:23
  127.7 0.0 copy-start.2
  127.7 0.0 copy-start.4
  127.8 15.4 %gather_fusion.1 = bf16[32,512,512]{2,1,0:T(8,128)(2,1)} fusion(bf16[48,512,512]{2,1,0:T(8,128)(2,1)} %pad_maximum_fusion, s32[1024]{0:T(1024)S(1)} %get-tuple-element.8), kind=kCustom, calls=%fused_computation.1 | custom fusion | bytes 33554560 | tf_op jit(solution)/shard_map/gather | solution.py:62
  143.2 0.0 copy-done.2
  143.2 0.0 copy-done.4
  143.2 0.0 copy-start.3
  143.2 22.7 %and_select_fusion.2 = (f32[32,128,128]{2,1,0:T(8,128)}, f32[32,128,128]{2,1,0:T(8,128)S(1)}) fusion(f32[32]{0:T(128)S(1)} %copy-done.4, f32[32,128]{1,0:T(8,128)S(1)} %copy-done.2, pred[32,128]{1,0:T(8,128)(4,1)S(1)} %iota_compare_fusion.1, bf16[32,512,512]{2,1,0:T(8,128)(2,1)} %gather_fusion.1, bf16[32,512,128]{2,1,0:T(8,128)(2,1)} %param.12, ...), kind=kOutput, calls=%fused_computation.19 | convolution fusion | flops 4839702528 | bytes 41963648 | tf_op jit(solution)/shard_map/pqa,pqb->pab/dot_general | solution.py:66
  165.9 1.9 collective-permute-start.2
  167.8 8.2 %collective-permute-start.3 = (f32[32,128,128]{2,1,0:T(8,128)}, f32[32,128,128]{2,1,0:T(8,128)}, u32[]{:S(2)}, u32[]{:S(2)}) collective-permute-start(f32[32,128,128]{2,1,0:T(8,128)} %get-tuple-element.4), channel_id=1, source_target_pairs={{1,0},{2,1},{3,2},{4,3},{5,4},{6,5},{7,6},{8,7},{9,8},{10,9},{11,1... | collective-permute-start | bytes 6291464 | tf_op jit(solution)/shard_map/ppermute | solution.py:22
  176.0 0.0 copy-done.3
  176.0 0.1 copy.11
  176.1 0.1 reshape.82
  176.2 21.7 %collective-permute-done.2 = f32[32,128,128]{2,1,0:T(8,128)} collective-permute-done((f32[32,128,128]{2,1,0:T(8,128)}, f32[32,128,128]{2,1,0:T(8,128)}, u32[]{:S(2)}, u32[]{:S(2)}) %collective-permute-start.2) | collective-permute-done | bytes 2097184 | tf_op jit(solution)/shard_map/ppermute | solution.py:19
  197.9 1.8 collective-permute-done.3
  199.7 6.3 %pad_maximum_fusion.1 = f32[96,128,128]{2,1,0:T(8,128)} fusion(f32[32,128,128]{2,1,0:T(8,128)} %collective-permute-done.3, f32[32,128,128]{2,1,0:T(8,128)} %get-tuple-element.4, f32[32,128,128]{2,1,0:T(8,128)} %collective-permute-done.2), kind=kLoop, calls=%fused_computation.10 | loop fusion | flops 3145728 | bytes 12582912 | tf_op jit(solution)/shard_map/concatenate | solution.py:23
  206.0 14.7 %gather_fusion.2 = f32[256,128,128]{2,1,0:T(8,128)} fusion(f32[96,128,128]{2,1,0:T(8,128)} %pad_maximum_fusion.1, s32[1024]{0:T(1024)S(1)} %pad_clamp_fusion), kind=kCustom, calls=%fused_computation.2 | custom fusion | bytes 33555456 | tf_op jit(solution)/shard_map/gather | solution.py:78
  220.7 18.0 %fusion.23 = f32[32,8,128,128]{2,3,1,0:T(8,128)} fusion(f32[32,8,128,128]{3,2,1,0:T(8,128)} %bitcast.51, bf16[32,8,128,128]{3,2,1,0:T(8,128)(2,1)} %param.17), kind=kOutput, calls=%fused_computation.42 | convolution fusion | flops 6442450944 | bytes 41943040 | tf_op jit(solution)/shard_map/pnac,pncd->pnad/dot_general | solution.py:79
  238.6 12.4 %and_select_fusion.1 = f32[32,128,128]{2,1,0:T(8,128)S(1)} fusion(f32[32,128,128]{2,1,0:T(8,128)S(1)} %get-tuple-element.5, bf16[32,8,128,128]{3,2,1,0:T(8,128)(2,1)} %param.17, f32[32,8,128,128]{2,3,1,0:T(8,128)} %fusion.23, f32[32]{0:T(128)S(1)} %copy-done.4, f32[32,128]{1,0:T(8,128)S(1)} %copy-done.2, pred[32,128]{1,0:T(8,128)(4,1)S(1)} %iota_compare_fusion.1), kind=kOutput, calls=%fused_computation.18 | convolution fusion | flops 6447169536 | bytes 29380736 | tf_op jit(solution)/shard_map/pnad,pnbd->pab/dot_general | solution.py:80
  251.1 1.9 collective-permute-start.4
  253.0 8.3 %collective-permute-start.5 = (f32[32,128,128]{2,1,0:T(8,128)S(1)}, f32[32,128,128]{2,1,0:T(8,128)S(1)}, u32[]{:S(2)}, u32[]{:S(2)}) collective-permute-start(f32[32,128,128]{2,1,0:T(8,128)S(1)} %and_select_fusion.1), channel_id=1, source_target_pairs={{1,0},{2,1},{3,2},{4,3},{5,4},{6,5},{7,6},{8,7},{9,8},{10,9},{11,1... | collective-permute-start | bytes 6291464 | tf_op jit(solution)/shard_map/ppermute | solution.py:22
  261.3 21.6 %collective-permute-done.4 = f32[32,128,128]{2,1,0:T(8,128)S(1)} collective-permute-done((f32[32,128,128]{2,1,0:T(8,128)S(1)}, f32[32,128,128]{2,1,0:T(8,128)S(1)}, u32[]{:S(2)}, u32[]{:S(2)}) %collective-permute-start.4) | collective-permute-done | bytes 2097184 | tf_op jit(solution)/shard_map/ppermute | solution.py:19
  282.8 1.8 collective-permute-done.5
  284.6 3.1 pad_maximum_fusion.2
  287.7 14.7 %gather_fusion.3 = f32[256,128,128]{2,1,0:T(8,128)} fusion(f32[96,128,128]{2,1,0:T(8,128)} %pad_maximum_fusion.2, s32[1024]{0:T(1024)S(1)} %pad_clamp_fusion), kind=kCustom, calls=%fused_computation.3 | custom fusion | bytes 33555456 | tf_op jit(solution)/shard_map/gather | solution.py:78
  302.4 18.0 %fusion.24 = f32[32,8,128,128]{2,3,1,0:T(8,128)} fusion(f32[32,8,128,128]{3,2,1,0:T(8,128)} %bitcast.50, bf16[32,8,128,128]{3,2,1,0:T(8,128)(2,1)} %param.17), kind=kOutput, calls=%fused_computation.43 | convolution fusion | flops 6442450944 | bytes 41943040 | tf_op jit(solution)/shard_map/pnac,pncd->pnad/dot_general | solution.py:79
  320.4 0.0 copy-start.1
  320.4 13.6 %multiply_reduce_fusion = (f32[32]{0:T(128)S(1)}, f32[32,128,128]{2,1,0:T(8,128)}) fusion(f32[32,128,128]{2,1,0:T(8,128)S(1)} %get-tuple-element.5, f32[32]{0:T(128)S(1)} %copy-done.4, f32[32,128]{1,0:T(8,128)S(1)} %copy-done.2, bf16[32,8,128,128]{3,2,1,0:T(8,128)(2,1)} %param.17, f32[32,8,128,128]{2,3,1,0:T(8,128)} %fusion.24, ...), kind=kOutput, calls=%fused_computation.28 | convolution fusion | flops 6448218112 | bytes 29380864 | tf_op jit(solution)/shard_map/pnad,pnbd->pab/dot_general | solution.py:80
  334.0 0.5 broadcast_multiply_fusion
  334.5 0.0 copy-done.1
  (4 shorter events, 0.0 us)
Async XLA Ops:
  0.6 18.3 %copy-start = (s32[4096,2]{0,1:T(2,128)S(1)}, s32[4096,2]{0,1:T(2,128)}, u32[]{:S(2)}) copy-start(s32[4096,2]{0,1:T(2,128)} %param.10) | copy-start | bytes 98308
  8.9 99.5 %collective-permute-start = (bf16[16,512,512]{2,1,0:T(8,128)(2,1)}, bf16[16,512,512]{2,1,0:T(8,128)(2,1)}, u32[]{:S(2)}, u32[]{:S(2)}) collective-permute-start(bf16[16,512,512]{2,1,0:T(8,128)(2,1)} %broadcast_select_fusion), channel_id=1, source_target_pairs={{0,1},{1,2},{2,3},{3,4},{4,5},{5,6},{6,7},{7,8},{8,9},{9,10},{10,1... | collective-permute-start | bytes 25165832 | tf_op jit(solution)/shard_map/ppermute | solution.py:19
  10.8 99.4 %collective-permute-start.1 = (bf16[16,512,512]{2,1,0:T(8,128)(2,1)}, bf16[16,512,512]{2,1,0:T(8,128)(2,1)}, u32[]{:S(2)}, u32[]{:S(2)}) collective-permute-start(bf16[16,512,512]{2,1,0:T(8,128)(2,1)} %broadcast_select_fusion), channel_id=1, source_target_pairs={{1,0},{2,1},{3,2},{4,3},{5,4},{6,5},{7,6},{8,7},{9,8},{10,9},{11,1... | collective-permute-start | bytes 25165832 | tf_op jit(solution)/shard_map/ppermute | solution.py:22
  19.0 10.6 %copy-start.5 = (s32[32]{0:T(128)S(1)}, s32[32]{0:T(128)}, u32[]{:S(2)}) copy-start(s32[32]{0:T(128)} %param.13) | copy-start | bytes 388
  127.7 15.5 %copy-start.2 = (f32[32,128]{1,0:T(8,128)S(1)}, f32[32,128]{1,0:T(8,128)}, u32[]{:S(2)}) copy-start(f32[32,128]{1,0:T(8,128)} %param.14) | copy-start | bytes 49156
  127.7 15.5 %copy-start.4 = (f32[32]{0:T(128)S(1)}, f32[32]{0:T(128)}, u32[]{:S(2)}) copy-start(f32[32]{0:T(128)} %param.15) | copy-start | bytes 388
  143.2 32.8 %copy-start.3 = (s32[32,8]{0,1:T(8,128)S(1)}, s32[32,8]{0,1:T(8,128)}, u32[]{:S(2)}) copy-start(s32[32,8]{0,1:T(8,128)} %param.16) | copy-start | bytes 3076
  165.9 32.0 %collective-permute-start.2 = (f32[32,128,128]{2,1,0:T(8,128)}, f32[32,128,128]{2,1,0:T(8,128)}, u32[]{:S(2)}, u32[]{:S(2)}) collective-permute-start(f32[32,128,128]{2,1,0:T(8,128)} %get-tuple-element.4), channel_id=1, source_target_pairs={{0,1},{1,2},{2,3},{3,4},{4,5},{5,6},{6,7},{7,8},{8,9},{9,10},{10,1... | collective-permute-start | bytes 6291464 | tf_op jit(solution)/shard_map/ppermute | solution.py:19
  167.8 31.9 %collective-permute-start.3 = (f32[32,128,128]{2,1,0:T(8,128)}, f32[32,128,128]{2,1,0:T(8,128)}, u32[]{:S(2)}, u32[]{:S(2)}) collective-permute-start(f32[32,128,128]{2,1,0:T(8,128)} %get-tuple-element.4), channel_id=1, source_target_pairs={{1,0},{2,1},{3,2},{4,3},{5,4},{6,5},{7,6},{8,7},{9,8},{10,9},{11,1... | collective-permute-start | bytes 6291464 | tf_op jit(solution)/shard_map/ppermute | solution.py:22
  251.1 31.8 %collective-permute-start.4 = (f32[32,128,128]{2,1,0:T(8,128)S(1)}, f32[32,128,128]{2,1,0:T(8,128)S(1)}, u32[]{:S(2)}, u32[]{:S(2)}) collective-permute-start(f32[32,128,128]{2,1,0:T(8,128)S(1)} %and_select_fusion.1), channel_id=1, source_target_pairs={{0,1},{1,2},{2,3},{3,4},{4,5},{5,6},{6,7},{7,8},{8,9},{9,10},{10,1... | collective-permute-start | bytes 6291464 | tf_op jit(solution)/shard_map/ppermute | solution.py:19
  253.0 31.6 %collective-permute-start.5 = (f32[32,128,128]{2,1,0:T(8,128)S(1)}, f32[32,128,128]{2,1,0:T(8,128)S(1)}, u32[]{:S(2)}, u32[]{:S(2)}) collective-permute-start(f32[32,128,128]{2,1,0:T(8,128)S(1)} %and_select_fusion.1), channel_id=1, source_target_pairs={{1,0},{2,1},{3,2},{4,3},{5,4},{6,5},{7,6},{8,7},{9,8},{10,9},{11,1... | collective-permute-start | bytes 6291464 | tf_op jit(solution)/shard_map/ppermute | solution.py:22
  320.4 14.1 %copy-start.1 = (s32[4096,2]{0,1:T(2,128)S(1)}, s32[4096,2]{0,1:T(2,128)}, u32[]{:S(2)}) copy-start(s32[4096,2]{0,1:T(2,128)} %param.10) | copy-start | bytes 98308
where the time goes:
time: 335 us; the launch traced here: 334 us
  waiting for transfers between devices  127 us (38%)
  matrix products  84.6 us (25%)
  local copies, waits for them, and re-layouts  56.5 us (17%)
  other arithmetic  35 us (10%)
  starting transfers between devices  30.3 us (9%)
    ppermute x3, waiting for transfers between devices, extended_2(): lax.ppermute(lax.slice_in_dim(block, block.shape[dim] - width, None, axis...  122 us
    dot_general x2, matrix products, shards(): jnp.einsum('pnac,pncd->pnad', intersection_factor, nearby, precision=larg...  35.9 us
    gather x2, local copies, waits for them, and re-layouts, shards(): nearby = extended_amps[local_index]  29.4 us
    concatenate x3, other arithmetic, extended_2(): block = jnp.concatenate([low, block, high], axis=dim)  26.9 us
    dot_general x2, matrix products, shards(): jnp.einsum('pnad,pnbd->pab', mixed, intersection_factor, precision=larges...  26 us
    ppermute x3, starting transfers between devices, extended_2(): lax.ppermute(lax.slice_in_dim(block, 0, width, axis=dim), axis, backward)  24.6 us
    dot_general x1, matrix products, shards(): jnp.einsum('pqa,pqb->pab', left_half_slice, right_half_slice, preferred_e...  22.7 us
    gather x1, local copies, waits for them, and re-layouts, shards(): extended[orbital_two - first_orbital + orbital_count]  15.4 us
  transfers between devices with their start and end apart: 6, of which 6 were waited for; matrix products, arithmetic and copies ran while one was open for 3% of the time, Pallas kernels for 0%

commit v1 on v0

v1 whole, which is shorter than its diff:
```python
import functools
import math

import jax
import jax.numpy as jnp
from jax import lax
from jax.experimental import pallas as pl
from jax.experimental.pallas import tpu as pltpu
from jax.sharding import PartitionSpec as P

ITERS = 2
COUPLING = 0.35
SLOTS = (16, 18, 20, 24, 32)
GROUP = 8
VMEM_LIMIT = 60 * 1024 * 1024

ANY = pl.BlockSpec(memory_space=pl.ANY)
VMEM = pl.BlockSpec(memory_space=pltpu.VMEM)
SMEM = pl.BlockSpec(memory_space=pltpu.SMEM)

ONE, SRC, SERVE, LIVE, PNO, NEAR = 0, 32, 64, 96, 128, 160


def call(body, outs, out_specs, in_specs, scratch, flops=0, moved=0, aliases=None, name=None):
    return pl.pallas_call(
        body,
        out_shape=outs,
        in_specs=in_specs,
        out_specs=out_specs,
        scratch_shapes=scratch,
        input_output_aliases=aliases or {},
        compiler_params=pltpu.CompilerParams(vmem_limit_bytes=VMEM_LIMIT),
        cost_estimate=pl.CostEstimate(flops=int(flops), bytes_accessed=int(moved), transcendentals=0),
        name=name,
    )


def dot(left, right):
    return jnp.dot(left, right, preferred_element_type=jnp.float32)


def dot_nt(left, right):
    return lax.dot_general(left, right, (((1,), (1,)), ((), ())), preferred_element_type=jnp.float32)


def collect(count, wanted, begin, slots):
    def step(index, found):
        chosen = wanted(index)

        @pl.when(chosen)
        def _():
            slots[found] = index
            begin(index, found)

        return found + chosen.astype(jnp.int32)

    return lax.fori_loop(0, count, step, jnp.int32(0))


def pack_body(first, table, maps, *refs):
    outs, slots, sem = refs[:-2], refs[-2], refs[-1]
    count = maps.shape[0]
    held = [out.shape[0] for out in outs]

    def begin(pair, slot):
        low = 0
        for out, size in zip(outs, held):
            lo, hi = low, low + size

            @pl.when((slot >= lo) & (slot < hi))
            def _(out=out, lo=lo):
                pltpu.make_async_copy(maps.at[pair], out.at[slot - lo], sem.at[slot]).start()

            low = hi

    found = collect(count, lambda p: table[SRC + p] >= 2 * first, begin, slots)

    @pl.loop(0, found)
    def _(slot):
        pltpu.make_async_copy(maps.at[0], outs[0].at[0], sem.at[slot]).wait()


def pack(table, maps, sizes, orbitals):
    count, depth, width = maps.shape
    return call(
        functools.partial(pack_body, orbitals),
        tuple(jax.ShapeDtypeStruct((s, depth, width), maps.dtype) for s in sizes),
        (VMEM,) * len(sizes),
        [SMEM, ANY],
        [pltpu.SMEM((count,), jnp.int32), pltpu.SemaphoreType.DMA((count,))],
        moved=2 * sum(sizes) * depth * width * 2,
        name="pack",
    )(table, maps)


def local_body(scale, table, shift, blocks, maps, energy, left, integ, inverse, start, early, late,
               held, map_held, sem, map_sem):
    orbitals = blocks.shape[0]
    count, _, width = maps.shape
    depth = blocks.shape[1]
    near = 8

    @pl.loop(0, orbitals)
    def _(o):
        pltpu.make_async_copy(blocks.at[o], held.at[o], sem.at[o]).start()

    @pl.loop(0, count)
    def _(p):
        pltpu.make_async_copy(maps.at[p], map_held.at[p], map_sem.at[p]).start()

    def note(entry, counts):
        soon, after = counts
        pair = entry // near
        where = table[NEAR + entry]
        is_late = where >= 2 * count

        @pl.when(is_late)
        def _():
            late[1 + after] = pair * 65536 + entry * 256 + (where - 2 * count)

        @pl.when(jnp.logical_not(is_late))
        def _():
            early[1 + soon] = pair * 65536 + entry * 256 + where

        step = is_late.astype(jnp.int32)
        return soon + 1 - step, after + step

    soon, after = lax.fori_loop(0, count * near, note, (jnp.int32(0), jnp.int32(0)))
    early[0] = soon
    late[0] = after
    for k in range(GROUP):
        early[1 + soon + k] = count * 65536
        late[1 + after + k] = count * 65536

    @pl.loop(0, count)
    def _(p):
        size = table[PNO + p]
        row = jnp.broadcast_to(energy[pl.ds(p, 1), :], (width, width))
        ids = lax.broadcasted_iota(jnp.int32, (width, width), 0)
        idt = lax.broadcasted_iota(jnp.int32, (width, width), 1)
        bottom = row + row.T + shift[p]
        inverse[p] = jnp.where((ids < size) & (idt < size), -1.0 / bottom, 0.0)

    @pl.loop(0, orbitals)
    def _(o):
        pltpu.make_async_copy(blocks.at[0], held.at[0], sem.at[o]).wait()

    @pl.loop(0, count)
    def _(p):
        pltpu.make_async_copy(maps.at[0], map_held.at[0], map_sem.at[p]).wait()
        half = dot(held[table[ONE + p]], map_held[p])
        rows = lax.broadcasted_iota(jnp.int32, (depth, width), 0)
        half = jnp.where(rows < table[LIVE + p], half, 0.0).astype(jnp.bfloat16).T
        left[p] = half
        where = table[SRC + p]

        @pl.when(where < orbitals)
        def _():
            right = dot(held[where], map_held[p]).astype(jnp.bfloat16)
            value = dot(half, right) * scale
            integ[p] = value
            start[p] = (value * inverse[p]).astype(jnp.bfloat16)


def local(table, shift, blocks, maps, energy, scale):
    orbitals, depth, wide = blocks.shape
    count, _, width = maps.shape
    entries = count * 8 + GROUP + 8
    return call(
        functools.partial(local_body, scale),
        (
            jax.ShapeDtypeStruct((count, width, depth), jnp.bfloat16),
            jax.ShapeDtypeStruct((count, width, width), jnp.float32),
            jax.ShapeDtypeStruct((count, width, width), jnp.float32),
            jax.ShapeDtypeStruct((count, width, width), jnp.bfloat16),
            jax.ShapeDtypeStruct((entries,), jnp.int32),
            jax.ShapeDtypeStruct((entries,), jnp.int32),
        ),
        (VMEM, VMEM, VMEM, VMEM, SMEM, SMEM),
        [SMEM, SMEM, ANY, ANY, VMEM],
        [
            pltpu.VMEM((orbitals, depth, wide), jnp.bfloat16),
            pltpu.VMEM((count, wide, width), jnp.bfloat16),
            pltpu.SemaphoreType.DMA((orbitals,)),
            pltpu.SemaphoreType.DMA((count,)),
        ],
        flops=2 * 1.5 * count * depth * wide * width,
        moved=(blocks.size + 2 * maps.size) * 2,
        name="local",
    )(table, shift, blocks, maps, energy)


def serve_body(low, table, blocks, maps, out, held, slots, sem):
    orbitals = blocks.shape[0]
    size = maps.shape[0]
    count = slots.shape[0]

    def begin(pair, found):
        slot = found - low

        @pl.when((slot >= 0) & (slot < size))
        def _():
            pltpu.make_async_copy(blocks.at[table[SERVE + pair]], held.at[slot], sem.at[slot]).start()

    found = collect(
        count,
        lambda p: (table[SERVE + p] >= 0) & (table[SERVE + p] < orbitals),
        begin,
        slots,
    )

    @pl.loop(0, jnp.clip(found - low, 0, size))
    def _(slot):
        pltpu.make_async_copy(blocks.at[0], held.at[0], sem.at[slot]).wait()
        out[slot] = dot(held[slot], maps[slot]).astype(jnp.bfloat16)


def serve(table, blocks, maps, low, count):
    orbitals, depth, wide = blocks.shape
    size, _, width = maps.shape
    return call(
        functools.partial(serve_body, low),
        jax.ShapeDtypeStruct((size, depth, width), jnp.bfloat16),
        VMEM,
        [SMEM, ANY, VMEM],
        [
            pltpu.VMEM((size, depth, wide), jnp.bfloat16),
            pltpu.SMEM((count,), jnp.int32),
            pltpu.SemaphoreType.DMA((size,)),
        ],
        flops=2 * size * depth * wide * width,
        moved=size * depth * (wide + 2 * width) * 2,
        name="serve",
    )(table, blocks, maps)


def beside_body(scale, orbitals, table, blocks, maps, left, inverse, integ_in, start_in, integ, start,
                blk, mp, lf, inv, val, amp, slots, sem, osem):
    del integ_in, start_in
    count = maps.shape[0]

    def copies(pair, slot):
        return (
            pltpu.make_async_copy(blocks.at[table[SRC + pair] - orbitals], blk.at[slot], sem.at[0, slot]),
            pltpu.make_async_copy(maps.at[pair], mp.at[slot], sem.at[1, slot]),
            pltpu.make_async_copy(left.at[pair], lf.at[slot], sem.at[2, slot]),
            pltpu.make_async_copy(inverse.at[pair], inv.at[slot], sem.at[3, slot]),
        )

    def begin(pair, slot):
        for copy in copies(pair, slot):
            copy.start()

    def results(pair, slot):
        return (
            pltpu.make_async_copy(val.at[slot], integ.at[pair], osem.at[0, slot]),
            pltpu.make_async_copy(amp.at[slot], start.at[pair], osem.at[1, slot]),
        )

    found = collect(
        count,
        lambda p: (table[SRC + p] >= orbitals) & (table[SRC + p] < 2 * orbitals),
        begin,
        slots,
    )

    @pl.loop(0, found)
    def _(slot):
        pair = slots[slot]
        for copy in copies(pair, slot):
            copy.wait()
        right = dot(blk[slot], mp[slot]).astype(jnp.bfloat16)
        value = dot(lf[slot], right) * scale
        val[slot] = value
        amp[slot] = (value * inv[slot]).astype(jnp.bfloat16)
        for copy in results(pair, slot):
            copy.start()

    @pl.loop(0, found)
    def _(slot):
        for copy in results(slots[slot], slot):
            copy.wait()


def beside(table, blocks, maps, left, inverse, integ, start, scale):
    orbitals, depth, wide = blocks.shape
    count, _, width = maps.shape
    return call(
        functools.partial(beside_body, scale, orbitals),
        (
            jax.ShapeDtypeStruct(integ.shape, integ.dtype),
            jax.ShapeDtypeStruct(start.shape, start.dtype),
        ),
        (ANY, ANY),
        [SMEM, ANY, ANY, ANY, ANY, ANY, ANY],
        [
            pltpu.VMEM((count, depth, wide), jnp.bfloat16),
            pltpu.VMEM((count, wide, width), jnp.bfloat16),
            pltpu.VMEM((count, width, depth), jnp.bfloat16),
            pltpu.VMEM((count, width, width), jnp.float32),
            pltpu.VMEM((count, width, width), jnp.float32),
            pltpu.VMEM((count, width, width), jnp.bfloat16),
            pltpu.SMEM((count,), jnp.int32),
            pltpu.SemaphoreType.DMA((4, count)),
            pltpu.SemaphoreType.DMA((2, count)),
        ],
        flops=count * depth * wide * width,
        moved=count * depth * wide,
        aliases={5: 0, 6: 1},
        name="beside",
    )(table, blocks, maps, left, inverse, integ, start)


def across_body(scale, orbitals, table, *refs):
    n = len(refs) - 13
    halves = refs[:n]
    left, inverse, _, _, integ, start, rt, lf, inv, val, amp, slots, sem = refs[n:]
    count = left.shape[0]

    def copies(pair, slot):
        return (
            pltpu.make_async_copy(left.at[pair], lf.at[slot], sem.at[1, slot]),
            pltpu.make_async_copy(inverse.at[pair], inv.at[slot], sem.at[2, slot]),
        )

    def begin(pair, slot):
        low = 0
        for half in halves:
            lo, hi = low, low + half.shape[0]

            @pl.when((slot >= lo) & (slot < hi))
            def _(half=half, lo=lo):
                pltpu.make_async_copy(half.at[slot - lo], rt.at[slot], sem.at[0, slot]).start()

            low = hi
        for copy in copies(pair, slot):
            copy.start()

    def results(pair, slot):
        return (
            pltpu.make_async_copy(val.at[slot], integ.at[pair], sem.at[3, slot]),
            pltpu.make_async_copy(amp.at[slot], start.at[pair], sem.at[4, slot]),
        )

    found = collect(count, lambda p: table[SRC + p] >= 2 * orbitals, begin, slots)

    @pl.loop(0, found)
    def _(slot):
        pair = slots[slot]
        pltpu.make_async_copy(halves[0].at[0], rt.at[slot], sem.at[0, slot]).wait()
        for copy in copies(pair, slot):
            copy.wait()
        value = dot(lf[slot], rt[slot]) * scale
        val[slot] = value
        amp[slot] = (value * inv[slot]).astype(jnp.bfloat16)
        for copy in results(pair, slot):
            copy.start()

    @pl.loop(0, found)
    def _(slot):
        for copy in results(slots[slot], slot):
            copy.wait()


def across(table, halves, left, inverse, integ, start, scale, orbitals):
    count, width, depth = left.shape
    n = len(halves)
    return call(
        functools.partial(across_body, scale, orbitals),
        (
            jax.ShapeDtypeStruct(integ.shape, integ.dtype),
            jax.ShapeDtypeStruct(start.shape, start.dtype),
        ),
        (ANY, ANY),
        [SMEM] + [ANY] * (n + 4),
        [
            pltpu.VMEM((count, depth, width), jnp.bfloat16),
            pltpu.VMEM((count, width, depth), jnp.bfloat16),
            pltpu.VMEM((count, width, width), jnp.float32),
            pltpu.VMEM((count, width, width), jnp.float32),
            pltpu.VMEM((count, width, width), jnp.bfloat16),
            pltpu.SMEM((count,), jnp.int32),
            pltpu.SemaphoreType.DMA((5, count)),
        ],
        flops=count * depth * width * width,
        moved=count * depth * width * 2,
        aliases={n + 3: 0, n + 4: 1},
        name="across",
    )(table, *halves, left, inverse, integ, start)


CHUNK = 4


def gather_coupling(listed, inter, tables, total, held, amps, sem, tsem):
    near = 8
    chunks = inter.shape[0] // (CHUNK * near)
    rows = CHUNK * near
    number = listed[0]
    for k, tab in enumerate(tables):
        size = tab.shape[0]
        pltpu.make_async_copy(tab, amps.at[pl.ds(k * size, size)], tsem.at[k]).start()

    @pl.loop(0, chunks)
    def _(c):
        pltpu.make_async_copy(
            inter.at[pl.ds(c * rows, rows)], held.at[pl.ds(c * rows, rows)], sem.at[c]
        ).start()

    def wait_chunk(c):
        pltpu.make_async_copy(inter.at[pl.ds(0, rows)], held.at[pl.ds(0, rows)], sem.at[c]).wait()

    def ready():
        for k, tab in enumerate(tables):
            size = tab.shape[0]
            pltpu.make_async_copy(tab, amps.at[pl.ds(k * size, size)], tsem.at[k]).wait()

    def group(g, waited):
        codes = [listed[1 + g * GROUP + k] for k in range(GROUP)]
        last = codes[0] // 65536
        for code in codes[1:]:
            last = jnp.maximum(last, jnp.minimum(code // 65536, 31))
        need = jnp.minimum(last // CHUNK + 1, chunks)

        @pl.loop(waited, need)
        def _(c):
            wait_chunk(c)

        mixed = []
        for code in codes:
            entry = (code // 256) % 256
            mixed.append(dot(held[entry], amps[code % 256]).astype(jnp.bfloat16))
        for code, part in zip(codes, mixed):
            entry = (code // 256) % 256
            total[code // 65536] += dot_nt(part, held[entry])
        return jnp.maximum(waited, need)

    return ready, group, wait_chunk, chunks, number


def early_body(listed, inter, here, beside_, integ, out, total, held, amps, sem, tsem):
    count = integ.shape[0]
    ready, group, wait_chunk, chunks, number = gather_coupling(
        listed, inter, (here, beside_), total, held, amps, sem, tsem
    )

    @pl.loop(0, count)
    def _(p):
        total[p] = jnp.zeros(total.shape[1:], jnp.float32)

    total[count] = jnp.zeros(total.shape[1:], jnp.float32)
    ready()
    waited = lax.fori_loop(0, (number + GROUP - 1) // GROUP, group, jnp.int32(0))
    pl.loop(waited, chunks)(wait_chunk)

    @pl.loop(0, count)
    def _(p):
        out[p] = integ[p] + COUPLING * total[p]


def late_body(final, listed, inter, other, so_far, inverse, *refs):
    if final:
        integ, out, energy, total, held, amps, sem, tsem = refs
    else:
        out, total, held, amps, sem, tsem = refs
    count = so_far.shape[0]
    ready, group, wait_chunk, chunks, number = gather_coupling(
        listed, inter, (other,), total, held, amps, sem, tsem
    )

    @pl.loop(0, count)
    def _(p):
        total[p] = jnp.zeros(total.shape[1:], jnp.float32)

    total[count] = jnp.zeros(total.shape[1:], jnp.float32)
    ready()
    waited = lax.fori_loop(0, (number + GROUP - 1) // GROUP, group, jnp.int32(0))
    pl.loop(waited, chunks)(wait_chunk)

    @pl.loop(0, count)
    def _(p):
        value = (so_far[p] + COUPLING * total[p]) * inverse[p]
        out[p] = value.astype(out.dtype)
        if final:
            energy[pl.ds(p, 1), :] = jnp.sum(integ[p] * value, axis=0, keepdims=True)


def coupling_scratch(count, entries, width, tables):
    chunks = count // CHUNK
    return [
        pltpu.VMEM((count + 1, width, width), jnp.float32),
        pltpu.VMEM((entries, width, width), jnp.bfloat16),
        pltpu.VMEM((tables * count, width, width), jnp.bfloat16),
        pltpu.SemaphoreType.DMA((chunks,)),
        pltpu.SemaphoreType.DMA((tables,)),
    ]


def early_part(listed, inter, here, other, integ):
    count, width, _ = integ.shape
    return call(
        early_body,
        jax.ShapeDtypeStruct(integ.shape, jnp.float32),
        VMEM,
        [SMEM, ANY, ANY, ANY, VMEM],
        coupling_scratch(count, inter.shape[0], width, 2),
        flops=2 * inter.shape[0] * width**3,
        moved=inter.size * 2,
        name="early",
    )(listed, inter, here, other, integ)


def late_part(listed, inter, other, so_far, inverse, integ=None):
    count, width, _ = so_far.shape
    final = integ is not None
    outs = jax.ShapeDtypeStruct(so_far.shape, jnp.float32 if final else jnp.bfloat16)
    args = (listed, inter, other, so_far, inverse)
    if final:
        outs = (outs, jax.ShapeDtypeStruct((count, width), jnp.float32))
        args += (integ,)
    return call(
        functools.partial(late_body, final),
        outs,
        (VMEM, VMEM) if final else VMEM,
        [SMEM, ANY, ANY] + [VMEM] * (len(args) - 3),
        coupling_scratch(count, inter.shape[0], width, 1),
        flops=inter.shape[0] * width**3,
        moved=inter.size * 2,
        name="late",
    )(*args)


def shards(
    blocks,
    pair_orbitals,
    block_sizes,
    pno_maps,
    pno_sizes,
    pno_energy,
    pair_shift,
    neighbours,
    intersections,
):
    devices = lax.axis_size("pairs")
    count, wide, width = pno_maps.shape
    orbitals, depth, _ = blocks.shape
    near = neighbours.shape[1]
    scale = 1.0 / math.sqrt(depth)
    device = lax.axis_index("pairs")
    side = 2 * (device % 2) - 1
    partner = device + side

    beside_perm = [(i, i ^ 1) for i in range(devices)]
    across_perm = []
    for i in range(1, devices - 1, 2):
        across_perm += [(i, i + 1), (i + 1, i)]
    swap_beside = lambda x: lax.ppermute(x, "pairs", beside_perm)
    swap_across = lambda x: lax.ppermute(x, "pairs", across_perm)

    def place(local_index, size):
        offset = jnp.where(local_index < 0, -1, jnp.where(local_index >= size, 1, 0))
        kind = jnp.where(offset == 0, 0, jnp.where(offset == side, 2, 1))
        return kind * size + local_index % size

    owner = jnp.arange(devices, dtype=jnp.int32)
    owner_across = owner + 2 * (owner % 2) - 1
    second = pair_orbitals[:, 1].reshape(devices, count)
    crossing = jnp.sum((second // orbitals == owner_across[:, None]).astype(jnp.int32), axis=1)
    most = jnp.max(crossing)
    branch = sum((most > s).astype(jnp.int32) for s in SLOTS[:-1])

    mine = lax.dynamic_slice_in_dim(pair_orbitals, device * count, count, 0)
    theirs = lax.dynamic_slice_in_dim(
        pair_orbitals, jnp.clip(partner, 0, devices - 1) * count, count, 0
    )
    valid = (partner >= 0) & (partner < devices)
    base = device * orbitals
    one = mine[:, 0] - base
    two = mine[:, 1] - base
    window = lax.dynamic_slice_in_dim(jnp.pad(block_sizes, (orbitals, orbitals)), base, 3 * orbitals, 0)
    hot = jnp.arange(3 * orbitals, dtype=jnp.int32)[None, :]
    size_of = lambda ids: jnp.sum(jnp.where(hot == ids[:, None] + orbitals, window[None, :], 0), axis=1)
    table = jnp.concatenate(
        [
            one,
            place(two, orbitals),
            jnp.where(valid, theirs[:, 1] - base, -1),
            jnp.minimum(size_of(one), size_of(two)),
            pno_sizes,
            place((neighbours - device * count).reshape(-1), count),
        ]
    )
    inter = intersections.reshape(count * near, width, width)

    def integrals_with(slots):
        def run(table, blocks, maps, energy, shift):
            sizes = (slots // 2, slots - slots // 2)
            packed = pack(table, maps, sizes, orbitals)
            got = [swap_across(x) for x in packed]
            blocks_beside = swap_beside(blocks)
            left, integ, inverse, start, early, late = local(table, shift, blocks, maps, energy, scale)
            halves = []
            low = 0
            for x in got:
                half = serve(table, blocks, x, low, count)
                low += x.shape[0]
                halves.append(half)
            back = [swap_across(x) for x in halves]
            integ, _ = lax.optimization_barrier((integ, halves[-1]))
            integ, start = beside(table, blocks_beside, maps, left, inverse, integ, start, scale)
            integ, start = across(table, back, left, inverse, integ, start, scale, orbitals)
            return integ, start, inverse, early, late

        return run

    integ, amps, inverse, early, late = lax.switch(
        branch,
        [integrals_with(s) for s in SLOTS],
        table,
        blocks,
        pno_maps,
        pno_energy,
        pair_shift,
    )
    for iteration in range(ITERS):
        far = swap_across(amps)
        close = swap_beside(amps)
        so_far = early_part(early, inter, amps, close, integ)
        if iteration < ITERS - 1:
            amps = late_part(late, inter, far, so_far, inverse)
        else:
            amps, energies = late_part(late, inter, far, so_far, inverse, integ)
    pair_energy = jnp.sum(energies, axis=1) / (width * width)
    return (amps, pair_energy)


def solution(mesh):
    in_specs = (
        P("pairs", None, None),
        P(),
        P(),
        P("pairs", None, None),
        P("pairs"),
        P("pairs", None),
        P("pairs"),
        P("pairs", None),
        P("pairs", None, None, None),
    )
    out_specs = (P("pairs", None, None), P("pairs"))
    return jax.shard_map(shards, mesh=mesh, in_specs=in_specs, out_specs=out_specs, check_vma=False)
```

time: 335 us -> 176 us (0.53)
  the two profiles are of different devices: /device:TPU:6 before, /device:TPU:4 now
where the time goes in v1:
time: 176 us; the launch traced here: 173 us
  Pallas kernels  113 us (64%)
  starting transfers between devices  32 us (18%)
  waiting for transfers between devices  10.8 us (6%)
  local copies, waits for them, and re-layouts  10.5 us (6%)
  between operations  3.44 us (2%)
  other arithmetic  3.09 us (2%)
    ppermute x6, starting transfers between devices, shards(): swap_across = lambda x: lax.ppermute(x, 'pairs', across_perm)  31.8 us
    pallas_call x2, Pallas kernels, early_part(): call(early_body, jax.ShapeDtypeStruct(integ.shape, jnp.float32), VMEM, [S...  31.5 us
    pallas_call x1, Pallas kernels, local(): call(functools.partial(local_body, scale), (jax.ShapeDtypeStruct((count,...  30 us
    pallas_call x2, Pallas kernels, late_part(): call(functools.partial(late_body, final), outs, (VMEM, VMEM) if final els...  23.1 us
    pallas_call x2, Pallas kernels, serve(): call(functools.partial(serve_body, low), jax.ShapeDtypeStruct((size, dept...  10.8 us
    ppermute x6, waiting for transfers between devices, shards(): swap_across = lambda x: lax.ppermute(x, 'pairs', across_perm)  10.8 us
    pallas_call x1, Pallas kernels, beside(): call(functools.partial(beside_body, scale, orbitals), (jax.ShapeDtypeStru...  8.24 us
    pallas_call x1, Pallas kernels, across(): call(functools.partial(across_body, scale, orbitals), (jax.ShapeDtypeStru...  5.62 us
  transfers between devices with their start and end apart: 9, of which 1 were waited for; matrix products, arithmetic and copies ran while one was open for 0% of the time, Pallas kernels for 49%

profile of v1, /device:TPU:4, one launch (start us, length us, event | category | flops | bytes accessed | tf_op | source)
XLA Modules:
  0.0 173.3 jit_solution(8139997619747280030)
XLA Ops:
  0.7 0.8 slice_reduce_fusion
  1.5 0.8 constant_dynamic-slice_fusion
  2.3 0.7 broadcast_subtract_fusion
  3.0 0.1 copy.32
  3.0 0.1 reshape.39
  3.2 0.1 reshape_squeeze.3
  3.2 0.2 convert_reduce_fusion
  3.4 0.6 reduce_max.9
  6.7 0.8 pad_dynamic-slice_fusion
  7.4 0.2 select_reduce_fusion
  7.7 0.7 concatenate.3
  8.4 95.2 %conditional.1 = (f32[32,128,128]{2,1,0:T(8,128)}, bf16[32,128,128]{2,1,0:T(8,128)(2,1)}, f32[32,128,128]{2,1,0:T(8,128)}, s32[272]{0:T(512)S(1)}, s32[272]{0:T(512)S(1)}) conditional(s32[]{:T(128)} %clamp.3, (s32[416]{0:T(512)S(1)}, bf16[32,512,128]{2,1,0:T(8,128)(2,1)}, bf16[16,512,512]{2,1,0:T(8,128)(2,1)}, ...), branch_computations={%region_4.5_spmd, %region_5.6_spmd, %region_6.7_spmd, %region_7.8_... | conditional | flops 6710886400 | bytes 146867040 | solution.py:616
  8.4 0.0 collective-permute-start.4
  8.4 3.7 %pack.5 = (bf16[8,512,128]{2,1,0:T(8,128)(2,1)}, bf16[8,512,128]{2,1,0:T(8,128)(2,1)}) custom-call(s32[416]{0:T(512)S(1)} %get-tuple-element.50.table, bf16[32,512,128]{2,1,0:T(8,128)(2,1)} %get-tuple-element.52.maps), custom_call_target="tpu_custom_call" | custom-call | bytes 4194304 | tf_op jit(solution)/shard_map/cond/branch_0_fun/pack/pallas_call | solution.py:85
  12.1 8.6 %collective-permute-start = (bf16[8,512,128]{2,1,0:T(8,128)(2,1)}, bf16[8,512,128]{2,1,0:T(8,128)(2,1)S(1)}, u32[]{:S(2)}, u32[]{:S(2)}) collective-permute-start(bf16[8,512,128]{2,1,0:T(8,128)(2,1)} %get-tuple-element.53), channel_id=1, source_target_pairs={{1,2},{2,1},{3,4},{4,3},{5,6},{6,5},{7,8},{8,7},{9,10},{10,9},{11,... | collective-permute-start | bytes 3145736 | tf_op jit(solution)/shard_map/cond/branch_0_fun/ppermute | solution.py:558
  20.7 1.9 %collective-permute-start.2 = (bf16[8,512,128]{2,1,0:T(8,128)(2,1)}, bf16[8,512,128]{2,1,0:T(8,128)(2,1)S(1)}, u32[]{:S(2)}, u32[]{:S(2)}) collective-permute-start(bf16[8,512,128]{2,1,0:T(8,128)(2,1)} %get-tuple-element.54), channel_id=1, source_target_pairs={{1,2},{2,1},{3,4},{4,3},{5,6},{6,5},{7,8},{8,7},{9,10},{10,9},{11,... | collective-permute-start | bytes 3145736 | tf_op jit(solution)/shard_map/cond/branch_0_fun/ppermute | solution.py:558
  22.6 10.8 %collective-permute-done.maps = bf16[8,512,128]{2,1,0:T(8,128)(2,1)S(1)} collective-permute-done((bf16[8,512,128]{2,1,0:T(8,128)(2,1)}, bf16[8,512,128]{2,1,0:T(8,128)(2,1)S(1)}, u32[]{:S(2)}, u32[]{:S(2)}) %collective-permute-start) | collective-permute-done | bytes 1048608 | tf_op jit(solution)/shard_map/cond/branch_0_fun/ppermute | solution.py:558
  33.4 0.0 copy-start.19
  33.4 1.0 copy-done.19
  34.3 5.7 %serve.10 = bf16[8,512,128]{2,1,0:T(8,128)(2,1)} custom-call(s32[416]{0:T(512)S(1)} %get-tuple-element.50.table, bf16[16,512,512]{2,1,0:T(8,128)(2,1)} %get-tuple-element.51.blocks, bf16[8,512,128]{2,1,0:T(8,128)(2,1)} %copy-done.19), custom_call_target="tpu_custom_call" | custom-call | flops 536870912 | bytes 6291456 | tf_op jit(solution)/shard_map/cond/branch_0_fun/serve/pallas_call | solution.py:221
  40.1 0.0 copy-start.22
  40.1 0.0 copy-start.27
  40.1 7.9 %collective-permute-start.1 = (bf16[8,512,128]{2,1,0:T(8,128)(2,1)}, bf16[8,512,128]{2,1,0:T(8,128)(2,1)S(1)}, u32[]{:S(2)}, u32[]{:S(2)}) collective-permute-start(bf16[8,512,128]{2,1,0:T(8,128)(2,1)} %serve.10), channel_id=1, source_target_pairs={{1,2},{2,1},{3,4},{4,3},{5,6},{6,5},{7,8},{8,7},{9,10},{10,9},{11,... | collective-permute-start | bytes 3145736 | tf_op jit(solution)/shard_map/cond/branch_0_fun/ppermute | solution.py:558
  48.0 0.0 collective-permute-done.2.maps
  48.0 0.0 copy-start.17
  48.0 1.0 copy-done.17
  49.0 5.1 %serve.11 = bf16[8,512,128]{2,1,0:T(8,128)(2,1)} custom-call(s32[416]{0:T(512)S(1)} %get-tuple-element.50.table, bf16[16,512,512]{2,1,0:T(8,128)(2,1)} %get-tuple-element.51.blocks, bf16[8,512,128]{2,1,0:T(8,128)(2,1)} %copy-done.17), custom_call_target="tpu_custom_call" | custom-call | flops 536870912 | bytes 6291456 | tf_op jit(solution)/shard_map/cond/branch_0_fun/serve/pallas_call | solution.py:221
  54.1 3.9 %collective-permute-start.3 = (bf16[8,512,128]{2,1,0:T(8,128)(2,1)}, bf16[8,512,128]{2,1,0:T(8,128)(2,1)S(1)}, u32[]{:S(2)}, u32[]{:S(2)}) collective-permute-start(bf16[8,512,128]{2,1,0:T(8,128)(2,1)} %serve.11), channel_id=1, source_target_pairs={{1,2},{2,1},{3,4},{4,3},{5,6},{6,5},{7,8},{8,7},{9,10},{10,9},{11,... | collective-permute-start | bytes 3145736 | tf_op jit(solution)/shard_map/cond/branch_0_fun/ppermute | solution.py:558
  58.0 0.0 copy-done.22
  58.0 0.0 copy-done.27
  58.0 30.0 %local.5 = (bf16[32,128,512]{2,1,0:T(8,128)(2,1)}, f32[32,128,128]{2,1,0:T(8,128)}, f32[32,128,128]{2,1,0:T(8,128)}, bf16[32,128,128]{2,1,0:T(8,128)(2,1)}, s32[272]{0:T(512)S(1)}, /*index=5*/s32[272]{0:T(512)S(1)}) custom-call(s32[416]{0:T(512)S(1)} %get-tuple-element.50.table, f32[32]{0:T(128)S(1)} %copy-done.27, ...), custom_call_target="tpu_custom_call" | custom-call | flops 3221225472 | bytes 16777216 | tf_op jit(solution)/shard_map/cond/branch_0_fun/local/pallas_call | solution.py:169
  88.1 0.0 collective-permute-done.4.blocks
  88.1 8.2 %beside.5 = (f32[32,128,128]{2,1,0:T(8,128)}, bf16[32,128,128]{2,1,0:T(8,128)(2,1)}) custom-call(s32[416]{0:T(512)S(1)} %get-tuple-element.50.table, bf16[16,512,512]{2,1,0:T(8,128)(2,1)} %collective-permute-done.4.blocks, bf16[32,512,128]{2,1,0:T(8,128)(2,1)} %get-tuple-element.52.maps, ...), custom_call_target="tpu_custom_call", output_to_operand_aliasing={{0}: (5, {}), {1}: (6, {})} | custom-call | flops 1073741824 | bytes 8388608 | tf_op jit(solution)/shard_map/cond/branch_0_fun/beside/pallas_call | solution.py:288
  96.3 0.0 collective-permute-done.1.refs_0_
  96.4 0.0 copy-start.14
  96.4 0.0 collective-permute-done.3.refs_1_
  96.4 0.0 copy-start.15
  96.4 0.9 copy-done.14
  97.3 0.4 copy-done.15
  97.7 5.6 %across.5 = (f32[32,128,128]{2,1,0:T(8,128)}, bf16[32,128,128]{2,1,0:T(8,128)(2,1)}) custom-call(s32[416]{0:T(512)S(1)} %get-tuple-element.50.table, bf16[8,512,128]{2,1,0:T(8,128)(2,1)} %copy-done.14, bf16[8,512,128]{2,1,0:T(8,128)(2,1)} %copy-done.15, ...), custom_call_target="tpu_custom_call", output_to_operand_aliasing={{0}: (5, {}), {1}: (6, {})} | custom-call | flops 268435456 | bytes 4194304 | tf_op jit(solution)/shard_map/cond/branch_0_fun/across/pallas_call | solution.py:368
  103.6 0.1 collective-permute-start.26
  103.7 5.0 %collective-permute-start.25 = (bf16[32,128,128]{2,1,0:T(8,128)(2,1)}, bf16[32,128,128]{2,1,0:T(8,128)(2,1)S(1)}, u32[]{:S(2)}, u32[]{:S(2)}) collective-permute-start(bf16[32,128,128]{2,1,0:T(8,128)(2,1)} %get-tuple-element.150.here), channel_id=1, source_target_pairs={{1,2},{2,1},{3,4},{4,3},{5,6},{6,5},{7,8},{8,7},{9,10},{10,9},{11,... | collective-permute-start | bytes 3145736 | tf_op jit(solution)/shard_map/ppermute | solution.py:558
  108.7 0.0 collective-permute-done.26.beside_
  108.7 0.0 copy-start.21
  108.7 1.0 copy-done.21
  109.7 15.8 %early.2.so_far = f32[32,128,128]{2,1,0:T(8,128)} custom-call(s32[272]{0:T(512)S(1)} %get-tuple-element.151.listed, bf16[256,128,128]{2,1,0:T(8,128)(2,1)} %bitcast.11, bf16[32,128,128]{2,1,0:T(8,128)(2,1)} %get-tuple-element.150.here, bf16[32,128,128]{2,1,0:T(8,128)(2,1)} %copy-done.21, f32[32,128,128]{2,1,0:T(8,128)} %get-tuple-element.152.integ.refs_0_), custom_call_target="tpu_custom_call" | custom-call | flops 1073741824 | bytes 8388608 | tf_op jit(solution)/shard_map/early/pallas_call | solution.py:501
  125.4 0.0 collective-permute-done.25.other
  125.5 0.0 copy-start.18
  125.5 1.0 copy-done.18
  126.4 10.9 %late.2.here = bf16[32,128,128]{2,1,0:T(8,128)(2,1)} custom-call(s32[272]{0:T(512)S(1)} %get-tuple-element.149.listed, bf16[256,128,128]{2,1,0:T(8,128)(2,1)} %bitcast.12, bf16[32,128,128]{2,1,0:T(8,128)(2,1)} %copy-done.18, f32[32,128,128]{2,1,0:T(8,128)} %early.2.so_far, f32[32,128,128]{2,1,0:T(8,128)} %get-tuple-element.153.inverse), custom_call_target="tpu_custom_call" | custom-call | flops 536870912 | bytes 8388608 | tf_op jit(solution)/shard_map/late/pallas_call | solution.py:521
  137.3 0.1 collective-permute-start.28
  137.4 4.4 %collective-permute-start.27 = (bf16[32,128,128]{2,1,0:T(8,128)(2,1)}, bf16[32,128,128]{2,1,0:T(8,128)(2,1)S(1)}, u32[]{:S(2)}, u32[]{:S(2)}) collective-permute-start(bf16[32,128,128]{2,1,0:T(8,128)(2,1)} %late.2.here), channel_id=1, source_target_pairs={{1,2},{2,1},{3,4},{4,3},{5,6},{6,5},{7,8},{8,7},{9,10},{10,9},{11,... | collective-permute-start | bytes 3145736 | tf_op jit(solution)/shard_map/ppermute | solution.py:558
  141.9 0.0 collective-permute-done.28.beside_
  141.9 0.0 copy-start.20
  141.9 1.0 copy-done.20
  142.9 15.7 %early.3.so_far = f32[32,128,128]{2,1,0:T(8,128)} custom-call(s32[272]{0:T(512)S(1)} %get-tuple-element.151.listed, bf16[256,128,128]{2,1,0:T(8,128)(2,1)} %bitcast.13, bf16[32,128,128]{2,1,0:T(8,128)(2,1)} %late.2.here, bf16[32,128,128]{2,1,0:T(8,128)(2,1)} %copy-done.20, f32[32,128,128]{2,1,0:T(8,128)} %get-tuple-element.152.integ.refs_0_), custom_call_target="tpu_custom_call" | custom-call | flops 1073741824 | bytes 8388608 | tf_op jit(solution)/shard_map/early/pallas_call | solution.py:501
  158.6 0.0 collective-permute-done.27.other
  158.6 0.0 copy-start.16
  158.7 1.0 copy-done.16
  159.7 12.2 %late.3 = (f32[32,128,128]{2,1,0:T(8,128)}, f32[32,128]{1,0:T(8,128)}) custom-call(s32[272]{0:T(512)S(1)} %get-tuple-element.149.listed, bf16[256,128,128]{2,1,0:T(8,128)(2,1)} %bitcast.14, bf16[32,128,128]{2,1,0:T(8,128)(2,1)} %copy-done.16, f32[32,128,128]{2,1,0:T(8,128)} %early.3.so_far, f32[32,128,128]{2,1,0:T(8,128)} %get-tuple-element.153.inverse, ...), custom_call_target="tpu_custom_call" | custom-call | flops 536870912 | bytes 8388608 | tf_op jit(solution)/shard_map/late/pallas_call | solution.py:521
  171.9 0.8 reduce_sum.39
  172.7 0.5 broadcast_multiply_fusion
  (5 shorter events, 0.0 us)
Async XLA Ops:
  8.4 79.7 %collective-permute-start.4 = (bf16[16,512,512]{2,1,0:T(8,128)(2,1)}, bf16[16,512,512]{2,1,0:T(8,128)(2,1)}, u32[]{:S(2)}, u32[]{:S(2)}) collective-permute-start(bf16[16,512,512]{2,1,0:T(8,128)(2,1)} %get-tuple-element.51.blocks), channel_id=1, source_target_pairs={{0,1},{1,0},{2,3},{3,2},{4,5},{5,4},{6,7},{7,6},{8,9},{9,8},{10,11... | collective-permute-start | bytes 25165832 | tf_op jit(solution)/shard_map/cond/branch_0_fun/ppermute | solution.py:557
  12.1 21.3 %collective-permute-start = (bf16[8,512,128]{2,1,0:T(8,128)(2,1)}, bf16[8,512,128]{2,1,0:T(8,128)(2,1)S(1)}, u32[]{:S(2)}, u32[]{:S(2)}) collective-permute-start(bf16[8,512,128]{2,1,0:T(8,128)(2,1)} %get-tuple-element.53), channel_id=1, source_target_pairs={{1,2},{2,1},{3,4},{4,3},{5,6},{6,5},{7,8},{8,7},{9,10},{10,9},{11,... | collective-permute-start | bytes 3145736 | tf_op jit(solution)/shard_map/cond/branch_0_fun/ppermute | solution.py:558
  20.7 27.3 %collective-permute-start.2 = (bf16[8,512,128]{2,1,0:T(8,128)(2,1)}, bf16[8,512,128]{2,1,0:T(8,128)(2,1)S(1)}, u32[]{:S(2)}, u32[]{:S(2)}) collective-permute-start(bf16[8,512,128]{2,1,0:T(8,128)(2,1)} %get-tuple-element.54), channel_id=1, source_target_pairs={{1,2},{2,1},{3,4},{4,3},{5,6},{6,5},{7,8},{8,7},{9,10},{10,9},{11,... | collective-permute-start | bytes 3145736 | tf_op jit(solution)/shard_map/cond/branch_0_fun/ppermute | solution.py:558
  33.4 1.0 copy-start.19
  40.1 17.9 %copy-start.22 = (f32[32,128]{1,0:T(8,128)S(1)}, f32[32,128]{1,0:T(8,128)}, u32[]{:S(2)}) copy-start(f32[32,128]{1,0:T(8,128)} %get-tuple-element.56.energy) | copy-start | bytes 49156 | tf_op jit(solution)/shard_map/cond
  40.1 17.9 %copy-start.27 = (f32[32]{0:T(128)S(1)}, f32[32]{0:T(128)}, u32[]{:S(2)}) copy-start(f32[32]{0:T(128)} %get-tuple-element.55.shift) | copy-start | bytes 388 | tf_op jit(solution)/shard_map/cond
  40.1 56.2 %collective-permute-start.1 = (bf16[8,512,128]{2,1,0:T(8,128)(2,1)}, bf16[8,512,128]{2,1,0:T(8,128)(2,1)S(1)}, u32[]{:S(2)}, u32[]{:S(2)}) collective-permute-start(bf16[8,512,128]{2,1,0:T(8,128)(2,1)} %serve.10), channel_id=1, source_target_pairs={{1,2},{2,1},{3,4},{4,3},{5,6},{6,5},{7,8},{8,7},{9,10},{10,9},{11,... | collective-permute-start | bytes 3145736 | tf_op jit(solution)/shard_map/cond/branch_0_fun/ppermute | solution.py:558
  48.0 1.0 copy-start.17
  54.1 42.3 %collective-permute-start.3 = (bf16[8,512,128]{2,1,0:T(8,128)(2,1)}, bf16[8,512,128]{2,1,0:T(8,128)(2,1)S(1)}, u32[]{:S(2)}, u32[]{:S(2)}) collective-permute-start(bf16[8,512,128]{2,1,0:T(8,128)(2,1)} %serve.11), channel_id=1, source_target_pairs={{1,2},{2,1},{3,4},{4,3},{5,6},{6,5},{7,8},{8,7},{9,10},{10,9},{11,... | collective-permute-start | bytes 3145736 | tf_op jit(solution)/shard_map/cond/branch_0_fun/ppermute | solution.py:558
  96.4 1.0 copy-start.14
  96.4 1.3 copy-start.15
  103.6 5.1 %collective-permute-start.26 = (bf16[32,128,128]{2,1,0:T(8,128)(2,1)}, bf16[32,128,128]{2,1,0:T(8,128)(2,1)S(1)}, u32[]{:S(2)}, u32[]{:S(2)}) collective-permute-start(bf16[32,128,128]{2,1,0:T(8,128)(2,1)} %get-tuple-element.150.here), channel_id=1, source_target_pairs={{0,1},{1,0},{2,3},{3,2},{4,5},{5,4},{6,7},{7,6},{8,9},{9,8},{10,11... | collective-permute-start | bytes 3145736 | tf_op jit(solution)/shard_map/ppermute | solution.py:557
  103.7 21.8 %collective-permute-start.25 = (bf16[32,128,128]{2,1,0:T(8,128)(2,1)}, bf16[32,128,128]{2,1,0:T(8,128)(2,1)S(1)}, u32[]{:S(2)}, u32[]{:S(2)}) collective-permute-start(bf16[32,128,128]{2,1,0:T(8,128)(2,1)} %get-tuple-element.150.here), channel_id=1, source_target_pairs={{1,2},{2,1},{3,4},{4,3},{5,6},{6,5},{7,8},{8,7},{9,10},{10,9},{11,... | collective-permute-start | bytes 3145736 | tf_op jit(solution)/shard_map/ppermute | solution.py:558
  108.7 1.0 copy-start.21
  125.5 1.0 copy-start.18
  137.3 4.6 %collective-permute-start.28 = (bf16[32,128,128]{2,1,0:T(8,128)(2,1)}, bf16[32,128,128]{2,1,0:T(8,128)(2,1)S(1)}, u32[]{:S(2)}, u32[]{:S(2)}) collective-permute-start(bf16[32,128,128]{2,1,0:T(8,128)(2,1)} %late.2.here), channel_id=1, source_target_pairs={{0,1},{1,0},{2,3},{3,2},{4,5},{5,4},{6,7},{7,6},{8,9},{9,8},{10,11... | collective-permute-start | bytes 3145736 | tf_op jit(solution)/shard_map/ppermute | solution.py:557
  137.4 21.2 %collective-permute-start.27 = (bf16[32,128,128]{2,1,0:T(8,128)(2,1)}, bf16[32,128,128]{2,1,0:T(8,128)(2,1)S(1)}, u32[]{:S(2)}, u32[]{:S(2)}) collective-permute-start(bf16[32,128,128]{2,1,0:T(8,128)(2,1)} %late.2.here), channel_id=1, source_target_pairs={{1,2},{2,1},{3,4},{4,3},{5,6},{6,5},{7,8},{8,7},{9,10},{10,9},{11,... | collective-permute-start | bytes 3145736 | tf_op jit(solution)/shard_map/ppermute | solution.py:558
  141.9 1.0 copy-start.20
  158.6 1.0 copy-start.16

commit v2 on v1

--- a/solution.py
+++ b/solution.py
@@ -11,8 +11,6 @@
 ITERS = 2
 COUPLING = 0.35
 SLOTS = (16, 18, 20, 24, 32)
-GROUP = 8
-VMEM_LIMIT = 60 * 1024 * 1024
 
 ANY = pl.BlockSpec(memory_space=pl.ANY)
 VMEM = pl.BlockSpec(memory_space=pltpu.VMEM)
@@ -21,7 +19,7 @@
 ONE, SRC, SERVE, LIVE, PNO, NEAR = 0, 32, 64, 96, 128, 160
 
 
-def call(body, outs, out_specs, in_specs, scratch, flops=0, moved=0, aliases=None, name=None):
+def call(body, outs, out_specs, in_specs, scratch, flops=0, moved=0, limit=60, aliases=None, name=None):
     return pl.pallas_call(
         body,
         out_shape=outs,
@@ -29,7 +27,7 @@
         out_specs=out_specs,
         scratch_shapes=scratch,
         input_output_aliases=aliases or {},
-        compiler_params=pltpu.CompilerParams(vmem_limit_bytes=VMEM_LIMIT),
+        compiler_params=pltpu.CompilerParams(vmem_limit_bytes=limit * 1024 * 1024),
         cost_estimate=pl.CostEstimate(flops=int(flops), bytes_accessed=int(moved), transcendentals=0),
         name=name,
     )
@@ -41,6 +39,10 @@
 
 def dot_nt(left, right):
     return lax.dot_general(left, right, (((1,), (1,)), ((), ())), preferred_element_type=jnp.float32)
+
+
+def dot_tn_nt(left, right):
+    return lax.dot_general(left, right, (((0,), (1,)), ((), ())), preferred_element_type=jnp.float32)
 
 
 def collect(count, wanted, begin, slots):
@@ -89,6 +91,7 @@
         [SMEM, ANY],
         [pltpu.SMEM((count,), jnp.int32), pltpu.SemaphoreType.DMA((count,))],
         moved=2 * sum(sizes) * depth * width * 2,
+        limit=8,
         name="pack",
     )(table, maps)
 
@@ -110,27 +113,45 @@
 
     def note(entry, counts):
         soon, after = counts
-        pair = entry // near
         where = table[NEAR + entry]
         is_late = where >= 2 * count
+        code = (entry // near) * 65536 + entry * 256 + where
 
         @pl.when(is_late)
         def _():
-            late[1 + after] = pair * 65536 + entry * 256 + (where - 2 * count)
+            late[1 + after] = code - 2 * count
 
         @pl.when(jnp.logical_not(is_late))
         def _():
-            early[1 + soon] = pair * 65536 + entry * 256 + where
+            early[1 + soon] = code
 
         step = is_late.astype(jnp.int32)
         return soon + 1 - step, after + step
 
-    soon, after = lax.fori_loop(0, count * near, note, (jnp.int32(0), jnp.int32(0)))
-    early[0] = soon
-    late[0] = after
-    for k in range(GROUP):
-        early[1 + soon + k] = count * 65536
-        late[1 + after + k] = count * 65536
+    def note_pair(pair, counts):
+        for k in range(near):
+            counts = note(pair * near + k, counts)
+        soon, after = counts
+        spare = pair * 65536 + pair * near * 256
+
+        @pl.when(soon % 2 == 1)
+        def _():
+            early[1 + soon] = spare + 2 * count
+
+        @pl.when(after % 2 == 1)
+        def _():
+            late[1 + after] = spare + count
+
+        return soon + soon % 2, after + after % 2
+
+    soon, after = lax.fori_loop(0, count, note_pair, (jnp.int32(0), jnp.int32(0)))
+    early[0] = soon // 2
+    late[0] = after // 2
+
+    @pl.loop(0, 6 * UNIT)
+    def _(k):
+        early[1 + soon + k] = count * 65536 + 2 * count
+        late[1 + after + k] = count * 65536 + count
 
     @pl.loop(0, count)
     def _(p):
@@ -145,19 +166,23 @@
     def _(o):
         pltpu.make_async_copy(blocks.at[0], held.at[0], sem.at[o]).wait()
 
+    columns = lax.broadcasted_iota(jnp.int32, (width, depth), 1)
+
+    @pl.loop(0, count // 2)
+    def _(duo):
+        for p in (2 * duo, 2 * duo + 1):
+            pltpu.make_async_copy(maps.at[0], map_held.at[0], map_sem.at[p]).wait()
+            half = dot_tn_nt(map_held[p], held[table[ONE + p]])
+            left[p] = jnp.where(columns < table[LIVE + p], half, 0.0).astype(jnp.bfloat16)
+
     @pl.loop(0, count)
     def _(p):
-        pltpu.make_async_copy(maps.at[0], map_held.at[0], map_sem.at[p]).wait()
-        half = dot(held[table[ONE + p]], map_held[p])
-        rows = lax.broadcasted_iota(jnp.int32, (depth, width), 0)
-        half = jnp.where(rows < table[LIVE + p], half, 0.0).astype(jnp.bfloat16).T
-        left[p] = half
         where = table[SRC + p]
 
         @pl.when(where < orbitals)
         def _():
             right = dot(held[where], map_held[p]).astype(jnp.bfloat16)
-            value = dot(half, right) * scale
+            value = dot(left[p], right) * scale
             integ[p] = value
             start[p] = (value * inverse[p]).astype(jnp.bfloat16)
 
@@ -165,7 +190,7 @@
 def local(table, shift, blocks, maps, energy, scale):
     orbitals, depth, wide = blocks.shape
     count, _, width = maps.shape
-    entries = count * 8 + GROUP + 8
+    entries = count * 8 + 6 * UNIT + 8
     return call(
         functools.partial(local_body, scale),
         (
@@ -186,6 +211,7 @@
         ],
         flops=2 * 1.5 * count * depth * wide * width,
         moved=(blocks.size + 2 * maps.size) * 2,
+        limit=30,
         name="local",
     )(table, shift, blocks, maps, energy)
 
@@ -230,6 +256,7 @@
         ],
         flops=2 * size * depth * wide * width,
         moved=size * depth * (wide + 2 * width) * 2,
+        limit=3 * size // 4 + 4,
         name="serve",
     )(table, blocks, maps)
 
@@ -307,6 +334,7 @@
         flops=count * depth * wide * width,
         moved=count * depth * wide,
         aliases={5: 0, 6: 1},
+        limit=34,
         name="beside",
     )(table, blocks, maps, left, inverse, integ, start)
 
@@ -385,114 +413,94 @@
         flops=count * depth * width * width,
         moved=count * depth * width * 2,
         aliases={n + 3: 0, n + 4: 1},
+        limit=20,
         name="across",
     )(table, *halves, left, inverse, integ, start)
 
 
-CHUNK = 4
-
-
-def gather_coupling(listed, inter, tables, total, held, amps, sem, tsem):
-    near = 8
-    chunks = inter.shape[0] // (CHUNK * near)
-    rows = CHUNK * near
-    number = listed[0]
-    for k, tab in enumerate(tables):
-        size = tab.shape[0]
-        pltpu.make_async_copy(tab, amps.at[pl.ds(k * size, size)], tsem.at[k]).start()
-
-    @pl.loop(0, chunks)
-    def _(c):
-        pltpu.make_async_copy(
-            inter.at[pl.ds(c * rows, rows)], held.at[pl.ds(c * rows, rows)], sem.at[c]
-        ).start()
-
-    def wait_chunk(c):
-        pltpu.make_async_copy(inter.at[pl.ds(0, rows)], held.at[pl.ds(0, rows)], sem.at[c]).wait()
-
-    def ready():
-        for k, tab in enumerate(tables):
-            size = tab.shape[0]
-            pltpu.make_async_copy(tab, amps.at[pl.ds(k * size, size)], tsem.at[k]).wait()
-
-    def group(g, waited):
-        codes = [listed[1 + g * GROUP + k] for k in range(GROUP)]
-        last = codes[0] // 65536
-        for code in codes[1:]:
-            last = jnp.maximum(last, jnp.minimum(code // 65536, 31))
-        need = jnp.minimum(last // CHUNK + 1, chunks)
-
-        @pl.loop(waited, need)
-        def _(c):
-            wait_chunk(c)
-
-        mixed = []
-        for code in codes:
-            entry = (code // 256) % 256
-            mixed.append(dot(held[entry], amps[code % 256]).astype(jnp.bfloat16))
-        for code, part in zip(codes, mixed):
-            entry = (code // 256) % 256
-            total[code // 65536] += dot_nt(part, held[entry])
-        return jnp.maximum(waited, need)
-
-    return ready, group, wait_chunk, chunks, number
-
-
-def early_body(listed, inter, here, beside_, integ, out, total, held, amps, sem, tsem):
-    count = integ.shape[0]
-    ready, group, wait_chunk, chunks, number = gather_coupling(
-        listed, inter, (here, beside_), total, held, amps, sem, tsem
-    )
-
-    @pl.loop(0, count)
+UNIT = 4
+
+
+def couple(listed, inter, tables, total, amps, ahead, behind):
+    count = total.shape[0] - 1
+    width = total.shape[1]
+    low = 0
+    for table in tables:
+        amps[pl.ds(low, table.shape[0])] = table[...]
+        low += table.shape[0]
+    amps[low] = jnp.zeros(amps.shape[1:], amps.dtype)
+
+    @pl.loop(0, count + 1)
     def _(p):
         total[p] = jnp.zeros(total.shape[1:], jnp.float32)
 
-    total[count] = jnp.zeros(total.shape[1:], jnp.float32)
-    ready()
-    waited = lax.fori_loop(0, (number + GROUP - 1) // GROUP, group, jnp.int32(0))
-    pl.loop(waited, chunks)(wait_chunk)
-
-    @pl.loop(0, count)
+    def codes(group):
+        for k in range(UNIT):
+            place = 1 + (group * UNIT + k) * 2
+            one, two = listed[place], listed[place + 1]
+            yield k, one // 65536, (one // 256) % 256, one % 256, (two // 256) % 256, two % 256
+
+    def first(group, mixed):
+        for k, _, one, amp_one, two, amp_two in codes(group):
+            mixed[k, :, 0:width] = dot(inter[one], amps[amp_one]).astype(jnp.bfloat16)
+            mixed[k, :, width : 2 * width] = dot(inter[two], amps[amp_two]).astype(jnp.bfloat16)
+
+    def second(group, mixed):
+        for k, pair, one, _, two, _ in codes(group):
+            total[pair] += dot_nt(mixed[k], jnp.concatenate([inter[one], inter[two]], axis=1))
+
+    first(0, ahead)
+
+    @pl.loop(0, (listed[0] + 2 * UNIT - 1) // (2 * UNIT))
+    def _(step):
+        first(2 * step + 1, behind)
+        second(2 * step, ahead)
+        first(2 * step + 2, ahead)
+        second(2 * step + 1, behind)
+
+
+def early_body(listed, inter, here, near_by, integ, out, total, *scratch):
+    couple(listed, inter, (here, near_by), total, *scratch)
+
+    @pl.loop(0, integ.shape[0])
     def _(p):
         out[p] = integ[p] + COUPLING * total[p]
 
 
-def late_body(final, listed, inter, other, so_far, inverse, *refs):
-    if final:
-        integ, out, energy, total, held, amps, sem, tsem = refs
-    else:
-        out, total, held, amps, sem, tsem = refs
-    count = so_far.shape[0]
-    ready, group, wait_chunk, chunks, number = gather_coupling(
-        listed, inter, (other,), total, held, amps, sem, tsem
-    )
-
-    @pl.loop(0, count)
+def late_body(listed, inter, other, so_far, inverse, out, total, *scratch):
+    couple(listed, inter, (other,), total, *scratch)
+
+    @pl.loop(0, so_far.shape[0])
     def _(p):
-        total[p] = jnp.zeros(total.shape[1:], jnp.float32)
-
-    total[count] = jnp.zeros(total.shape[1:], jnp.float32)
-    ready()
-    waited = lax.fori_loop(0, (number + GROUP - 1) // GROUP, group, jnp.int32(0))
-    pl.loop(waited, chunks)(wait_chunk)
-
-    @pl.loop(0, count)
+        out[p] = ((so_far[p] + COUPLING * total[p]) * inverse[p]).astype(out.dtype)
+
+
+def last_body(listed, inter, other, so_far, inverse, integ, out, energy, rows, total, *scratch):
+    couple(listed, inter, (other,), total, *scratch)
+    width = total.shape[1]
+
+    @pl.loop(0, so_far.shape[0])
     def _(p):
         value = (so_far[p] + COUPLING * total[p]) * inverse[p]
-        out[p] = value.astype(out.dtype)
-        if final:
-            energy[pl.ds(p, 1), :] = jnp.sum(integ[p] * value, axis=0, keepdims=True)
-
-
-def coupling_scratch(count, entries, width, tables):
-    chunks = count // CHUNK
+        out[p] = value
+        rows[pl.ds(p, 1), :] = jnp.sum(integ[p] * value, axis=0, keepdims=True)
+
+    sums = lax.dot_general(
+        jnp.ones((8, width), jnp.float32),
+        rows[...],
+        (((1,), (1,)), ((), ())),
+        precision=lax.Precision.HIGHEST,
+        preferred_element_type=jnp.float32,
+    )
+    energy[...] = sums[0:1, :] * (1.0 / (width * width))
+
+
+def coupling_scratch(count, width, tables):
     return [
         pltpu.VMEM((count + 1, width, width), jnp.float32),
-        pltpu.VMEM((entries, width, width), jnp.bfloat16),
-        pltpu.VMEM((tables * count, width, width), jnp.bfloat16),
-        pltpu.SemaphoreType.DMA((chunks,)),
-        pltpu.SemaphoreType.DMA((tables,)),
+        pltpu.VMEM((tables * count + 1, width, width), jnp.bfloat16),
+        pltpu.VMEM((UNIT, width, 2 * width), jnp.bfloat16),
+        pltpu.VMEM((UNIT, width, 2 * width), jnp.bfloat16),
     ]
 
 
@@ -502,32 +510,46 @@
         early_body,
         jax.ShapeDtypeStruct(integ.shape, jnp.float32),
         VMEM,
-        [SMEM, ANY, ANY, ANY, VMEM],
-        coupling_scratch(count, inter.shape[0], width, 2),
+        [SMEM, VMEM, VMEM, VMEM, VMEM],
+        coupling_scratch(count, width, 2),
         flops=2 * inter.shape[0] * width**3,
         moved=inter.size * 2,
+        limit=24,
         name="early",
     )(listed, inter, here, other, integ)
 
 
-def late_part(listed, inter, other, so_far, inverse, integ=None):
+def late_part(listed, inter, other, so_far, inverse):
     count, width, _ = so_far.shape
-    final = integ is not None
-    outs = jax.ShapeDtypeStruct(so_far.shape, jnp.float32 if final else jnp.bfloat16)
-    args = (listed, inter, other, so_far, inverse)
-    if final:
-        outs = (outs, jax.ShapeDtypeStruct((count, width), jnp.float32))
-        args += (integ,)
-    return call(
-        functools.partial(late_body, final),
-        outs,
-        (VMEM, VMEM) if final else VMEM,
-        [SMEM, ANY, ANY] + [VMEM] * (len(args) - 3),
-        coupling_scratch(count, inter.shape[0], width, 1),
+    return call(
+        late_body,
+        jax.ShapeDtypeStruct(so_far.shape, jnp.bfloat16),
+        VMEM,
+        [SMEM, VMEM, VMEM, VMEM, VMEM],
+        coupling_scratch(count, width, 1),
         flops=inter.shape[0] * width**3,
         moved=inter.size * 2,
+        limit=24,
         name="late",
-    )(*args)
+    )(listed, inter, other, so_far, inverse)
+
+
+def last_part(listed, inter, other, so_far, inverse, integ):
+    count, width, _ = so_far.shape
+    return call(
+        last_body,
+        (
+            jax.ShapeDtypeStruct(so_far.shape, jnp.float32),
+            jax.ShapeDtypeStruct((1, count), jnp.float32),
+        ),
+        (VMEM, VMEM),
+        [SMEM, VMEM, VMEM, VMEM, VMEM, VMEM],
+        [pltpu.VMEM((count, width), jnp.float32)] + coupling_scratch(count, width, 1),
+        flops=inter.shape[0] * width**3,
+        moved=inter.size * 2,
+        limit=24,
+        name="last",
+    )(listed, inter, other, so_far, inverse, integ)
 
 
 def shards(
@@ -601,6 +623,7 @@
             left, integ, inverse, start, early, late = local(table, shift, blocks, maps, energy, scale)
             halves = []
             low = 0
+            table, _ = lax.optimization_barrier((table, late))
             for x in got:
                 half = serve(table, blocks, x, low, count)
                 low += x.shape[0]
@@ -629,9 +652,8 @@
         if iteration < ITERS - 1:
             amps = late_part(late, inter, far, so_far, inverse)
         else:
-            amps, energies = late_part(late, inter, far, so_far, inverse, integ)
-    pair_energy = jnp.sum(energies, axis=1) / (width * width)
-    return (amps, pair_energy)
+            amps, energies = last_part(late, inter, far, so_far, inverse, integ)
+    return (amps, energies.reshape(count))
 
 
 def solution(mesh):

time: 176 us -> 155 us (0.88)
  the two profiles are of different devices: /device:TPU:4 before, /device:TPU:6 now
where the time goes in v2:
time: 155 us; the launch traced here: 154 us
  Pallas kernels  91.5 us (59%)
  starting transfers between devices  35.6 us (23%)
  waiting for transfers between devices  15 us (10%)
  local copies, waits for them, and re-layouts  6.73 us (4%)
  between operations  3.39 us (2%)
  other arithmetic  1.74 us (1%)
    ppermute x6, starting transfers between devices, shards(): swap_across = lambda x: lax.ppermute(x, 'pairs', across_perm)  35.5 us
    pallas_call x1, Pallas kernels, local(): call(functools.partial(local_body, scale), (jax.ShapeDtypeStruct((count,...  24.6 us
    pallas_call x2, Pallas kernels, early_part(): call(early_body, jax.ShapeDtypeStruct(integ.shape, jnp.float32), VMEM, [S...  19 us
    ppermute x6, waiting for transfers between devices, shards(): swap_across = lambda x: lax.ppermute(x, 'pairs', across_perm)  15 us
    pallas_call x1, Pallas kernels, beside(): call(functools.partial(beside_body, scale, orbitals), (jax.ShapeDtypeStru...  12.1 us
    pallas_call x1, Pallas kernels, across(): call(functools.partial(across_body, scale, orbitals), (jax.ShapeDtypeStru...  11.1 us
    pallas_call x1, Pallas kernels, last_part(): call(last_body, (jax.ShapeDtypeStruct(so_far.shape, jnp.float32), jax.Sha...  8.94 us
    pallas_call x1, Pallas kernels, late_part(): call(late_body, jax.ShapeDtypeStruct(so_far.shape, jnp.bfloat16), VMEM, [...  6.54 us
  transfers between devices with their start and end apart: 9, of which 3 were waited for; matrix products, arithmetic and copies ran while one was open for 0% of the time, Pallas kernels for 42%

profile of v2, /device:TPU:6, one launch (start us, length us, event | category | flops | bytes accessed | tf_op | source)
XLA Modules:
  0.0 154.4 jit_solution(18244371195605899294)
XLA Ops:
  0.7 0.8 slice_reduce_fusion
  1.5 0.8 constant_dynamic-slice_fusion
  2.3 0.7 broadcast_subtract_fusion
  3.0 0.1 copy.32
  3.0 0.1 reshape.42
  3.2 0.1 reshape_squeeze.3
  3.2 0.2 convert_reduce_fusion
  3.4 0.6 reduce_max.9
  6.7 0.8 pad_dynamic-slice_fusion
  7.4 0.2 select_reduce_fusion
  7.6 0.7 concatenate.3
  8.4 89.4 %conditional.1 = (f32[32,128,128]{2,1,0:T(8,128)}, bf16[32,128,128]{2,1,0:T(8,128)(2,1)}, f32[32,128,128]{2,1,0:T(8,128)}, s32[288]{0:T(512)S(1)}, s32[288]{0:T(512)S(1)}) conditional(s32[]{:T(128)} %clamp.3, (s32[416]{0:T(512)S(1)}, f32[32]{0:T(128)}, bf16[16,512,512]{2,1,0:T(8,128)(2,1)}, ...), branch_computations={%region_4.5_spmd, %region_5.6_spmd, %region_6.7_spmd, %region_7.8_... | conditional | flops 6710886400 | bytes 155190080 | solution.py:639
  8.4 0.0 collective-permute-start.9
  8.4 0.0 copy-start.6
  8.4 0.0 slice-start.2
  8.4 2.7 %pack.6 = (bf16[9,512,128]{2,1,0:T(8,128)(2,1)S(1)}, bf16[9,512,128]{2,1,0:T(8,128)(2,1)S(1)}) custom-call(s32[416]{0:T(512)S(1)} %get-tuple-element.75.table, bf16[32,512,128]{2,1,0:T(8,128)(2,1)} %get-tuple-element.72.maps), custom_call_target="tpu_custom_call" | custom-call | bytes 4718592 | tf_op jit(solution)/shard_map/cond/branch_1_fun/pack/pallas_call | solution.py:87
  11.1 8.7 %collective-permute-start.5 = (bf16[9,512,128]{2,1,0:T(8,128)(2,1)S(1)}, bf16[9,512,128]{2,1,0:T(8,128)(2,1)S(1)}, u32[]{:S(2)}, u32[]{:S(2)}) collective-permute-start(bf16[9,512,128]{2,1,0:T(8,128)(2,1)S(1)} %get-tuple-element.76), channel_id=1, source_target_pairs={{1,2},{2,1},{3,4},{4,3},{5,6},{6,5},{7,8},{8,7},{9,10},{10,9},{11,... | collective-permute-start | bytes 3538952 | tf_op jit(solution)/shard_map/cond/branch_1_fun/ppermute | solution.py:580
  19.9 1.9 %collective-permute-start.7 = (bf16[9,512,128]{2,1,0:T(8,128)(2,1)S(1)}, bf16[9,512,128]{2,1,0:T(8,128)(2,1)S(1)}, u32[]{:S(2)}, u32[]{:S(2)}) collective-permute-start(bf16[9,512,128]{2,1,0:T(8,128)(2,1)S(1)} %get-tuple-element.77), channel_id=1, source_target_pairs={{1,2},{2,1},{3,4},{4,3},{5,6},{6,5},{7,8},{8,7},{9,10},{10,9},{11,... | collective-permute-start | bytes 3538952 | tf_op jit(solution)/shard_map/cond/branch_1_fun/ppermute | solution.py:580
  21.8 0.0 copy-done.6
  21.8 0.0 slice-start.3
  21.8 24.6 %local.6 = (bf16[32,128,512]{2,1,0:T(8,128)(2,1)S(1)}, f32[32,128,128]{2,1,0:T(8,128)}, f32[32,128,128]{2,1,0:T(8,128)}, bf16[32,128,128]{2,1,0:T(8,128)(2,1)}, s32[288]{0:T(512)S(1)}, /*index=5*/s32[288]{0:T(512)S(1)}) custom-call(s32[416]{0:T(512)S(1)} %get-tuple-element.75.table, f32[32]{0:T(128)S(1)} %copy-done.6, ...), custom_call_target="tpu_custom_call" | custom-call | flops 3221225472 | bytes 16777216 | tf_op jit(solution)/shard_map/cond/branch_1_fun/local/pallas_call | solution.py:194
  46.5 0.0 collective-permute-done.5.maps
  46.5 0.0 slice-done.2
  46.5 0.0 slice-done.3
  46.5 4.2 %serve.12 = bf16[9,512,128]{2,1,0:T(8,128)(2,1)S(1)} custom-call(s32[416]{0:T(512)S(1)} %get-tuple-element.75.table, bf16[16,512,512]{2,1,0:T(8,128)(2,1)S(1)} %bitcast.19, bf16[9,512,128]{2,1,0:T(8,128)(2,1)S(1)} %collective-permute-done.5.maps), custom_call_target="tpu_custom_call" | custom-call | flops 603979776 | bytes 7077888 | tf_op jit(solution)/shard_map/cond/branch_1_fun/serve/pallas_call | solution.py:247
  50.7 9.3 %collective-permute-start.6 = (bf16[9,512,128]{2,1,0:T(8,128)(2,1)S(1)}, bf16[9,512,128]{2,1,0:T(8,128)(2,1)S(1)}, u32[]{:S(2)}, u32[]{:S(2)}) collective-permute-start(bf16[9,512,128]{2,1,0:T(8,128)(2,1)S(1)} %serve.12), channel_id=1, source_target_pairs={{1,2},{2,1},{3,4},{4,3},{5,6},{6,5},{7,8},{8,7},{9,10},{10,9},{11,... | collective-permute-start | bytes 3538952 | tf_op jit(solution)/shard_map/cond/branch_1_fun/ppermute | solution.py:580
  60.0 0.0 collective-permute-done.7.maps
  60.0 0.0 copy-start.2
  60.0 2.2 %serve.13 = bf16[9,512,128]{2,1,0:T(8,128)(2,1)S(1)} custom-call(s32[416]{0:T(512)S(1)} %get-tuple-element.75.table, bf16[16,512,512]{2,1,0:T(8,128)(2,1)S(1)} %bitcast.19, bf16[9,512,128]{2,1,0:T(8,128)(2,1)S(1)} %collective-permute-done.7.maps), custom_call_target="tpu_custom_call" | custom-call | flops 603979776 | bytes 7077888 | tf_op jit(solution)/shard_map/cond/branch_1_fun/serve/pallas_call | solution.py:247
  62.2 2.9 %collective-permute-start.8 = (bf16[9,512,128]{2,1,0:T(8,128)(2,1)S(1)}, bf16[9,512,128]{2,1,0:T(8,128)(2,1)S(1)}, u32[]{:S(2)}, u32[]{:S(2)}) collective-permute-start(bf16[9,512,128]{2,1,0:T(8,128)(2,1)S(1)} %serve.13), channel_id=1, source_target_pairs={{1,2},{2,1},{3,4},{4,3},{5,6},{6,5},{7,8},{8,7},{9,10},{10,9},{11,... | collective-permute-start | bytes 3538952 | tf_op jit(solution)/shard_map/cond/branch_1_fun/ppermute | solution.py:580
  65.2 0.0 collective-permute-done.9.blocks
  65.2 0.0 copy-done.2
  65.2 12.1 %beside.6 = (f32[32,128,128]{2,1,0:T(8,128)}, bf16[32,128,128]{2,1,0:T(8,128)(2,1)}) custom-call(s32[416]{0:T(512)S(1)} %get-tuple-element.75.table, bf16[16,512,512]{2,1,0:T(8,128)(2,1)S(1)} %collective-permute-done.9.blocks, bf16[32,512,128]{2,1,0:T(8,128)(2,1)S(1)} %copy-done.2, ...), custom_call_target="tpu_custom_call", output_to_operand_aliasing={{0}: (5, {}), {1}: (6, {})} | custom-call | flops 1073741824 | bytes 8388608 | tf_op jit(solution)/shard_map/cond/branch_1_fun/beside/pallas_call | solution.py:315
  77.4 0.0 collective-permute-done.6.refs_0_
  77.4 9.2 %collective-permute-done.8.refs_1_ = bf16[9,512,128]{2,1,0:T(8,128)(2,1)S(1)} collective-permute-done((bf16[9,512,128]{2,1,0:T(8,128)(2,1)S(1)}, bf16[9,512,128]{2,1,0:T(8,128)(2,1)S(1)}, u32[]{:S(2)}, u32[]{:S(2)}) %collective-permute-start.8) | collective-permute-done | bytes 1179680 | tf_op jit(solution)/shard_map/cond/branch_1_fun/ppermute | solution.py:580
  86.5 11.1 %across.6 = (f32[32,128,128]{2,1,0:T(8,128)}, bf16[32,128,128]{2,1,0:T(8,128)(2,1)}) custom-call(s32[416]{0:T(512)S(1)} %get-tuple-element.75.table, bf16[9,512,128]{2,1,0:T(8,128)(2,1)S(1)} %collective-permute-done.6.refs_0_, bf16[9,512,128]{2,1,0:T(8,128)(2,1)S(1)} %collective-permute-done.8.refs_1_, ...), custom_call_target="tpu_custom_call", output_to_operand_aliasing={{0}: (5, {}), {1}: (6, {})} | custom-call | flops 268435456 | bytes 4194304 | tf_op jit(solution)/shard_map/cond/branch_1_fun/across/pallas_call | solution.py:396
  97.8 0.1 collective-permute-start.26
  97.9 6.3 %collective-permute-start.25 = (bf16[32,128,128]{2,1,0:T(8,128)(2,1)}, bf16[32,128,128]{2,1,0:T(8,128)(2,1)S(1)}, u32[]{:S(2)}, u32[]{:S(2)}) collective-permute-start(bf16[32,128,128]{2,1,0:T(8,128)(2,1)} %get-tuple-element.155.here), channel_id=1, source_target_pairs={{1,2},{2,1},{3,4},{4,3},{5,6},{6,5},{7,8},{8,7},{9,10},{10,9},{11,... | collective-permute-start | bytes 3145736 | tf_op jit(solution)/shard_map/ppermute | solution.py:580
  104.2 0.0 collective-permute-done.26.near_by
  104.2 0.0 copy-start
  104.2 3.4 %copy-done = bf16[32,8,128,128]{3,2,1,0:T(8,128)(2,1)S(1)} copy-done((bf16[32,8,128,128]{3,2,1,0:T(8,128)(2,1)S(1)}, bf16[32,8,128,128]{3,2,1,0:T(8,128)(2,1)}, u32[]{:S(2)}) %copy-start) | copy-done | bytes 8388632
  107.6 9.7 %early.2.so_far = f32[32,128,128]{2,1,0:T(8,128)S(1)} custom-call(s32[288]{0:T(512)S(1)} %get-tuple-element.156.listed, bf16[256,128,128]{2,1,0:T(8,128)(2,1)S(1)} %bitcast.12, bf16[32,128,128]{2,1,0:T(8,128)(2,1)} %get-tuple-element.155.here, bf16[32,128,128]{2,1,0:T(8,128)(2,1)S(1)} %collective-permute-done.26.near_by, ...), custom_call_target="tpu_custom_call" | custom-call | flops 1073741824 | bytes 8388608 | tf_op jit(solution)/shard_map/early/pallas_call | solution.py:509
  117.3 1.2 collective-permute-done.25.other
  118.5 6.5 %late.1.here = bf16[32,128,128]{2,1,0:T(8,128)(2,1)S(1)} custom-call(s32[288]{0:T(512)S(1)} %get-tuple-element.154.listed, bf16[256,128,128]{2,1,0:T(8,128)(2,1)S(1)} %bitcast.13, bf16[32,128,128]{2,1,0:T(8,128)(2,1)S(1)} %collective-permute-done.25.other, f32[32,128,128]{2,1,0:T(8,128)S(1)} %early.2.so_far, f32[32,128,128]{2,1,0:T(8,128)} %get-tuple-element.158.inverse), custom_call_target="tpu_custom_call" | custom-call | flops 536870912 | bytes 8388608 | tf_op jit(solution)/shard_map/late/pallas_call | solution.py:524
  125.0 0.1 collective-permute-start.28
  125.1 6.3 %collective-permute-start.27 = (bf16[32,128,128]{2,1,0:T(8,128)(2,1)S(1)}, bf16[32,128,128]{2,1,0:T(8,128)(2,1)S(1)}, u32[]{:S(2)}, u32[]{:S(2)}) collective-permute-start(bf16[32,128,128]{2,1,0:T(8,128)(2,1)S(1)} %late.1.here), channel_id=1, source_target_pairs={{1,2},{2,1},{3,4},{4,3},{5,6},{6,5},{7,8},{8,7},{9,10},{10,9},{11,... | collective-permute-start | bytes 3145736 | tf_op jit(solution)/shard_map/ppermute | solution.py:580
  131.4 0.0 collective-permute-done.28.near_by
  131.4 9.4 %early.3.so_far = f32[32,128,128]{2,1,0:T(8,128)S(1)} custom-call(s32[288]{0:T(512)S(1)} %get-tuple-element.156.listed, bf16[256,128,128]{2,1,0:T(8,128)(2,1)S(1)} %bitcast.14, bf16[32,128,128]{2,1,0:T(8,128)(2,1)S(1)} %late.1.here, bf16[32,128,128]{2,1,0:T(8,128)(2,1)S(1)} %collective-permute-done.28.near_by, f32[32,128,128]{2,1,0:T(8,128)} %get-tuple-element.157.integ), custom_call_target="tpu_custom_call" | custom-call | flops 1073741824 | bytes 8388608 | tf_op jit(solution)/shard_map/early/pallas_call | solution.py:509
  140.8 4.6 %collective-permute-done.27.other = bf16[32,128,128]{2,1,0:T(8,128)(2,1)S(1)} collective-permute-done((bf16[32,128,128]{2,1,0:T(8,128)(2,1)S(1)}, bf16[32,128,128]{2,1,0:T(8,128)(2,1)S(1)}, u32[]{:S(2)}, u32[]{:S(2)}) %collective-permute-start.27) | collective-permute-done | bytes 1048608 | tf_op jit(solution)/shard_map/ppermute | solution.py:580
  145.4 8.9 %last.1 = (f32[32,128,128]{2,1,0:T(8,128)}, f32[1,32]{1,0:T(1,128)}) custom-call(s32[288]{0:T(512)S(1)} %get-tuple-element.154.listed, bf16[256,128,128]{2,1,0:T(8,128)(2,1)S(1)} %bitcast.15, bf16[32,128,128]{2,1,0:T(8,128)(2,1)S(1)} %collective-permute-done.27.other, f32[32,128,128]{2,1,0:T(8,128)S(1)} %early.3.so_far, ...), custom_call_target="tpu_custom_call" | custom-call | flops 536870912 | bytes 8388608 | tf_op jit(solution)/shard_map/last/pallas_call | solution.py:539
  (6 shorter events, 0.0 us)
Async XLA Ops:
  8.4 56.8 %collective-permute-start.9 = (bf16[16,512,512]{2,1,0:T(8,128)(2,1)}, bf16[16,512,512]{2,1,0:T(8,128)(2,1)S(1)}, u32[]{:S(2)}, u32[]{:S(2)}) collective-permute-start(bf16[16,512,512]{2,1,0:T(8,128)(2,1)} %get-tuple-element.71.blocks), channel_id=1, source_target_pairs={{0,1},{1,0},{2,3},{3,2},{4,5},{5,4},{6,7},{7,6},{8,9},{9,8},{10,11... | collective-permute-start | bytes 25165832 | tf_op jit(solution)/shard_map/cond/branch_1_fun/ppermute | solution.py:579
  8.4 13.4 %copy-start.6 = (f32[32]{0:T(128)S(1)}, f32[32]{0:T(128)}, u32[]{:S(2)}) copy-start(f32[32]{0:T(128)} %get-tuple-element.70.shift) | copy-start | bytes 388 | tf_op jit(solution)/shard_map/cond
  8.4 38.1 %slice-start.2 = ((s8[8388608]{0:T(1024)(128)(4,1)}), s8[4194304]{0:T(1024)(128)(4,1)S(1)}, s32[]{:S(2)}) async-start(s8[8388608]{0:T(1024)(128)(4,1)} %bitcast.18), calls=%async_computation.2 | async-start | bytes 8388608 | tf_op jit(solution)/shard_map/cond
  11.1 35.3 %collective-permute-start.5 = (bf16[9,512,128]{2,1,0:T(8,128)(2,1)S(1)}, bf16[9,512,128]{2,1,0:T(8,128)(2,1)S(1)}, u32[]{:S(2)}, u32[]{:S(2)}) collective-permute-start(bf16[9,512,128]{2,1,0:T(8,128)(2,1)S(1)} %get-tuple-element.76), channel_id=1, source_target_pairs={{1,2},{2,1},{3,4},{4,3},{5,6},{6,5},{7,8},{8,7},{9,10},{10,9},{11,... | collective-permute-start | bytes 3538952 | tf_op jit(solution)/shard_map/cond/branch_1_fun/ppermute | solution.py:580
  19.9 40.2 %collective-permute-start.7 = (bf16[9,512,128]{2,1,0:T(8,128)(2,1)S(1)}, bf16[9,512,128]{2,1,0:T(8,128)(2,1)S(1)}, u32[]{:S(2)}, u32[]{:S(2)}) collective-permute-start(bf16[9,512,128]{2,1,0:T(8,128)(2,1)S(1)} %get-tuple-element.77), channel_id=1, source_target_pairs={{1,2},{2,1},{3,4},{4,3},{5,6},{6,5},{7,8},{8,7},{9,10},{10,9},{11,... | collective-permute-start | bytes 3538952 | tf_op jit(solution)/shard_map/cond/branch_1_fun/ppermute | solution.py:580
  21.8 24.7 %slice-start.3 = ((s8[8388608]{0:T(1024)(128)(4,1)}), s8[4194304]{0:T(1024)(128)(4,1)S(1)}, s32[]{:S(2)}) async-start(s8[8388608]{0:T(1024)(128)(4,1)} %bitcast.18), calls=%async_computation.3 | async-start | bytes 8388608 | tf_op jit(solution)/shard_map/cond
  50.7 26.7 %collective-permute-start.6 = (bf16[9,512,128]{2,1,0:T(8,128)(2,1)S(1)}, bf16[9,512,128]{2,1,0:T(8,128)(2,1)S(1)}, u32[]{:S(2)}, u32[]{:S(2)}) collective-permute-start(bf16[9,512,128]{2,1,0:T(8,128)(2,1)S(1)} %serve.12), channel_id=1, source_target_pairs={{1,2},{2,1},{3,4},{4,3},{5,6},{6,5},{7,8},{8,7},{9,10},{10,9},{11,... | collective-permute-start | bytes 3538952 | tf_op jit(solution)/shard_map/cond/branch_1_fun/ppermute | solution.py:580
  60.0 5.2 %copy-start.2 = (bf16[32,512,128]{2,1,0:T(8,128)(2,1)S(1)}, bf16[32,512,128]{2,1,0:T(8,128)(2,1)}, u32[]{:S(2)}) copy-start(bf16[32,512,128]{2,1,0:T(8,128)(2,1)} %get-tuple-element.72.maps) | copy-start | bytes 12582916 | tf_op jit(solution)/shard_map/cond
  62.2 24.3 %collective-permute-start.8 = (bf16[9,512,128]{2,1,0:T(8,128)(2,1)S(1)}, bf16[9,512,128]{2,1,0:T(8,128)(2,1)S(1)}, u32[]{:S(2)}, u32[]{:S(2)}) collective-permute-start(bf16[9,512,128]{2,1,0:T(8,128)(2,1)S(1)} %serve.13), channel_id=1, source_target_pairs={{1,2},{2,1},{3,4},{4,3},{5,6},{6,5},{7,8},{8,7},{9,10},{10,9},{11,... | collective-permute-start | bytes 3538952 | tf_op jit(solution)/shard_map/cond/branch_1_fun/ppermute | solution.py:580
  97.8 6.4 %collective-permute-start.26 = (bf16[32,128,128]{2,1,0:T(8,128)(2,1)}, bf16[32,128,128]{2,1,0:T(8,128)(2,1)S(1)}, u32[]{:S(2)}, u32[]{:S(2)}) collective-permute-start(bf16[32,128,128]{2,1,0:T(8,128)(2,1)} %get-tuple-element.155.here), channel_id=1, source_target_pairs={{0,1},{1,0},{2,3},{3,2},{4,5},{5,4},{6,7},{7,6},{8,9},{9,8},{10,11... | collective-permute-start | bytes 3145736 | tf_op jit(solution)/shard_map/ppermute | solution.py:579
  97.9 20.5 %collective-permute-start.25 = (bf16[32,128,128]{2,1,0:T(8,128)(2,1)}, bf16[32,128,128]{2,1,0:T(8,128)(2,1)S(1)}, u32[]{:S(2)}, u32[]{:S(2)}) collective-permute-start(bf16[32,128,128]{2,1,0:T(8,128)(2,1)} %get-tuple-element.155.here), channel_id=1, source_target_pairs={{1,2},{2,1},{3,4},{4,3},{5,6},{6,5},{7,8},{8,7},{9,10},{10,9},{11,... | collective-permute-start | bytes 3145736 | tf_op jit(solution)/shard_map/ppermute | solution.py:580
  104.2 3.4 %copy-start = (bf16[32,8,128,128]{3,2,1,0:T(8,128)(2,1)S(1)}, bf16[32,8,128,128]{3,2,1,0:T(8,128)(2,1)}, u32[]{:S(2)}) copy-start(bf16[32,8,128,128]{3,2,1,0:T(8,128)(2,1)} %param.22) | copy-start | bytes 25165828
  125.0 6.4 %collective-permute-start.28 = (bf16[32,128,128]{2,1,0:T(8,128)(2,1)S(1)}, bf16[32,128,128]{2,1,0:T(8,128)(2,1)S(1)}, u32[]{:S(2)}, u32[]{:S(2)}) collective-permute-start(bf16[32,128,128]{2,1,0:T(8,128)(2,1)S(1)} %late.1.here), channel_id=1, source_target_pairs={{0,1},{1,0},{2,3},{3,2},{4,5},{5,4},{6,7},{7,6},{8,9},{9,8},{10,11... | collective-permute-start | bytes 3145736 | tf_op jit(solution)/shard_map/ppermute | solution.py:579
  125.1 20.3 %collective-permute-start.27 = (bf16[32,128,128]{2,1,0:T(8,128)(2,1)S(1)}, bf16[32,128,128]{2,1,0:T(8,128)(2,1)S(1)}, u32[]{:S(2)}, u32[]{:S(2)}) collective-permute-start(bf16[32,128,128]{2,1,0:T(8,128)(2,1)S(1)} %late.1.here), channel_id=1, source_target_pairs={{1,2},{2,1},{3,4},{4,3},{5,6},{6,5},{7,8},{8,7},{9,10},{10,9},{11,... | collective-permute-start | bytes 3145736 | tf_op jit(solution)/shard_map/ppermute | solution.py:580

commit v3 on v2

v3 whole, which is shorter than its diff:
```python
import functools
import math

import jax
import jax.numpy as jnp
from jax import lax
from jax.experimental import pallas as pl
from jax.experimental.pallas import tpu as pltpu
from jax.sharding import PartitionSpec as P

ITERS = 2
COUPLING = 0.35
SLOTS = (16, 18, 20, 24, 32)

ANY = pl.BlockSpec(memory_space=pl.ANY)
VMEM = pl.BlockSpec(memory_space=pltpu.VMEM)
SMEM = pl.BlockSpec(memory_space=pltpu.SMEM)

ONE, SRC, SERVE, LIVE = 0, 32, 64, 96


def call(body, outs, out_specs, in_specs, scratch, flops=0, moved=0, limit=60, aliases=None, name=None):
    return pl.pallas_call(
        body,
        out_shape=outs,
        in_specs=in_specs,
        out_specs=out_specs,
        scratch_shapes=scratch,
        input_output_aliases=aliases or {},
        compiler_params=pltpu.CompilerParams(vmem_limit_bytes=limit * 1024 * 1024),
        cost_estimate=pl.CostEstimate(flops=int(flops), bytes_accessed=int(moved), transcendentals=0),
        name=name,
    )


def dot(left, right):
    return jnp.dot(left, right, preferred_element_type=jnp.float32)


def dot_nt(left, right):
    return lax.dot_general(left, right, (((1,), (1,)), ((), ())), preferred_element_type=jnp.float32)


def dot_tn_nt(left, right):
    return lax.dot_general(left, right, (((0,), (1,)), ((), ())), preferred_element_type=jnp.float32)


def collect(count, wanted, slots, begin=None):
    def step(index, found):
        chosen = wanted(index)
        slots[found] = index
        if begin is not None:
            pl.when(chosen)(lambda: begin(index, found))
        return found + chosen.astype(jnp.int32)

    return lax.fori_loop(0, count, step, jnp.int32(0))


def by_twos(number, work, store):
    @pl.loop(0, (number + 1) // 2)
    def _(step):
        both = (2 * step, jnp.minimum(2 * step + 1, number - 1))
        done = [work(k) for k in both]
        for k, values in zip(both, done):
            store(k, values)


def plan_body(orbitals, everyone, pairs_hbm, sizes, table, branch, mine, theirs, sem):
    count = mine.shape[1] // 4
    lanes = mine.shape[1]
    devices = everyone.shape[1] // count
    device = lax.axis_index("pairs")
    side = 2 * (device % 2) - 1
    partner = device + side
    valid = (partner >= 0) & (partner < devices)
    near_by = jnp.clip(partner, 0, devices - 1)

    def fetch(who, place, k):
        start = pl.multiple_of(who // 4 * lanes, lanes)
        return pltpu.make_async_copy(pairs_hbm.at[:, pl.ds(start, lanes)], place, sem.at[k])

    copies = (fetch(device, mine, 0), fetch(near_by, theirs, 1))
    for copy in copies:
        copy.start()

    groups = devices * count // lanes
    second = jnp.concatenate([everyone[1:2, g * lanes : (g + 1) * lanes] for g in range(groups)], axis=0)
    row = lax.broadcasted_iota(jnp.int32, (groups, lanes), 0)
    lane = lax.broadcasted_iota(jnp.int32, (groups, lanes), 1)
    owner = row * (lanes // count) + lane // count
    crossing = jnp.where(second // orbitals == owner + 2 * (owner % 2) - 1, 1.0, 0.0)
    from_lane = lax.broadcasted_iota(jnp.int32, (lanes, lanes), 0) // count
    to_lane = lax.broadcasted_iota(jnp.int32, (lanes, lanes), 1)
    together = jnp.where(from_lane == to_lane, 1.0, 0.0).astype(jnp.bfloat16)
    most = jnp.max(dot(crossing.astype(jnp.bfloat16), together)).astype(jnp.int32)
    branch[0] = sum((most > s).astype(jnp.int32) for s in SLOTS[:-1])

    for copy in copies:
        copy.wait()
    base = device * orbitals
    here = device % 4 * count
    there = near_by % 4 * count

    @pl.loop(0, count)
    def _(p):
        first = mine[0, here + p]
        second = mine[1, here + p]
        local = second - base
        offset = (local >= orbitals).astype(jnp.int32) - (local < 0).astype(jnp.int32)
        kind = jnp.where(offset == 0, 0, jnp.where(offset == side, 2, 1))
        table[ONE + p] = first - base
        table[SRC + p] = kind * orbitals + local - offset * orbitals
        table[SERVE + p] = jnp.where(valid, theirs[1, there + p] - base, -1)
        table[LIVE + p] = jnp.minimum(sizes[first], sizes[second])


def plan(pair_orbitals, block_sizes, orbitals):
    turned = pair_orbitals.T
    return call(
        functools.partial(plan_body, orbitals),
        (jax.ShapeDtypeStruct((128,), jnp.int32), jax.ShapeDtypeStruct((1,), jnp.int32)),
        (SMEM, SMEM),
        [VMEM, ANY, SMEM],
        [pltpu.SMEM((2, 128), jnp.int32), pltpu.SMEM((2, 128), jnp.int32), pltpu.SemaphoreType.DMA((2,))],
        moved=turned.size * 8,
        limit=4,
        name="plan",
    )(turned, turned, block_sizes)


def pack_body(orbitals, table, maps, *refs):
    outs, slots, sem = refs[:-2], refs[-2], refs[-1]
    count = maps.shape[0]

    def begin(pair, slot):
        low = 0
        for out in outs:
            lo, hi = low, low + out.shape[0]

            @pl.when((slot >= lo) & (slot < hi))
            def _(out=out, lo=lo):
                pltpu.make_async_copy(maps.at[pair], out.at[slot - lo], sem.at[slot]).start()

            low = hi

    found = collect(count, lambda p: table[SRC + p] >= 2 * orbitals, slots, begin)

    @pl.loop(0, found)
    def _(slot):
        pltpu.make_async_copy(maps.at[0], outs[0].at[0], sem.at[slot]).wait()


def pack(table, maps, sizes, orbitals):
    count, depth, width = maps.shape
    return call(
        functools.partial(pack_body, orbitals),
        tuple(jax.ShapeDtypeStruct((s, depth, width), maps.dtype) for s in sizes),
        (VMEM,) * len(sizes),
        [SMEM, ANY],
        [pltpu.SMEM((count + 1,), jnp.int32), pltpu.SemaphoreType.DMA((count,))],
        moved=2 * sum(sizes) * depth * width * 2,
        limit=8,
        name="pack",
    )(table, maps)


def left_body(table, blocks, maps, left):
    count, width, depth = left.shape
    columns = lax.broadcasted_iota(jnp.int32, (width, depth), 1)

    def work(p):
        half = dot_tn_nt(maps[p], blocks[table[ONE + p]])
        return jnp.where(columns < table[LIVE + p], half, 0.0).astype(jnp.bfloat16)

    def store(p, half):
        left[p] = half

    by_twos(count, work, store)


def left_part(table, blocks, maps):
    orbitals, depth, wide = blocks.shape
    count, _, width = maps.shape
    return call(
        left_body,
        jax.ShapeDtypeStruct((count, width, depth), jnp.bfloat16),
        VMEM,
        [SMEM, VMEM, VMEM],
        [],
        flops=2 * count * depth * wide * width,
        moved=blocks.size * 2,
        limit=20,
        name="left",
    )(table, blocks, maps)


def own_body(scale, orbitals, table, sizes, shift, near_pairs, blocks, maps, energy, left,
             integ, start, inverse, early, late, slots):
    count, width, _ = left.shape
    near = near_pairs.shape[0]
    device = lax.axis_index("pairs")
    side = 2 * (device % 2) - 1
    ids = lax.broadcasted_iota(jnp.int32, (width, width), 0)
    across_ids = lax.broadcasted_iota(jnp.int32, (width, width), 1)

    def pair_step(pair, counts):
        soon, after = counts
        for k in range(near):
            entry = pair * near + k
            local = near_pairs[k, pair] - device * count
            offset = (local >= count).astype(jnp.int32) - (local < 0).astype(jnp.int32)
            is_late = (offset == side).astype(jnp.int32)
            code = pair * 65536 + entry * 256 + local - offset * count
            early[1 + soon] = code + jnp.where(offset == 0, 0, count)
            late[1 + after] = code
            soon = soon + 1 - is_late
            after = after + is_late
        spare = pair * 65536 + pair * near * 256
        early[1 + soon] = spare + 2 * count
        late[1 + after] = spare + count
        row = jnp.broadcast_to(energy[pl.ds(pair, 1), :], (width, width))
        bottom = row + row.T + shift[pair]
        size = sizes[pair]
        inverse[pair] = jnp.where((ids < size) & (across_ids < size), -1.0 / bottom, 0.0)
        return soon + soon % 2, after + after % 2

    soon, after = lax.fori_loop(0, count, pair_step, (jnp.int32(0), jnp.int32(0)))
    early[0] = soon // 2
    late[0] = after // 2

    @pl.loop(0, 6 * UNIT)
    def _(k):
        early[1 + soon + k] = count * 65536 + 2 * count
        late[1 + after + k] = count * 65536 + count

    found = collect(count, lambda p: table[SRC + p] < orbitals, slots)

    def work(slot):
        pair = slots[slot]
        right = dot(blocks[table[SRC + pair]], maps[pair]).astype(jnp.bfloat16)
        return dot(left[pair], right) * scale

    def store(slot, value):
        pair = slots[slot]
        integ[pair] = value
        start[pair] = (value * inverse[pair]).astype(jnp.bfloat16)

    by_twos(found, work, store)


def own_part(table, sizes, shift, near_pairs, blocks, maps, energy, left, scale):
    orbitals = blocks.shape[0]
    count, width, depth = left.shape
    entries = near_pairs.size + 6 * UNIT + 8
    return call(
        functools.partial(own_body, scale, orbitals),
        (
            jax.ShapeDtypeStruct((count, width, width), jnp.float32),
            jax.ShapeDtypeStruct((count, width, width), jnp.bfloat16),
            jax.ShapeDtypeStruct((count, width, width), jnp.float32),
            jax.ShapeDtypeStruct((entries,), jnp.int32),
            jax.ShapeDtypeStruct((entries,), jnp.int32),
        ),
        (VMEM, VMEM, VMEM, SMEM, SMEM),
        [SMEM, SMEM, SMEM, SMEM, VMEM, VMEM, VMEM, VMEM],
        [pltpu.SMEM((count + 1,), jnp.int32)],
        flops=count * depth * depth * width,
        moved=blocks.size * 2,
        limit=28,
        name="own",
    )(table, sizes, shift, near_pairs, blocks, maps, energy, left)


def serve_body(low, table, blocks, maps, out, slots):
    orbitals = blocks.shape[0]
    size = maps.shape[0]
    found = collect(
        slots.shape[0] - 1,
        lambda p: (table[SERVE + p] >= 0) & (table[SERVE + p] < orbitals),
        slots,
    )

    def work(slot):
        return dot(blocks[table[SERVE + slots[low + slot]]], maps[slot]).astype(jnp.bfloat16)

    def store(slot, half):
        out[slot] = half

    by_twos(jnp.clip(found - low, 0, size), work, store)


def serve(table, blocks, maps, low, count):
    orbitals, depth, wide = blocks.shape
    size, _, width = maps.shape
    return call(
        functools.partial(serve_body, low),
        jax.ShapeDtypeStruct((size, depth, width), jnp.bfloat16),
        VMEM,
        [SMEM, VMEM, VMEM],
        [pltpu.SMEM((count + 1,), jnp.int32)],
        flops=2 * size * depth * wide * width,
        moved=size * depth * (wide + 2 * width) * 2,
        limit=20,
        name="serve",
    )(table, blocks, maps)


def carry_over(integ_in, start_in, integ, start):
    @pl.loop(0, integ.shape[0])
    def _(p):
        integ[p] = integ_in[p]
        start[p] = start_in[p]


def beside_body(scale, table, blocks, maps, left, inverse, integ_in, start_in, integ, start, slots):
    carry_over(integ_in, start_in, integ, start)
    orbitals = blocks.shape[0]
    found = collect(
        left.shape[0],
        lambda p: (table[SRC + p] >= orbitals) & (table[SRC + p] < 2 * orbitals),
        slots,
    )

    def work(slot):
        pair = slots[slot]
        right = dot(blocks[table[SRC + pair] - orbitals], maps[pair]).astype(jnp.bfloat16)
        return dot(left[pair], right) * scale

    def store(slot, value):
        pair = slots[slot]
        integ[pair] = value
        start[pair] = (value * inverse[pair]).astype(jnp.bfloat16)

    by_twos(found, work, store)


def across_body(scale, orbitals, table, *refs):
    n = len(refs) - 8
    halves = refs[:n]
    left, inverse, integ_in, start_in, integ, start, joined, slots = refs[n:]
    carry_over(integ_in, start_in, integ, start)
    low = 0
    for half in halves:
        joined[pl.ds(low, half.shape[0])] = half[...]
        low += half.shape[0]
    found = collect(left.shape[0], lambda p: table[SRC + p] >= 2 * orbitals, slots)

    def work(slot):
        return dot(left[slots[slot]], joined[slot]) * scale

    def store(slot, value):
        pair = slots[slot]
        integ[pair] = value
        start[pair] = (value * inverse[pair]).astype(jnp.bfloat16)

    by_twos(found, work, store)


def integrals_part(body, table, operands, left, inverse, integ, start, scratch, limit, name):
    count, width, depth = left.shape
    n = len(operands)
    return call(
        body,
        (
            jax.ShapeDtypeStruct(integ.shape, integ.dtype),
            jax.ShapeDtypeStruct(start.shape, start.dtype),
        ),
        (VMEM, VMEM),
        [SMEM] + [VMEM] * (n + 4),
        scratch + [pltpu.SMEM((count + 1,), jnp.int32)],
        flops=count * depth * depth * width,
        moved=count * depth * width * 2,
        limit=limit,
        name=name,
    )(table, *operands, left, inverse, integ, start)


UNIT = 4


def couple(listed, inter, tables, total, amps, ahead, behind):
    count = total.shape[0] - 1
    width = total.shape[1]
    low = 0
    for table in tables:
        amps[pl.ds(low, table.shape[0])] = table[...]
        low += table.shape[0]
    amps[low] = jnp.zeros(amps.shape[1:], amps.dtype)

    @pl.loop(0, count + 1)
    def _(p):
        total[p] = jnp.zeros(total.shape[1:], jnp.float32)

    def codes(group):
        for k in range(UNIT):
            place = 1 + (group * UNIT + k) * 2
            one, two = listed[place], listed[place + 1]
            yield k, one // 65536, (one // 256) % 256, one % 256, (two // 256) % 256, two % 256

    def first(group, mixed):
        for k, _, one, amp_one, two, amp_two in codes(group):
            mixed[k, :, 0:width] = dot(inter[one], amps[amp_one]).astype(jnp.bfloat16)
            mixed[k, :, width : 2 * width] = dot(inter[two], amps[amp_two]).astype(jnp.bfloat16)

    def second(group, mixed):
        for k, pair, one, _, two, _ in codes(group):
            total[pair] += dot_nt(mixed[k], jnp.concatenate([inter[one], inter[two]], axis=1))

    first(0, ahead)

    @pl.loop(0, (listed[0] + 2 * UNIT - 1) // (2 * UNIT))
    def _(step):
        first(2 * step + 1, behind)
        second(2 * step, ahead)
        first(2 * step + 2, ahead)
        second(2 * step + 1, behind)


def early_body(listed, inter, here, near_by, integ, out, total, *scratch):
    couple(listed, inter, (here, near_by), total, *scratch)

    @pl.loop(0, integ.shape[0])
    def _(p):
        out[p] = integ[p] + COUPLING * total[p]


def late_body(listed, inter, other, so_far, inverse, out, total, *scratch):
    couple(listed, inter, (other,), total, *scratch)

    @pl.loop(0, so_far.shape[0])
    def _(p):
        out[p] = ((so_far[p] + COUPLING * total[p]) * inverse[p]).astype(out.dtype)


def last_body(listed, inter, other, so_far, inverse, integ, out, energy, rows, total, *scratch):
    couple(listed, inter, (other,), total, *scratch)
    width = total.shape[1]

    @pl.loop(0, so_far.shape[0])
    def _(p):
        value = (so_far[p] + COUPLING * total[p]) * inverse[p]
        out[p] = value
        rows[pl.ds(p, 1), :] = jnp.sum(integ[p] * value, axis=0, keepdims=True)

    sums = lax.dot_general(
        jnp.ones((8, width), jnp.float32),
        rows[...],
        (((1,), (1,)), ((), ())),
        precision=lax.Precision.HIGHEST,
        preferred_element_type=jnp.float32,
    )
    energy[...] = sums[0:1, :] * (1.0 / (width * width))


def coupling_scratch(count, width, tables):
    return [
        pltpu.VMEM((count + 1, width, width), jnp.float32),
        pltpu.VMEM((tables * count + 1, width, width), jnp.bfloat16),
        pltpu.VMEM((UNIT, width, 2 * width), jnp.bfloat16),
        pltpu.VMEM((UNIT, width, 2 * width), jnp.bfloat16),
    ]


def early_part(listed, inter, here, other, integ):
    count, width, _ = integ.shape
    return call(
        early_body,
        jax.ShapeDtypeStruct(integ.shape, jnp.float32),
        VMEM,
        [SMEM, VMEM, VMEM, VMEM, VMEM],
        coupling_scratch(count, width, 2),
        flops=2 * inter.shape[0] * width**3,
        moved=inter.size * 2,
        limit=24,
        name="early",
    )(listed, inter, here, other, integ)


def late_part(listed, inter, other, so_far, inverse):
    count, width, _ = so_far.shape
    return call(
        late_body,
        jax.ShapeDtypeStruct(so_far.shape, jnp.bfloat16),
        VMEM,
        [SMEM, VMEM, VMEM, VMEM, VMEM],
        coupling_scratch(count, width, 1),
        flops=inter.shape[0] * width**3,
        moved=inter.size * 2,
        limit=24,
        name="late",
    )(listed, inter, other, so_far, inverse)


def last_part(listed, inter, other, so_far, inverse, integ):
    count, width, _ = so_far.shape
    return call(
        last_body,
        (
            jax.ShapeDtypeStruct(so_far.shape, jnp.float32),
            jax.ShapeDtypeStruct((1, count), jnp.float32),
        ),
        (VMEM, VMEM),
        [SMEM, VMEM, VMEM, VMEM, VMEM, VMEM],
        [pltpu.VMEM((count, width), jnp.float32)] + coupling_scratch(count, width, 1),
        flops=inter.shape[0] * width**3,
        moved=inter.size * 2,
        limit=24,
        name="last",
    )(listed, inter, other, so_far, inverse, integ)


def shards(
    blocks,
    pair_orbitals,
    block_sizes,
    pno_maps,
    pno_sizes,
    pno_energy,
    pair_shift,
    neighbours,
    intersections,
):
    devices = lax.axis_size("pairs")
    count, wide, width = pno_maps.shape
    orbitals, depth, _ = blocks.shape
    near = neighbours.shape[1]
    scale = 1.0 / math.sqrt(depth)
    beside_perm = [(i, i ^ 1) for i in range(devices)]
    across_perm = []
    for i in range(1, devices - 1, 2):
        across_perm += [(i, i + 1), (i + 1, i)]
    swap_beside = lambda x: lax.ppermute(x, "pairs", beside_perm)
    swap_across = lambda x: lax.ppermute(x, "pairs", across_perm)

    inter = intersections.reshape(count * near, width, width)
    table, branch = plan(pair_orbitals, block_sizes, orbitals)

    def after(value, *before):
        return lax.optimization_barrier((value,) + before)[0]

    def integrals_with(slots):
        def run(table, blocks, maps, energy, shift, sizes, near_pairs):
            blocks_beside = swap_beside(blocks)
            packed = pack(table, maps, (slots // 2, slots - slots // 2), orbitals)
            got = [swap_across(x) for x in packed]
            left = left_part(table, blocks, maps)
            integ, start, inverse, early, late = own_part(
                table, sizes, shift, near_pairs, blocks, maps, energy, left, scale
            )
            half_one = serve(after(table, early), blocks, got[0], 0, count)
            back_one = swap_across(half_one)
            integ, start = integrals_part(
                functools.partial(beside_body, scale),
                after(table, half_one),
                (blocks_beside, maps),
                left,
                inverse,
                integ,
                start,
                [],
                24,
                "beside",
            )
            half_two = serve(after(table, start), blocks, got[1], got[0].shape[0], count)
            back_two = swap_across(half_two)
            integ, start = integrals_part(
                functools.partial(across_body, scale, orbitals),
                table,
                (back_one, back_two),
                left,
                inverse,
                integ,
                start,
                [pltpu.VMEM((slots, depth, width), jnp.bfloat16)],
                24,
                "across",
            )
            return integ, start, inverse, early, late

        return run

    integ, amps, inverse, early, late = lax.switch(
        branch[0],
        [integrals_with(s) for s in SLOTS],
        table,
        blocks,
        pno_maps,
        pno_energy,
        pair_shift,
        pno_sizes,
        neighbours.T,
    )
    for iteration in range(ITERS):
        far = swap_across(amps)
        close = swap_beside(amps)
        so_far = early_part(early, inter, amps, close, integ)
        if iteration < ITERS - 1:
            amps = late_part(late, inter, far, so_far, inverse)
        else:
            amps, energies = last_part(late, inter, far, so_far, inverse, integ)
    return (amps, energies.reshape(count))


def solution(mesh):
    in_specs = (
        P("pairs", None, None),
        P(),
        P(),
        P("pairs", None, None),
        P("pairs"),
        P("pairs", None),
        P("pairs"),
        P("pairs", None),
        P("pairs", None, None, None),
    )
    out_specs = (P("pairs", None, None), P("pairs"))
    return jax.shard_map(shards, mesh=mesh, in_specs=in_specs, out_specs=out_specs, check_vma=False)
```

time: 155 us -> 143 us (0.923)
  waiting for transfers between devices: 15 us -> 33.9 us
  Pallas kernels: 91.5 us -> 73.1 us
  starting transfers between devices: 35.6 us -> 28.3 us
  between operations: 3.39 us -> 1.39 us
  local copies, waits for them, and re-layouts: 6.73 us -> 4.87 us
  other arithmetic: 1.74 us -> 0.01 us
    ppermute x6, waiting for transfers between devices: 15 us -> 33.9 us  [shards(): swap_across = lambda x: lax.ppermute(x, 'pairs', across_perm)]
    pallas_call x3 -> x5, Pallas kernels: 47.8 us -> 36 us  [the longest x2 11.5 us: integrals_part(): call(body, (jax.ShapeDtypeStruct(integ.shape, integ.dtype), jax.ShapeDtyp...]
    ppermute x6, starting transfers between devices: 35.5 us -> 28.1 us  [shards(): swap_across = lambda x: lax.ppermute(x, 'pairs', across_perm)]
    pallas_call x2, Pallas kernels: 19 us -> 16.7 us  [early_part(): call(early_body, jax.ShapeDtypeStruct(integ.shape, jnp.float32), VMEM, [S...]
    pallas_call x2, Pallas kernels: 6.36 us -> 4.27 us  [serve(): call(functools.partial(serve_body, low), jax.ShapeDtypeStruct((size, dept...]
    dynamic_slice x2 -> x0, local copies, waits for them, and re-layouts: 1.55 us -> none  [the longest x1 0.78 us: shards(): lax.dynamic_slice_in_dim(pair_orbitals, jnp.clip(partner, 0, devices - 1)...]
    unnamed x2 -> x6, local copies, waits for them, and re-layouts: 3.38 us -> 4.82 us
  transfers between devices with their start and end apart: 9 -> 9, of which waited for: 3 -> 4; matrix products, arithmetic and copies ran while one was open for 0% -> 0% of each run, Pallas kernels for 42% -> 38%
where the time goes in v3:
time: 143 us; the launch traced here: 142 us
  Pallas kernels  73.1 us (51%)
  waiting for transfers between devices  33.9 us (24%)
  starting transfers between devices  28.3 us (20%)
  local copies, waits for them, and re-layouts  4.87 us (3%)
    ppermute x6, waiting for transfers between devices, shards(): swap_across = lambda x: lax.ppermute(x, 'pairs', across_perm)  33.9 us
    ppermute x6, starting transfers between devices, shards(): swap_across = lambda x: lax.ppermute(x, 'pairs', across_perm)  28.1 us
    pallas_call x2, Pallas kernels, early_part(): call(early_body, jax.ShapeDtypeStruct(integ.shape, jnp.float32), VMEM, [S...  16.7 us
    pallas_call x2, Pallas kernels, integrals_part(): call(body, (jax.ShapeDtypeStruct(integ.shape, integ.dtype), jax.ShapeDtyp...  11.5 us
    pallas_call x1, Pallas kernels, left_part(): call(left_body, jax.ShapeDtypeStruct((count, width, depth), jnp.bfloat16)...  11.2 us
    pallas_call x1, Pallas kernels, own_part(): call(functools.partial(own_body, scale, orbitals), (jax.ShapeDtypeStruct(...  11 us
    pallas_call x1, Pallas kernels, last_part(): call(last_body, (jax.ShapeDtypeStruct(so_far.shape, jnp.float32), jax.Sha...  7.72 us
    pallas_call x1, Pallas kernels, late_part(): call(late_body, jax.ShapeDtypeStruct(so_far.shape, jnp.bfloat16), VMEM, [...  5.95 us
  transfers between devices with their start and end apart: 9, of which 4 were waited for; matrix products, arithmetic and copies ran while one was open for 0% of the time, Pallas kernels for 38%

profile of v3, /device:TPU:6, one launch (start us, length us, event | category | flops | bytes accessed | tf_op | source)
XLA Modules:
  0.0 142.1 jit_solution(3864125705887121173)
XLA Ops:
  0.6 0.0 copy-start.1
  0.6 0.7 copy-done.1
  1.4 0.0 copy-start.2
  1.4 0.7 copy-done.2
  2.1 2.3 %plan.1 = (s32[128]{0:T(128)S(1)}, s32[1]{0:T(128)}) custom-call(s32[2,4096]{1,0:T(2,128)S(1)} %bitcast.9, s32[2,4096]{1,0:T(2,128)S(1)} %bitcast.10, s32[2048]{0:T(1024)S(1)} %copy-done.2), custom_call_target="tpu_custom_call" | custom-call | bytes 65536 | tf_op jit(solution)/shard_map/plan/pallas_call | solution.py:119
  5.1 82.5 %conditional.1 = (f32[32,128,128]{2,1,0:T(8,128)S(1)}, bf16[32,128,128]{2,1,0:T(8,128)(2,1)S(1)}, f32[32,128,128]{2,1,0:T(8,128)}, s32[288]{0:T(512)S(1)}, s32[288]{0:T(512)S(1)}) conditional(s32[]{:T(128)} %bitcast.1, (s32[128]{0:T(128)S(1)}, bf16[16,512,512]{2,1,0:T(8,128)(2,1)}, bf16[32,512,128]{2,1,0:T(8,128)(2,1)}, ...), branch_computations={%region_0.0_spmd, %region_1.0_spmd, %region_2.0_spmd, %region_3.0_... | conditional | flops 7516192768 | bytes 167843264 | solution.py:582
  5.1 0.1 collective-permute-start.7
  5.2 0.0 copy-start.4
  5.2 2.5 %pack.6 = (bf16[9,512,128]{2,1,0:T(8,128)(2,1)S(1)}, bf16[9,512,128]{2,1,0:T(8,128)(2,1)S(1)}) custom-call(s32[128]{0:T(128)S(1)} %get-tuple-element.106.table, bf16[32,512,128]{2,1,0:T(8,128)(2,1)} %get-tuple-element.96.maps), custom_call_target="tpu_custom_call" | custom-call | bytes 4718592 | tf_op jit(solution)/shard_map/cond/branch_1_fun/pack/pallas_call | solution.py:155
  7.7 8.7 %collective-permute-start.5 = (bf16[9,512,128]{2,1,0:T(8,128)(2,1)S(1)}, bf16[9,512,128]{2,1,0:T(8,128)(2,1)S(1)}, u32[]{:S(2)}, u32[]{:S(2)}) collective-permute-start(bf16[9,512,128]{2,1,0:T(8,128)(2,1)S(1)} %get-tuple-element.100), channel_id=1, source_target_pairs={{1,2},{2,1},{3,4},{4,3},{5,6},{6,5},{7,8},{8,7},{9,10},{10,9},{11,... | collective-permute-start | bytes 3538952 | tf_op jit(solution)/shard_map/cond/branch_1_fun/ppermute | solution.py:533
  16.5 0.0 slice-start.2
  16.5 0.0 slice-start.3
  16.5 0.0 copy-start.9
  16.5 0.0 copy-start.14
  16.5 0.0 copy-start.19
  16.5 0.0 copy-start.24
  16.6 2.3 %collective-permute-start.8 = (bf16[9,512,128]{2,1,0:T(8,128)(2,1)S(1)}, bf16[9,512,128]{2,1,0:T(8,128)(2,1)S(1)}, u32[]{:S(2)}, u32[]{:S(2)}) collective-permute-start(bf16[9,512,128]{2,1,0:T(8,128)(2,1)S(1)} %get-tuple-element.107), channel_id=1, source_target_pairs={{1,2},{2,1},{3,4},{4,3},{5,6},{6,5},{7,8},{8,7},{9,10},{10,9},{11,... | collective-permute-start | bytes 3538952 | tf_op jit(solution)/shard_map/cond/branch_1_fun/ppermute | solution.py:533
  18.9 0.0 copy-done.4
  18.9 11.2 %left.6.refs_2_ = bf16[32,128,512]{2,1,0:T(8,128)(2,1)S(1)} custom-call(s32[128]{0:T(128)S(1)} %get-tuple-element.106.table, bf16[16,512,512]{2,1,0:T(8,128)(2,1)} %get-tuple-element.95.blocks, bf16[32,512,128]{2,1,0:T(8,128)(2,1)S(1)} %copy-done.4), custom_call_target="tpu_custom_call" | custom-call | flops 2147483648 | bytes 8388608 | tf_op jit(solution)/shard_map/cond/branch_1_fun/left/pallas_call | solution.py:184
  30.1 0.0 slice-done.2
  30.1 0.0 slice-done.3
  30.1 0.0 copy-done.9
  30.1 0.0 copy-done.14
  30.1 0.0 copy-done.19
  30.1 0.0 copy-done.24
  30.1 11.0 %own.6 = (f32[32,128,128]{2,1,0:T(8,128)S(1)}, bf16[32,128,128]{2,1,0:T(8,128)(2,1)S(1)}, f32[32,128,128]{2,1,0:T(8,128)}, s32[288]{0:T(512)S(1)}, s32[288]{0:T(512)S(1)}) custom-call(s32[128]{0:T(128)S(1)} %get-tuple-element.106.table, s32[32]{0:T(128)S(1)} %copy-done.19, f32[32]{0:T(128)S(1)} %copy-done.24, s32[8,32]{1,0:T(8,128)S(1)} %copy-done.14, ...), custom_call_target="tpu_custom_call" | custom-call | flops 1073741824 | bytes 8388608 | tf_op jit(solution)/shard_map/cond/branch_1_fun/own/pallas_call | solution.py:255
  41.2 0.0 collective-permute-done.5.maps
  41.2 3.0 %serve.12 = bf16[9,512,128]{2,1,0:T(8,128)(2,1)S(1)} custom-call(s32[128]{0:T(128)S(1)} %get-tuple-element.106.table, bf16[16,512,512]{2,1,0:T(8,128)(2,1)S(1)} %bitcast.14, bf16[9,512,128]{2,1,0:T(8,128)(2,1)S(1)} %collective-permute-done.5.maps), custom_call_target="tpu_custom_call" | custom-call | flops 603979776 | bytes 7077888 | tf_op jit(solution)/shard_map/cond/branch_1_fun/serve/pallas_call | solution.py:295
  44.2 8.6 %collective-permute-start.6 = (bf16[9,512,128]{2,1,0:T(8,128)(2,1)S(1)}, bf16[9,512,128]{2,1,0:T(8,128)(2,1)S(1)}, u32[]{:S(2)}, u32[]{:S(2)}) collective-permute-start(bf16[9,512,128]{2,1,0:T(8,128)(2,1)S(1)} %serve.12), channel_id=1, source_target_pairs={{1,2},{2,1},{3,4},{4,3},{5,6},{6,5},{7,8},{8,7},{9,10},{10,9},{11,... | collective-permute-start | bytes 3538952 | tf_op jit(solution)/shard_map/cond/branch_1_fun/ppermute | solution.py:533
  52.8 0.0 collective-permute-done.7.blocks
  52.8 8.1 %beside.6 = (f32[32,128,128]{2,1,0:T(8,128)S(1)}, bf16[32,128,128]{2,1,0:T(8,128)(2,1)S(1)}) custom-call(s32[128]{0:T(128)S(1)} %get-tuple-element.106.table, bf16[16,512,512]{2,1,0:T(8,128)(2,1)S(1)} %collective-permute-done.7.blocks, bf16[32,512,128]{2,1,0:T(8,128)(2,1)S(1)} %copy-done.4, bf16[32,128,512]{2,1,0:T(8,128)(2,1)S(1)} %left.6.refs_2_, ...), custom_call_target="tpu_custom_call" | custom-call | flops 1073741824 | bytes 4194304 | tf_op jit(solution)/shard_map/cond/branch_1_fun/beside/pallas_call | solution.py:362
  60.9 0.0 collective-permute-done.8.maps
  61.0 1.2 serve.13
  62.2 1.9 %collective-permute-start.9 = (bf16[9,512,128]{2,1,0:T(8,128)(2,1)S(1)}, bf16[9,512,128]{2,1,0:T(8,128)(2,1)S(1)}, u32[]{:S(2)}, u32[]{:S(2)}) collective-permute-start(bf16[9,512,128]{2,1,0:T(8,128)(2,1)S(1)} %serve.13), channel_id=1, source_target_pairs={{1,2},{2,1},{3,4},{4,3},{5,6},{6,5},{7,8},{8,7},{9,10},{10,9},{11,... | collective-permute-start | bytes 3538952 | tf_op jit(solution)/shard_map/cond/branch_1_fun/ppermute | solution.py:533
  64.1 2.5 %collective-permute-done.6.refs_0_ = bf16[9,512,128]{2,1,0:T(8,128)(2,1)S(1)} collective-permute-done((bf16[9,512,128]{2,1,0:T(8,128)(2,1)S(1)}, bf16[9,512,128]{2,1,0:T(8,128)(2,1)S(1)}, u32[]{:S(2)}, u32[]{:S(2)}) %collective-permute-start.6) | collective-permute-done | bytes 1179680 | tf_op jit(solution)/shard_map/cond/branch_1_fun/ppermute | solution.py:533
  66.7 17.3 %collective-permute-done.9.refs_1_ = bf16[9,512,128]{2,1,0:T(8,128)(2,1)S(1)} collective-permute-done((bf16[9,512,128]{2,1,0:T(8,128)(2,1)S(1)}, bf16[9,512,128]{2,1,0:T(8,128)(2,1)S(1)}, u32[]{:S(2)}, u32[]{:S(2)}) %collective-permute-start.9) | collective-permute-done | bytes 1179680 | tf_op jit(solution)/shard_map/cond/branch_1_fun/ppermute | solution.py:533
  84.0 3.4 %across.6 = (f32[32,128,128]{2,1,0:T(8,128)S(1)}, bf16[32,128,128]{2,1,0:T(8,128)(2,1)S(1)}) custom-call(s32[128]{0:T(128)S(1)} %get-tuple-element.106.table, bf16[9,512,128]{2,1,0:T(8,128)(2,1)S(1)} %collective-permute-done.6.refs_0_, bf16[9,512,128]{2,1,0:T(8,128)(2,1)S(1)} %collective-permute-done.9.refs_1_, bf16[32,128,512]{2,1,0:T(8,128)(2,1)S(1)} %left.6.refs_2_, ...), custom_call_target="tpu_custom_call" | custom-call | flops 1073741824 | bytes 4194304 | tf_op jit(solution)/shard_map/cond/branch_1_fun/across/pallas_call | solution.py:362
  87.6 0.1 collective-permute-start.26
  87.7 3.2 %collective-permute-start.25 = (bf16[32,128,128]{2,1,0:T(8,128)(2,1)S(1)}, bf16[32,128,128]{2,1,0:T(8,128)(2,1)S(1)}, u32[]{:S(2)}, u32[]{:S(2)}) collective-permute-start(bf16[32,128,128]{2,1,0:T(8,128)(2,1)S(1)} %get-tuple-element.189.here), channel_id=1, source_target_pairs={{1,2},{2,1},{3,4},{4,3},{5,6},{6,5},{7,8},{8,7},{9,10},{10,9},{11,... | collective-permute-start | bytes 3145736 | tf_op jit(solution)/shard_map/ppermute | solution.py:533
  90.9 0.0 collective-permute-done.26.near_by
  90.9 0.0 copy-start
  90.9 3.4 %copy-done = bf16[32,8,128,128]{3,2,1,0:T(8,128)(2,1)S(1)} copy-done((bf16[32,8,128,128]{3,2,1,0:T(8,128)(2,1)S(1)}, bf16[32,8,128,128]{3,2,1,0:T(8,128)(2,1)}, u32[]{:S(2)}) %copy-start) | copy-done | bytes 8388632
  94.3 8.3 %early.2.so_far = f32[32,128,128]{2,1,0:T(8,128)S(1)} custom-call(s32[288]{0:T(512)S(1)} %get-tuple-element.190.listed, bf16[256,128,128]{2,1,0:T(8,128)(2,1)S(1)} %bitcast.5, bf16[32,128,128]{2,1,0:T(8,128)(2,1)S(1)} %get-tuple-element.189.here, bf16[32,128,128]{2,1,0:T(8,128)(2,1)S(1)} %collective-permute-done.26.near_by, ...), custom_call_target="tpu_custom_call" | custom-call | flops 1073741824 | bytes 8388608 | tf_op jit(solution)/shard_map/early/pallas_call | solution.py:466
  102.6 5.4 %collective-permute-done.25.other = bf16[32,128,128]{2,1,0:T(8,128)(2,1)S(1)} collective-permute-done((bf16[32,128,128]{2,1,0:T(8,128)(2,1)S(1)}, bf16[32,128,128]{2,1,0:T(8,128)(2,1)S(1)}, u32[]{:S(2)}, u32[]{:S(2)}) %collective-permute-start.25) | collective-permute-done | bytes 1048608 | tf_op jit(solution)/shard_map/ppermute | solution.py:533
  108.0 6.0 %late.1.here = bf16[32,128,128]{2,1,0:T(8,128)(2,1)S(1)} custom-call(s32[288]{0:T(512)S(1)} %get-tuple-element.188.listed, bf16[256,128,128]{2,1,0:T(8,128)(2,1)S(1)} %bitcast.6, bf16[32,128,128]{2,1,0:T(8,128)(2,1)S(1)} %collective-permute-done.25.other, f32[32,128,128]{2,1,0:T(8,128)S(1)} %early.2.so_far, f32[32,128,128]{2,1,0:T(8,128)} %get-tuple-element.192.inverse), custom_call_target="tpu_custom_call" | custom-call | flops 536870912 | bytes 8388608 | tf_op jit(solution)/shard_map/late/pallas_call | solution.py:481
  113.9 0.1 collective-permute-start.28
  114.0 3.2 %collective-permute-start.27 = (bf16[32,128,128]{2,1,0:T(8,128)(2,1)S(1)}, bf16[32,128,128]{2,1,0:T(8,128)(2,1)S(1)}, u32[]{:S(2)}, u32[]{:S(2)}) collective-permute-start(bf16[32,128,128]{2,1,0:T(8,128)(2,1)S(1)} %late.1.here), channel_id=1, source_target_pairs={{1,2},{2,1},{3,4},{4,3},{5,6},{6,5},{7,8},{8,7},{9,10},{10,9},{11,... | collective-permute-start | bytes 3145736 | tf_op jit(solution)/shard_map/ppermute | solution.py:533
  117.3 0.0 collective-permute-done.28.near_by
  117.3 8.3 %early.3.so_far = f32[32,128,128]{2,1,0:T(8,128)S(1)} custom-call(s32[288]{0:T(512)S(1)} %get-tuple-element.190.listed, bf16[256,128,128]{2,1,0:T(8,128)(2,1)S(1)} %bitcast.7, bf16[32,128,128]{2,1,0:T(8,128)(2,1)S(1)} %late.1.here, bf16[32,128,128]{2,1,0:T(8,128)(2,1)S(1)} %collective-permute-done.28.near_by, f32[32,128,128]{2,1,0:T(8,128)S(1)} %get-tuple-element.191.integ), custom_call_target="tpu_custom_call" | custom-call | flops 1073741824 | bytes 8388608 | tf_op jit(solution)/shard_map/early/pallas_call | solution.py:466
  125.6 8.7 %collective-permute-done.27.other = bf16[32,128,128]{2,1,0:T(8,128)(2,1)S(1)} collective-permute-done((bf16[32,128,128]{2,1,0:T(8,128)(2,1)S(1)}, bf16[32,128,128]{2,1,0:T(8,128)(2,1)S(1)}, u32[]{:S(2)}, u32[]{:S(2)}) %collective-permute-start.27) | collective-permute-done | bytes 1048608 | tf_op jit(solution)/shard_map/ppermute | solution.py:533
  134.4 7.7 %last.1 = (f32[32,128,128]{2,1,0:T(8,128)}, f32[1,32]{1,0:T(1,128)}) custom-call(s32[288]{0:T(512)S(1)} %get-tuple-element.188.listed, bf16[256,128,128]{2,1,0:T(8,128)(2,1)S(1)} %bitcast.8, bf16[32,128,128]{2,1,0:T(8,128)(2,1)S(1)} %collective-permute-done.27.other, f32[32,128,128]{2,1,0:T(8,128)S(1)} %early.3.so_far, ...), custom_call_target="tpu_custom_call" | custom-call | flops 536870912 | bytes 8388608 | tf_op jit(solution)/shard_map/last/pallas_call | solution.py:496
  (1 shorter events, 0.0 us)
Async XLA Ops:
  0.6 0.8 copy-start.1
  1.4 0.7 copy-start.2
  5.1 47.7 %collective-permute-start.7 = (bf16[16,512,512]{2,1,0:T(8,128)(2,1)}, bf16[16,512,512]{2,1,0:T(8,128)(2,1)S(1)}, u32[]{:S(2)}, u32[]{:S(2)}) collective-permute-start(bf16[16,512,512]{2,1,0:T(8,128)(2,1)} %get-tuple-element.95.blocks), channel_id=1, source_target_pairs={{0,1},{1,0},{2,3},{3,2},{4,5},{5,4},{6,7},{7,6},{8,9},{9,8},{10,11... | collective-permute-start | bytes 25165832 | tf_op jit(solution)/shard_map/cond/branch_1_fun/ppermute | solution.py:532
  5.2 13.7 %copy-start.4 = (bf16[32,512,128]{2,1,0:T(8,128)(2,1)S(1)}, bf16[32,512,128]{2,1,0:T(8,128)(2,1)}, u32[]{:S(2)}) copy-start(bf16[32,512,128]{2,1,0:T(8,128)(2,1)} %get-tuple-element.96.maps) | copy-start | bytes 12582916 | tf_op jit(solution)/shard_map/cond
  7.7 33.4 %collective-permute-start.5 = (bf16[9,512,128]{2,1,0:T(8,128)(2,1)S(1)}, bf16[9,512,128]{2,1,0:T(8,128)(2,1)S(1)}, u32[]{:S(2)}, u32[]{:S(2)}) collective-permute-start(bf16[9,512,128]{2,1,0:T(8,128)(2,1)S(1)} %get-tuple-element.100), channel_id=1, source_target_pairs={{1,2},{2,1},{3,4},{4,3},{5,6},{6,5},{7,8},{8,7},{9,10},{10,9},{11,... | collective-permute-start | bytes 3538952 | tf_op jit(solution)/shard_map/cond/branch_1_fun/ppermute | solution.py:533
  16.5 13.6 %slice-start.2 = ((s8[8388608]{0:T(1024)(128)(4,1)}), s8[4194304]{0:T(1024)(128)(4,1)S(1)}, s32[]{:S(2)}) async-start(s8[8388608]{0:T(1024)(128)(4,1)} %bitcast.13), calls=%async_computation.2 | async-start | bytes 8388608 | tf_op jit(solution)/shard_map/cond
  16.5 13.6 %slice-start.3 = ((s8[8388608]{0:T(1024)(128)(4,1)}), s8[4194304]{0:T(1024)(128)(4,1)S(1)}, s32[]{:S(2)}) async-start(s8[8388608]{0:T(1024)(128)(4,1)} %bitcast.13), calls=%async_computation.3 | async-start | bytes 8388608 | tf_op jit(solution)/shard_map/cond
  16.5 13.6 %copy-start.9 = (f32[32,128]{1,0:T(8,128)S(1)}, f32[32,128]{1,0:T(8,128)}, u32[]{:S(2)}) copy-start(f32[32,128]{1,0:T(8,128)} %get-tuple-element.97.energy) | copy-start | bytes 49156 | tf_op jit(solution)/shard_map/cond
  16.5 13.6 %copy-start.14 = (s32[8,32]{1,0:T(8,128)S(1)}, s32[8,32]{1,0:T(8,128)}, u32[]{:S(2)}) copy-start(s32[8,32]{1,0:T(8,128)} %get-tuple-element.94.near_pairs) | copy-start | bytes 3076 | tf_op jit(solution)/shard_map/cond
  16.5 13.6 %copy-start.19 = (s32[32]{0:T(128)S(1)}, s32[32]{0:T(128)}, u32[]{:S(2)}) copy-start(s32[32]{0:T(128)} %get-tuple-element.92.sizes) | copy-start | bytes 388 | tf_op jit(solution)/shard_map/cond
  16.5 13.6 %copy-start.24 = (f32[32]{0:T(128)S(1)}, f32[32]{0:T(128)}, u32[]{:S(2)}) copy-start(f32[32]{0:T(128)} %get-tuple-element.93.shift) | copy-start | bytes 388 | tf_op jit(solution)/shard_map/cond
  16.6 44.4 %collective-permute-start.8 = (bf16[9,512,128]{2,1,0:T(8,128)(2,1)S(1)}, bf16[9,512,128]{2,1,0:T(8,128)(2,1)S(1)}, u32[]{:S(2)}, u32[]{:S(2)}) collective-permute-start(bf16[9,512,128]{2,1,0:T(8,128)(2,1)S(1)} %get-tuple-element.107), channel_id=1, source_target_pairs={{1,2},{2,1},{3,4},{4,3},{5,6},{6,5},{7,8},{8,7},{9,10},{10,9},{11,... | collective-permute-start | bytes 3538952 | tf_op jit(solution)/shard_map/cond/branch_1_fun/ppermute | solution.py:533
  44.2 22.5 %collective-permute-start.6 = (bf16[9,512,128]{2,1,0:T(8,128)(2,1)S(1)}, bf16[9,512,128]{2,1,0:T(8,128)(2,1)S(1)}, u32[]{:S(2)}, u32[]{:S(2)}) collective-permute-start(bf16[9,512,128]{2,1,0:T(8,128)(2,1)S(1)} %serve.12), channel_id=1, source_target_pairs={{1,2},{2,1},{3,4},{4,3},{5,6},{6,5},{7,8},{8,7},{9,10},{10,9},{11,... | collective-permute-start | bytes 3538952 | tf_op jit(solution)/shard_map/cond/branch_1_fun/ppermute | solution.py:533
  62.2 21.7 %collective-permute-start.9 = (bf16[9,512,128]{2,1,0:T(8,128)(2,1)S(1)}, bf16[9,512,128]{2,1,0:T(8,128)(2,1)S(1)}, u32[]{:S(2)}, u32[]{:S(2)}) collective-permute-start(bf16[9,512,128]{2,1,0:T(8,128)(2,1)S(1)} %serve.13), channel_id=1, source_target_pairs={{1,2},{2,1},{3,4},{4,3},{5,6},{6,5},{7,8},{8,7},{9,10},{10,9},{11,... | collective-permute-start | bytes 3538952 | tf_op jit(solution)/shard_map/cond/branch_1_fun/ppermute | solution.py:533
  87.6 3.3 %collective-permute-start.26 = (bf16[32,128,128]{2,1,0:T(8,128)(2,1)S(1)}, bf16[32,128,128]{2,1,0:T(8,128)(2,1)S(1)}, u32[]{:S(2)}, u32[]{:S(2)}) collective-permute-start(bf16[32,128,128]{2,1,0:T(8,128)(2,1)S(1)} %get-tuple-element.189.here), channel_id=1, source_target_pairs={{0,1},{1,0},{2,3},{3,2},{4,5},{5,4},{6,7},{7,6},{8,9},{9,8},{10,11... | collective-permute-start | bytes 3145736 | tf_op jit(solution)/shard_map/ppermute | solution.py:532
  87.7 20.3 %collective-permute-start.25 = (bf16[32,128,128]{2,1,0:T(8,128)(2,1)S(1)}, bf16[32,128,128]{2,1,0:T(8,128)(2,1)S(1)}, u32[]{:S(2)}, u32[]{:S(2)}) collective-permute-start(bf16[32,128,128]{2,1,0:T(8,128)(2,1)S(1)} %get-tuple-element.189.here), channel_id=1, source_target_pairs={{1,2},{2,1},{3,4},{4,3},{5,6},{6,5},{7,8},{8,7},{9,10},{10,9},{11,... | collective-permute-start | bytes 3145736 | tf_op jit(solution)/shard_map/ppermute | solution.py:533
  90.9 3.4 %copy-start = (bf16[32,8,128,128]{3,2,1,0:T(8,128)(2,1)S(1)}, bf16[32,8,128,128]{3,2,1,0:T(8,128)(2,1)}, u32[]{:S(2)}) copy-start(bf16[32,8,128,128]{3,2,1,0:T(8,128)(2,1)} %param.22) | copy-start | bytes 25165828
  113.9 3.3 %collective-permute-start.28 = (bf16[32,128,128]{2,1,0:T(8,128)(2,1)S(1)}, bf16[32,128,128]{2,1,0:T(8,128)(2,1)S(1)}, u32[]{:S(2)}, u32[]{:S(2)}) collective-permute-start(bf16[32,128,128]{2,1,0:T(8,128)(2,1)S(1)} %late.1.here), channel_id=1, source_target_pairs={{0,1},{1,0},{2,3},{3,2},{4,5},{5,4},{6,7},{7,6},{8,9},{9,8},{10,11... | collective-permute-start | bytes 3145736 | tf_op jit(solution)/shard_map/ppermute | solution.py:532
  114.0 20.3 %collective-permute-start.27 = (bf16[32,128,128]{2,1,0:T(8,128)(2,1)S(1)}, bf16[32,128,128]{2,1,0:T(8,128)(2,1)S(1)}, u32[]{:S(2)}, u32[]{:S(2)}) collective-permute-start(bf16[32,128,128]{2,1,0:T(8,128)(2,1)S(1)} %late.1.here), channel_id=1, source_target_pairs={{1,2},{2,1},{3,4},{4,3},{5,6},{6,5},{7,8},{8,7},{9,10},{10,9},{11,... | collective-permute-start | bytes 3145736 | tf_op jit(solution)/shard_map/ppermute | solution.py:533

commit v4 on v3

--- a/solution.py
+++ b/solution.py
@@ -375,10 +375,11 @@
     )(table, *operands, left, inverse, integ, start)
 
 
+CHUNKS = 8
 UNIT = 4
 
 
-def couple(listed, inter, tables, total, amps, ahead, behind):
+def couple(listed, inter, tables, total, amps, ahead, behind, arrived=None):
     count = total.shape[0] - 1
     width = total.shape[1]
     low = 0
@@ -406,14 +407,58 @@
         for k, pair, one, _, two, _ in codes(group):
             total[pair] += dot_nt(mixed[k], jnp.concatenate([inter[one], inter[two]], axis=1))
 
+    def ready(group, waited):
+        if arrived is None:
+            return waited
+        return arrived(listed[2 * (group + 1) * UNIT] // 65536, waited)
+
+    waited = ready(0, jnp.int32(0))
     first(0, ahead)
 
-    @pl.loop(0, (listed[0] + 2 * UNIT - 1) // (2 * UNIT))
-    def _(step):
-        first(2 * step + 1, behind)
-        second(2 * step, ahead)
-        first(2 * step + 2, ahead)
-        second(2 * step + 1, behind)
+    def step(k, waited):
+        waited = ready(2 * k + 2, waited)
+        first(2 * k + 1, behind)
+        second(2 * k, ahead)
+        first(2 * k + 2, ahead)
+        second(2 * k + 1, behind)
+        return waited
+
+    waited = lax.fori_loop(0, (listed[0] + 2 * UNIT - 1) // (2 * UNIT), step, waited)
+    if arrived is not None:
+        arrived(total.shape[0] - 1, waited)
+
+
+def opening_body(listed, inter_hbm, here, near_by, integ_hbm, inverse_hbm,
+                 out, inter, integ, inverse, total, amps, ahead, behind, sem, more):
+    count = integ.shape[0]
+    rows = inter.shape[0] // CHUNKS
+    pairs = count // CHUNKS
+
+    def piece(k):
+        span = pl.ds(k * rows, rows)
+        return pltpu.make_async_copy(inter_hbm.at[span], inter.at[span], sem.at[k])
+
+    for k in range(CHUNKS):
+        piece(k).start()
+    copies = (
+        pltpu.make_async_copy(integ_hbm, integ, more.at[0]),
+        pltpu.make_async_copy(inverse_hbm, inverse, more.at[1]),
+    )
+    for copy in copies:
+        copy.start()
+
+    def arrived(pair, waited):
+        need = jnp.maximum(waited, jnp.minimum(pair // pairs + 1, CHUNKS))
+        pl.loop(waited, need)(lambda k: piece(k).wait())
+        return need
+
+    couple(listed, inter, (here, near_by), total, amps, ahead, behind, arrived)
+    for copy in copies:
+        copy.wait()
+
+    @pl.loop(0, count)
+    def _(p):
+        out[p] = integ[p] + COUPLING * total[p]
 
 
 def early_body(listed, inter, here, near_by, integ, out, total, *scratch):
@@ -432,14 +477,19 @@
         out[p] = ((so_far[p] + COUPLING * total[p]) * inverse[p]).astype(out.dtype)
 
 
-def last_body(listed, inter, other, so_far, inverse, integ, out, energy, rows, total, *scratch):
+def last_body(listed, inter, other, so_far, inverse, integ, out, energy, rows, kept, sem, total, *scratch):
     couple(listed, inter, (other,), total, *scratch)
     width = total.shape[1]
-
-    @pl.loop(0, so_far.shape[0])
+    count = so_far.shape[0]
+
+    def result(p):
+        return pltpu.make_async_copy(kept.at[p], out.at[p], sem.at[p])
+
+    @pl.loop(0, count)
     def _(p):
         value = (so_far[p] + COUPLING * total[p]) * inverse[p]
-        out[p] = value
+        kept[p] = value
+        result(p).start()
         rows[pl.ds(p, 1), :] = jnp.sum(integ[p] * value, axis=0, keepdims=True)
 
     sums = lax.dot_general(
@@ -450,6 +500,7 @@
         preferred_element_type=jnp.float32,
     )
     energy[...] = sums[0:1, :] * (1.0 / (width * width))
+    pl.loop(0, count)(lambda p: result(p).wait())
 
 
 def coupling_scratch(count, width, tables):
@@ -459,6 +510,22 @@
         pltpu.VMEM((UNIT, width, 2 * width), jnp.bfloat16),
         pltpu.VMEM((UNIT, width, 2 * width), jnp.bfloat16),
     ]
+
+
+def opening_part(listed, inter, here, other, integ, inverse):
+    count, width, _ = integ.shape
+    return call(
+        opening_body,
+        tuple(jax.ShapeDtypeStruct(x.shape, x.dtype) for x in (integ, inter, integ, inverse)),
+        (VMEM,) * 4,
+        [SMEM, ANY, VMEM, VMEM, ANY, ANY],
+        coupling_scratch(count, width, 2)
+        + [pltpu.SemaphoreType.DMA((CHUNKS,)), pltpu.SemaphoreType.DMA((2,))],
+        flops=2 * inter.shape[0] * width**3,
+        moved=inter.size * 2,
+        limit=26,
+        name="opening",
+    )(listed, inter, here, other, integ, inverse)
 
 
 def early_part(listed, inter, here, other, integ):
@@ -499,9 +566,14 @@
             jax.ShapeDtypeStruct(so_far.shape, jnp.float32),
             jax.ShapeDtypeStruct((1, count), jnp.float32),
         ),
-        (VMEM, VMEM),
+        (ANY, VMEM),
         [SMEM, VMEM, VMEM, VMEM, VMEM, VMEM],
-        [pltpu.VMEM((count, width), jnp.float32)] + coupling_scratch(count, width, 1),
+        [
+            pltpu.VMEM((count, width), jnp.float32),
+            pltpu.VMEM((count, width, width), jnp.float32),
+            pltpu.SemaphoreType.DMA((count,)),
+        ]
+        + coupling_scratch(count, width, 1),
         flops=inter.shape[0] * width**3,
         moved=inter.size * 2,
         limit=24,
@@ -544,14 +616,16 @@
             packed = pack(table, maps, (slots // 2, slots - slots // 2), orbitals)
             got = [swap_across(x) for x in packed]
             left = left_part(table, blocks, maps)
+            half_one = serve(after(table, left), blocks, got[0], 0, count)
+            back_one = swap_across(half_one)
             integ, start, inverse, early, late = own_part(
-                table, sizes, shift, near_pairs, blocks, maps, energy, left, scale
+                after(table, half_one), sizes, shift, near_pairs, blocks, maps, energy, left, scale
             )
-            half_one = serve(after(table, early), blocks, got[0], 0, count)
-            back_one = swap_across(half_one)
+            half_two = serve(after(table, early), blocks, got[1], got[0].shape[0], count)
+            back_two = swap_across(half_two)
             integ, start = integrals_part(
                 functools.partial(beside_body, scale),
-                after(table, half_one),
+                after(table, half_two),
                 (blocks_beside, maps),
                 left,
                 inverse,
@@ -561,8 +635,6 @@
                 24,
                 "beside",
             )
-            half_two = serve(after(table, start), blocks, got[1], got[0].shape[0], count)
-            back_two = swap_across(half_two)
             integ, start = integrals_part(
                 functools.partial(across_body, scale, orbitals),
                 table,
@@ -593,7 +665,10 @@
     for iteration in range(ITERS):
         far = swap_across(amps)
         close = swap_beside(amps)
-        so_far = early_part(early, inter, amps, close, integ)
+        if iteration == 0:
+            so_far, inter, integ, inverse = opening_part(early, inter, amps, close, integ, inverse)
+        else:
+            so_far = early_part(early, inter, amps, close, integ)
         if iteration < ITERS - 1:
             amps = late_part(late, inter, far, so_far, inverse)
         else:

time: 143 us -> 137 us (0.958)
  the two profiles are of different devices: /device:TPU:6 before, /device:TPU:4 now
where the time goes in v4:
time: 137 us; the launch traced here: 134 us
  Pallas kernels  74.3 us (54%)
  waiting for transfers between devices  27.4 us (20%)
  starting transfers between devices  25.4 us (19%)
  local copies, waits for them, and re-layouts  4.87 us (4%)
  between operations  1.55 us (1%)
    ppermute x6, waiting for transfers between devices, shards(): swap_across = lambda x: lax.ppermute(x, 'pairs', across_perm)  27.1 us
    ppermute x6, starting transfers between devices, shards(): swap_across = lambda x: lax.ppermute(x, 'pairs', across_perm)  25.1 us
    pallas_call x1, Pallas kernels, own_part(): call(functools.partial(own_body, scale, orbitals), (jax.ShapeDtypeStruct(...  15 us
    pallas_call x1, Pallas kernels, left_part(): call(left_body, jax.ShapeDtypeStruct((count, width, depth), jnp.bfloat16)...  11.1 us
    pallas_call x2, Pallas kernels, integrals_part(): call(body, (jax.ShapeDtypeStruct(integ.shape, integ.dtype), jax.ShapeDtyp...  10 us
    pallas_call x1, Pallas kernels, opening_part(): call(opening_body, tuple((jax.ShapeDtypeStruct(x.shape, x.dtype) for x in...  9.47 us
    pallas_call x1, Pallas kernels, early_part(): call(early_body, jax.ShapeDtypeStruct(integ.shape, jnp.float32), VMEM, [S...  8.33 us
    pallas_call x1, Pallas kernels, last_part(): call(last_body, (jax.ShapeDtypeStruct(so_far.shape, jnp.float32), jax.Sha...  6.75 us
  transfers between devices with their start and end apart: 9, of which 5 were waited for; matrix products, arithmetic and copies ran while one was open for 0% of the time, Pallas kernels for 43%

profile of v4, /device:TPU:4, one launch (start us, length us, event | category | flops | bytes accessed | tf_op | source)
XLA Modules:
  0.0 133.9 jit_solution(11940125092507357049)
XLA Ops:
  0.6 0.0 copy-start.1
  0.6 0.7 copy-done.1
  1.4 0.0 copy-start.2
  1.4 0.7 copy-done.2
  2.1 2.3 %plan.1 = (s32[128]{0:T(128)S(1)}, s32[1]{0:T(128)}) custom-call(s32[2,4096]{1,0:T(2,128)S(1)} %bitcast.6, s32[2,4096]{1,0:T(2,128)S(1)} %bitcast.7, s32[2048]{0:T(1024)S(1)} %copy-done.2), custom_call_target="tpu_custom_call" | custom-call | bytes 65536 | tf_op jit(solution)/shard_map/plan/pallas_call | solution.py:119
  5.1 76.1 %conditional.1 = (f32[32,128,128]{2,1,0:T(8,128)S(1)}, bf16[32,128,128]{2,1,0:T(8,128)(2,1)S(1)}, f32[32,128,128]{2,1,0:T(8,128)}, s32[288]{0:T(512)S(1)}, s32[288]{0:T(512)S(1)}) conditional(s32[]{:T(128)} %bitcast.1, (s32[128]{0:T(128)S(1)}, bf16[16,512,512]{2,1,0:T(8,128)(2,1)}, bf16[32,512,128]{2,1,0:T(8,128)(2,1)}, ...), branch_computations={%region_0.0_spmd, %region_1.0_spmd, %region_2.0_spmd, %region_3.0_... | conditional | flops 7516192768 | bytes 167843264 | solution.py:654
  5.1 0.1 collective-permute-start.9
  5.2 0.0 copy-start.4
  5.2 0.0 slice-start.2
  5.2 2.5 %pack.6 = (bf16[9,512,128]{2,1,0:T(8,128)(2,1)S(1)}, bf16[9,512,128]{2,1,0:T(8,128)(2,1)S(1)}) custom-call(s32[128]{0:T(128)S(1)} %get-tuple-element.106.table, bf16[32,512,128]{2,1,0:T(8,128)(2,1)} %get-tuple-element.94.maps), custom_call_target="tpu_custom_call" | custom-call | bytes 4718592 | tf_op jit(solution)/shard_map/cond/branch_1_fun/pack/pallas_call | solution.py:155
  7.8 8.8 %collective-permute-start.5 = (bf16[9,512,128]{2,1,0:T(8,128)(2,1)S(1)}, bf16[9,512,128]{2,1,0:T(8,128)(2,1)S(1)}, u32[]{:S(2)}, u32[]{:S(2)}) collective-permute-start(bf16[9,512,128]{2,1,0:T(8,128)(2,1)S(1)} %get-tuple-element.96), channel_id=1, source_target_pairs={{1,2},{2,1},{3,4},{4,3},{5,6},{6,5},{7,8},{8,7},{9,10},{10,9},{11,... | collective-permute-start | bytes 3538952 | tf_op jit(solution)/shard_map/cond/branch_1_fun/ppermute | solution.py:605
  16.5 0.0 slice-start.3
  16.5 2.2 %collective-permute-start.7 = (bf16[9,512,128]{2,1,0:T(8,128)(2,1)S(1)}, bf16[9,512,128]{2,1,0:T(8,128)(2,1)S(1)}, u32[]{:S(2)}, u32[]{:S(2)}) collective-permute-start(bf16[9,512,128]{2,1,0:T(8,128)(2,1)S(1)} %get-tuple-element.104), channel_id=1, source_target_pairs={{1,2},{2,1},{3,4},{4,3},{5,6},{6,5},{7,8},{8,7},{9,10},{10,9},{11,... | collective-permute-start | bytes 3538952 | tf_op jit(solution)/shard_map/cond/branch_1_fun/ppermute | solution.py:605
  18.7 0.0 copy-done.4
  18.7 11.1 %left.6.refs_2_ = bf16[32,128,512]{2,1,0:T(8,128)(2,1)S(1)} custom-call(s32[128]{0:T(128)S(1)} %get-tuple-element.106.table, bf16[16,512,512]{2,1,0:T(8,128)(2,1)} %get-tuple-element.93.blocks, bf16[32,512,128]{2,1,0:T(8,128)(2,1)S(1)} %copy-done.4), custom_call_target="tpu_custom_call" | custom-call | flops 2147483648 | bytes 8388608 | tf_op jit(solution)/shard_map/cond/branch_1_fun/left/pallas_call | solution.py:184
  29.8 0.0 copy-start.9
  29.8 0.0 copy-start.14
  29.8 0.0 copy-start.19
  29.9 0.0 copy-start.24
  29.9 0.5 collective-permute-done.5.maps
  30.4 0.0 slice-done.2
  30.4 0.0 slice-done.3
  30.4 3.0 %serve.12 = bf16[9,512,128]{2,1,0:T(8,128)(2,1)S(1)} custom-call(s32[128]{0:T(128)S(1)} %get-tuple-element.106.table, bf16[16,512,512]{2,1,0:T(8,128)(2,1)S(1)} %bitcast.11, bf16[9,512,128]{2,1,0:T(8,128)(2,1)S(1)} %collective-permute-done.5.maps), custom_call_target="tpu_custom_call" | custom-call | flops 603979776 | bytes 7077888 | tf_op jit(solution)/shard_map/cond/branch_1_fun/serve/pallas_call | solution.py:295
  33.4 7.0 %collective-permute-start.6 = (bf16[9,512,128]{2,1,0:T(8,128)(2,1)S(1)}, bf16[9,512,128]{2,1,0:T(8,128)(2,1)S(1)}, u32[]{:S(2)}, u32[]{:S(2)}) collective-permute-start(bf16[9,512,128]{2,1,0:T(8,128)(2,1)S(1)} %serve.12), channel_id=1, source_target_pairs={{1,2},{2,1},{3,4},{4,3},{5,6},{6,5},{7,8},{8,7},{9,10},{10,9},{11,... | collective-permute-start | bytes 3538952 | tf_op jit(solution)/shard_map/cond/branch_1_fun/ppermute | solution.py:605
  40.4 0.0 copy-done.9
  40.4 0.0 copy-done.14
  40.4 0.0 copy-done.19
  40.4 0.0 copy-done.24
  40.4 15.0 %own.6 = (f32[32,128,128]{2,1,0:T(8,128)S(1)}, bf16[32,128,128]{2,1,0:T(8,128)(2,1)S(1)}, f32[32,128,128]{2,1,0:T(8,128)}, s32[288]{0:T(512)S(1)}, s32[288]{0:T(512)S(1)}) custom-call(s32[128]{0:T(128)S(1)} %get-tuple-element.106.table, s32[32]{0:T(128)S(1)} %copy-done.19, f32[32]{0:T(128)S(1)} %copy-done.24, s32[8,32]{1,0:T(8,128)S(1)} %copy-done.14, ...), custom_call_target="tpu_custom_call" | custom-call | flops 1073741824 | bytes 8388608 | tf_op jit(solution)/shard_map/cond/branch_1_fun/own/pallas_call | solution.py:255
  55.5 0.0 collective-permute-done.7.maps
  55.5 0.8 serve.13
  56.3 1.9 %collective-permute-start.8 = (bf16[9,512,128]{2,1,0:T(8,128)(2,1)S(1)}, bf16[9,512,128]{2,1,0:T(8,128)(2,1)S(1)}, u32[]{:S(2)}, u32[]{:S(2)}) collective-permute-start(bf16[9,512,128]{2,1,0:T(8,128)(2,1)S(1)} %serve.13), channel_id=1, source_target_pairs={{1,2},{2,1},{3,4},{4,3},{5,6},{6,5},{7,8},{8,7},{9,10},{10,9},{11,... | collective-permute-start | bytes 3538952 | tf_op jit(solution)/shard_map/cond/branch_1_fun/ppermute | solution.py:605
  58.2 0.0 collective-permute-done.9.blocks
  58.2 7.1 %beside.6 = (f32[32,128,128]{2,1,0:T(8,128)S(1)}, bf16[32,128,128]{2,1,0:T(8,128)(2,1)S(1)}) custom-call(s32[128]{0:T(128)S(1)} %get-tuple-element.106.table, bf16[16,512,512]{2,1,0:T(8,128)(2,1)S(1)} %collective-permute-done.9.blocks, bf16[32,512,128]{2,1,0:T(8,128)(2,1)S(1)} %copy-done.4, bf16[32,128,512]{2,1,0:T(8,128)(2,1)S(1)} %left.6.refs_2_, ...), custom_call_target="tpu_custom_call" | custom-call | flops 1073741824 | bytes 4194304 | tf_op jit(solution)/shard_map/cond/branch_1_fun/beside/pallas_call | solution.py:362
  65.3 0.0 collective-permute-done.6.refs_0_
  65.4 12.7 %collective-permute-done.8.refs_1_ = bf16[9,512,128]{2,1,0:T(8,128)(2,1)S(1)} collective-permute-done((bf16[9,512,128]{2,1,0:T(8,128)(2,1)S(1)}, bf16[9,512,128]{2,1,0:T(8,128)(2,1)S(1)}, u32[]{:S(2)}, u32[]{:S(2)}) %collective-permute-start.8) | collective-permute-done | bytes 1179680 | tf_op jit(solution)/shard_map/cond/branch_1_fun/ppermute | solution.py:605
  78.0 2.9 %across.6 = (f32[32,128,128]{2,1,0:T(8,128)S(1)}, bf16[32,128,128]{2,1,0:T(8,128)(2,1)S(1)}) custom-call(s32[128]{0:T(128)S(1)} %get-tuple-element.106.table, bf16[9,512,128]{2,1,0:T(8,128)(2,1)S(1)} %collective-permute-done.6.refs_0_, bf16[9,512,128]{2,1,0:T(8,128)(2,1)S(1)} %collective-permute-done.8.refs_1_, bf16[32,128,512]{2,1,0:T(8,128)(2,1)S(1)} %left.6.refs_2_, ...), custom_call_target="tpu_custom_call" | custom-call | flops 1073741824 | bytes 4194304 | tf_op jit(solution)/shard_map/cond/branch_1_fun/across/pallas_call | solution.py:362
  81.2 0.1 collective-permute-start.25
  81.3 2.4 %collective-permute-start.26 = (bf16[32,128,128]{2,1,0:T(8,128)(2,1)S(1)}, bf16[32,128,128]{2,1,0:T(8,128)(2,1)S(1)}, u32[]{:S(2)}, u32[]{:S(2)}) collective-permute-start(bf16[32,128,128]{2,1,0:T(8,128)(2,1)S(1)} %get-tuple-element.199.here), channel_id=1, source_target_pairs={{1,2},{2,1},{3,4},{4,3},{5,6},{6,5},{7,8},{8,7},{9,10},{10,9},{11,... | collective-permute-start | bytes 3145736 | tf_op jit(solution)/shard_map/ppermute | solution.py:605
  83.7 0.3 collective-permute-done.25.near_by
  83.9 0.0 copy-start
  83.9 3.4 %copy-done = bf16[32,8,128,128]{3,2,1,0:T(8,128)(2,1)S(1)} copy-done((bf16[32,8,128,128]{3,2,1,0:T(8,128)(2,1)S(1)}, bf16[32,8,128,128]{3,2,1,0:T(8,128)(2,1)}, u32[]{:S(2)}) %copy-start) | copy-done | bytes 8388632
  87.3 9.5 %opening.1 = (f32[32,128,128]{2,1,0:T(8,128)S(1)}, bf16[256,128,128]{2,1,0:T(8,128)(2,1)S(1)}, f32[32,128,128]{2,1,0:T(8,128)S(1)}, f32[32,128,128]{2,1,0:T(8,128)S(1)}) custom-call(s32[288]{0:T(512)S(1)} %get-tuple-element.198.listed, bf16[256,128,128]{2,1,0:T(8,128)(2,1)S(1)} %bitcast.5, bf16[32,128,128]{2,1,0:T(8,128)(2,1)S(1)} %get-tuple-element.199.here, ...), custom_call_target="tpu_custom_call" | custom-call | flops 1073741824 | bytes 8388608 | tf_op jit(solution)/shard_map/opening/pallas_call | solution.py:517
  96.8 4.8 %collective-permute-done.26.other = bf16[32,128,128]{2,1,0:T(8,128)(2,1)S(1)} collective-permute-done((bf16[32,128,128]{2,1,0:T(8,128)(2,1)S(1)}, bf16[32,128,128]{2,1,0:T(8,128)(2,1)S(1)}, u32[]{:S(2)}, u32[]{:S(2)}) %collective-permute-start.26) | collective-permute-done | bytes 1048608 | tf_op jit(solution)/shard_map/ppermute | solution.py:605
  101.6 5.0 %late.1.here = bf16[32,128,128]{2,1,0:T(8,128)(2,1)S(1)} custom-call(s32[288]{0:T(512)S(1)} %get-tuple-element.197.listed, bf16[256,128,128]{2,1,0:T(8,128)(2,1)S(1)} %get-tuple-element.202.inter, bf16[32,128,128]{2,1,0:T(8,128)(2,1)S(1)} %collective-permute-done.26.other, f32[32,128,128]{2,1,0:T(8,128)S(1)} %get-tuple-element.203.so_far, ...), custom_call_target="tpu_custom_call" | custom-call | flops 536870912 | bytes 8388608 | tf_op jit(solution)/shard_map/late/pallas_call | solution.py:548
  106.6 0.1 collective-permute-start.28
  106.7 2.9 %collective-permute-start.27 = (bf16[32,128,128]{2,1,0:T(8,128)(2,1)S(1)}, bf16[32,128,128]{2,1,0:T(8,128)(2,1)S(1)}, u32[]{:S(2)}, u32[]{:S(2)}) collective-permute-start(bf16[32,128,128]{2,1,0:T(8,128)(2,1)S(1)} %late.1.here), channel_id=1, source_target_pairs={{1,2},{2,1},{3,4},{4,3},{5,6},{6,5},{7,8},{8,7},{9,10},{10,9},{11,... | collective-permute-start | bytes 3145736 | tf_op jit(solution)/shard_map/ppermute | solution.py:605
  109.6 0.0 collective-permute-done.28.near_by
  109.6 8.3 %early.1.so_far = f32[32,128,128]{2,1,0:T(8,128)S(1)} custom-call(s32[288]{0:T(512)S(1)} %get-tuple-element.198.listed, bf16[256,128,128]{2,1,0:T(8,128)(2,1)S(1)} %get-tuple-element.202.inter, bf16[32,128,128]{2,1,0:T(8,128)(2,1)S(1)} %late.1.here, bf16[32,128,128]{2,1,0:T(8,128)(2,1)S(1)} %collective-permute-done.28.near_by, ...), custom_call_target="tpu_custom_call" | custom-call | flops 1073741824 | bytes 8388608 | tf_op jit(solution)/shard_map/early/pallas_call | solution.py:533
  118.0 9.0 %collective-permute-done.27.other = bf16[32,128,128]{2,1,0:T(8,128)(2,1)S(1)} collective-permute-done((bf16[32,128,128]{2,1,0:T(8,128)(2,1)S(1)}, bf16[32,128,128]{2,1,0:T(8,128)(2,1)S(1)}, u32[]{:S(2)}, u32[]{:S(2)}) %collective-permute-start.27) | collective-permute-done | bytes 1048608 | tf_op jit(solution)/shard_map/ppermute | solution.py:605
  127.0 6.7 %last.1 = (f32[32,128,128]{2,1,0:T(8,128)}, f32[1,32]{1,0:T(1,128)}) custom-call(s32[288]{0:T(512)S(1)} %get-tuple-element.197.listed, bf16[256,128,128]{2,1,0:T(8,128)(2,1)S(1)} %get-tuple-element.202.inter, bf16[32,128,128]{2,1,0:T(8,128)(2,1)S(1)} %collective-permute-done.27.other, f32[32,128,128]{2,1,0:T(8,128)S(1)} %early.1.so_far, ...), custom_call_target="tpu_custom_call" | custom-call | flops 536870912 | bytes 8388608 | tf_op jit(solution)/shard_map/last/pallas_call | solution.py:563
  (1 shorter events, 0.0 us)
Async XLA Ops:
  0.6 0.8 copy-start.1
  1.4 0.7 copy-start.2
  5.1 53.1 %collective-permute-start.9 = (bf16[16,512,512]{2,1,0:T(8,128)(2,1)}, bf16[16,512,512]{2,1,0:T(8,128)(2,1)S(1)}, u32[]{:S(2)}, u32[]{:S(2)}) collective-permute-start(bf16[16,512,512]{2,1,0:T(8,128)(2,1)} %get-tuple-element.93.blocks), channel_id=1, source_target_pairs={{0,1},{1,0},{2,3},{3,2},{4,5},{5,4},{6,7},{7,6},{8,9},{9,8},{10,11... | collective-permute-start | bytes 25165832 | tf_op jit(solution)/shard_map/cond/branch_1_fun/ppermute | solution.py:604
  5.2 13.5 %copy-start.4 = (bf16[32,512,128]{2,1,0:T(8,128)(2,1)S(1)}, bf16[32,512,128]{2,1,0:T(8,128)(2,1)}, u32[]{:S(2)}) copy-start(bf16[32,512,128]{2,1,0:T(8,128)(2,1)} %get-tuple-element.94.maps) | copy-start | bytes 12582916 | tf_op jit(solution)/shard_map/cond
  5.2 25.2 %slice-start.2 = ((s8[8388608]{0:T(1024)(128)(4,1)}), s8[4194304]{0:T(1024)(128)(4,1)S(1)}, s32[]{:S(2)}) async-start(s8[8388608]{0:T(1024)(128)(4,1)} %bitcast.10), calls=%async_computation.2 | async-start | bytes 8388608 | tf_op jit(solution)/shard_map/cond
  7.8 22.6 %collective-permute-start.5 = (bf16[9,512,128]{2,1,0:T(8,128)(2,1)S(1)}, bf16[9,512,128]{2,1,0:T(8,128)(2,1)S(1)}, u32[]{:S(2)}, u32[]{:S(2)}) collective-permute-start(bf16[9,512,128]{2,1,0:T(8,128)(2,1)S(1)} %get-tuple-element.96), channel_id=1, source_target_pairs={{1,2},{2,1},{3,4},{4,3},{5,6},{6,5},{7,8},{8,7},{9,10},{10,9},{11,... | collective-permute-start | bytes 3538952 | tf_op jit(solution)/shard_map/cond/branch_1_fun/ppermute | solution.py:605
  16.5 13.9 %slice-start.3 = ((s8[8388608]{0:T(1024)(128)(4,1)}), s8[4194304]{0:T(1024)(128)(4,1)S(1)}, s32[]{:S(2)}) async-start(s8[8388608]{0:T(1024)(128)(4,1)} %bitcast.10), calls=%async_computation.3 | async-start | bytes 8388608 | tf_op jit(solution)/shard_map/cond
  16.5 38.9 %collective-permute-start.7 = (bf16[9,512,128]{2,1,0:T(8,128)(2,1)S(1)}, bf16[9,512,128]{2,1,0:T(8,128)(2,1)S(1)}, u32[]{:S(2)}, u32[]{:S(2)}) collective-permute-start(bf16[9,512,128]{2,1,0:T(8,128)(2,1)S(1)} %get-tuple-element.104), channel_id=1, source_target_pairs={{1,2},{2,1},{3,4},{4,3},{5,6},{6,5},{7,8},{8,7},{9,10},{10,9},{11,... | collective-permute-start | bytes 3538952 | tf_op jit(solution)/shard_map/cond/branch_1_fun/ppermute | solution.py:605
  29.8 10.6 %copy-start.9 = (f32[32,128]{1,0:T(8,128)S(1)}, f32[32,128]{1,0:T(8,128)}, u32[]{:S(2)}) copy-start(f32[32,128]{1,0:T(8,128)} %get-tuple-element.101.energy) | copy-start | bytes 49156 | tf_op jit(solution)/shard_map/cond
  29.8 10.6 %copy-start.14 = (s32[8,32]{1,0:T(8,128)S(1)}, s32[8,32]{1,0:T(8,128)}, u32[]{:S(2)}) copy-start(s32[8,32]{1,0:T(8,128)} %get-tuple-element.100.near_pairs) | copy-start | bytes 3076 | tf_op jit(solution)/shard_map/cond
  29.8 10.6 %copy-start.19 = (s32[32]{0:T(128)S(1)}, s32[32]{0:T(128)}, u32[]{:S(2)}) copy-start(s32[32]{0:T(128)} %get-tuple-element.98.sizes) | copy-start | bytes 388 | tf_op jit(solution)/shard_map/cond
  29.9 10.6 %copy-start.24 = (f32[32]{0:T(128)S(1)}, f32[32]{0:T(128)}, u32[]{:S(2)}) copy-start(f32[32]{0:T(128)} %get-tuple-element.99.shift) | copy-start | bytes 388 | tf_op jit(solution)/shard_map/cond
  33.4 31.9 %collective-permute-start.6 = (bf16[9,512,128]{2,1,0:T(8,128)(2,1)S(1)}, bf16[9,512,128]{2,1,0:T(8,128)(2,1)S(1)}, u32[]{:S(2)}, u32[]{:S(2)}) collective-permute-start(bf16[9,512,128]{2,1,0:T(8,128)(2,1)S(1)} %serve.12), channel_id=1, source_target_pairs={{1,2},{2,1},{3,4},{4,3},{5,6},{6,5},{7,8},{8,7},{9,10},{10,9},{11,... | collective-permute-start | bytes 3538952 | tf_op jit(solution)/shard_map/cond/branch_1_fun/ppermute | solution.py:605
  56.3 21.7 %collective-permute-start.8 = (bf16[9,512,128]{2,1,0:T(8,128)(2,1)S(1)}, bf16[9,512,128]{2,1,0:T(8,128)(2,1)S(1)}, u32[]{:S(2)}, u32[]{:S(2)}) collective-permute-start(bf16[9,512,128]{2,1,0:T(8,128)(2,1)S(1)} %serve.13), channel_id=1, source_target_pairs={{1,2},{2,1},{3,4},{4,3},{5,6},{6,5},{7,8},{8,7},{9,10},{10,9},{11,... | collective-permute-start | bytes 3538952 | tf_op jit(solution)/shard_map/cond/branch_1_fun/ppermute | solution.py:605
  81.2 2.7 %collective-permute-start.25 = (bf16[32,128,128]{2,1,0:T(8,128)(2,1)S(1)}, bf16[32,128,128]{2,1,0:T(8,128)(2,1)S(1)}, u32[]{:S(2)}, u32[]{:S(2)}) collective-permute-start(bf16[32,128,128]{2,1,0:T(8,128)(2,1)S(1)} %get-tuple-element.199.here), channel_id=1, source_target_pairs={{0,1},{1,0},{2,3},{3,2},{4,5},{5,4},{6,7},{7,6},{8,9},{9,8},{10,11... | collective-permute-start | bytes 3145736 | tf_op jit(solution)/shard_map/ppermute | solution.py:604
  81.3 20.3 %collective-permute-start.26 = (bf16[32,128,128]{2,1,0:T(8,128)(2,1)S(1)}, bf16[32,128,128]{2,1,0:T(8,128)(2,1)S(1)}, u32[]{:S(2)}, u32[]{:S(2)}) collective-permute-start(bf16[32,128,128]{2,1,0:T(8,128)(2,1)S(1)} %get-tuple-element.199.here), channel_id=1, source_target_pairs={{1,2},{2,1},{3,4},{4,3},{5,6},{6,5},{7,8},{8,7},{9,10},{10,9},{11,... | collective-permute-start | bytes 3145736 | tf_op jit(solution)/shard_map/ppermute | solution.py:605
  83.9 3.4 %copy-start = (bf16[32,8,128,128]{3,2,1,0:T(8,128)(2,1)S(1)}, bf16[32,8,128,128]{3,2,1,0:T(8,128)(2,1)}, u32[]{:S(2)}) copy-start(bf16[32,8,128,128]{3,2,1,0:T(8,128)(2,1)} %param.22) | copy-start | bytes 25165828
  106.6 3.0 %collective-permute-start.28 = (bf16[32,128,128]{2,1,0:T(8,128)(2,1)S(1)}, bf16[32,128,128]{2,1,0:T(8,128)(2,1)S(1)}, u32[]{:S(2)}, u32[]{:S(2)}) collective-permute-start(bf16[32,128,128]{2,1,0:T(8,128)(2,1)S(1)} %late.1.here), channel_id=1, source_target_pairs={{0,1},{1,0},{2,3},{3,2},{4,5},{5,4},{6,7},{7,6},{8,9},{9,8},{10,11... | collective-permute-start | bytes 3145736 | tf_op jit(solution)/shard_map/ppermute | solution.py:604
  106.7 20.3 %collective-permute-start.27 = (bf16[32,128,128]{2,1,0:T(8,128)(2,1)S(1)}, bf16[32,128,128]{2,1,0:T(8,128)(2,1)S(1)}, u32[]{:S(2)}, u32[]{:S(2)}) collective-permute-start(bf16[32,128,128]{2,1,0:T(8,128)(2,1)S(1)} %late.1.here), channel_id=1, source_target_pairs={{1,2},{2,1},{3,4},{4,3},{5,6},{6,5},{7,8},{8,7},{9,10},{10,9},{11,... | collective-permute-start | bytes 3145736 | tf_op jit(solution)/shard_map/ppermute | solution.py:605

commit v5 on v4

--- a/solution.py
+++ b/solution.py
@@ -10,9 +10,10 @@
 
 ITERS = 2
 COUPLING = 0.35
-SLOTS = (16, 18, 20, 24, 32)
+SLOTS = (17, 18, 19, 20, 24, 32)
 
 ANY = pl.BlockSpec(memory_space=pl.ANY)
+HBM = pl.BlockSpec(memory_space=pltpu.HBM)
 VMEM = pl.BlockSpec(memory_space=pltpu.VMEM)
 SMEM = pl.BlockSpec(memory_space=pltpu.SMEM)
 
@@ -65,7 +66,7 @@
             store(k, values)
 
 
-def plan_body(orbitals, everyone, pairs_hbm, sizes, table, branch, mine, theirs, sem):
+def plan_body(orbitals, pairs_hbm, sizes_hbm, table, branch, everyone, sizes, mine, theirs, sem):
     count = mine.shape[1] // 4
     lanes = mine.shape[1]
     devices = everyone.shape[1] // count
@@ -79,9 +80,16 @@
         start = pl.multiple_of(who // 4 * lanes, lanes)
         return pltpu.make_async_copy(pairs_hbm.at[:, pl.ds(start, lanes)], place, sem.at[k])
 
-    copies = (fetch(device, mine, 0), fetch(near_by, theirs, 1))
+    copies = (
+        fetch(device, mine, 0),
+        fetch(near_by, theirs, 1),
+        pltpu.make_async_copy(sizes_hbm, sizes, sem.at[3]),
+    )
+    whole = pltpu.make_async_copy(pairs_hbm, everyone, sem.at[2])
+    whole.start()
     for copy in copies:
         copy.start()
+    whole.wait()
 
     groups = devices * count // lanes
     second = jnp.concatenate([everyone[1:2, g * lanes : (g + 1) * lanes] for g in range(groups)], axis=0)
@@ -120,12 +128,21 @@
         functools.partial(plan_body, orbitals),
         (jax.ShapeDtypeStruct((128,), jnp.int32), jax.ShapeDtypeStruct((1,), jnp.int32)),
         (SMEM, SMEM),
-        [VMEM, ANY, SMEM],
-        [pltpu.SMEM((2, 128), jnp.int32), pltpu.SMEM((2, 128), jnp.int32), pltpu.SemaphoreType.DMA((2,))],
+        [HBM, HBM],
+        [
+            pltpu.VMEM(turned.shape, jnp.int32),
+            pltpu.SMEM(block_sizes.shape, jnp.int32),
+            pltpu.SMEM((2, 128), jnp.int32),
+            pltpu.SMEM((2, 128), jnp.int32),
+            pltpu.SemaphoreType.DMA((4,)),
+        ],
         moved=turned.size * 8,
         limit=4,
         name="plan",
-    )(turned, turned, block_sizes)
+    )(
+        pltpu.with_memory_space_constraint(turned, pltpu.HBM),
+        pltpu.with_memory_space_constraint(block_sizes, pltpu.HBM),
+    )
 
 
 def pack_body(orbitals, table, maps, *refs):
@@ -195,8 +212,9 @@
 
 
 def own_body(scale, orbitals, table, sizes, shift, near_pairs, blocks, maps, energy, left,
-             integ, start, inverse, early, late, slots):
+             integ, start, inverse, early, late, later, slots):
     count, width, _ = left.shape
+    part = count // 2
     near = near_pairs.shape[0]
     device = lax.axis_index("pairs")
     side = 2 * (device % 2) - 1
@@ -204,34 +222,40 @@
     across_ids = lax.broadcasted_iota(jnp.int32, (width, width), 1)
 
     def pair_step(pair, counts):
-        soon, after = counts
+        soon, after, last = counts
         for k in range(near):
             entry = pair * near + k
             local = near_pairs[k, pair] - device * count
             offset = (local >= count).astype(jnp.int32) - (local < 0).astype(jnp.int32)
             is_late = (offset == side).astype(jnp.int32)
             code = pair * 65536 + entry * 256 + local - offset * count
+            is_last = ((local - offset * count) // part) * is_late
             early[1 + soon] = code + jnp.where(offset == 0, 0, count)
             late[1 + after] = code
+            later[1 + last] = code - part
             soon = soon + 1 - is_late
-            after = after + is_late
+            after = after + is_late - is_last
+            last = last + is_last
         spare = pair * 65536 + pair * near * 256
         early[1 + soon] = spare + 2 * count
-        late[1 + after] = spare + count
+        late[1 + after] = spare + part
+        later[1 + last] = spare + part
         row = jnp.broadcast_to(energy[pl.ds(pair, 1), :], (width, width))
         bottom = row + row.T + shift[pair]
         size = sizes[pair]
         inverse[pair] = jnp.where((ids < size) & (across_ids < size), -1.0 / bottom, 0.0)
-        return soon + soon % 2, after + after % 2
-
-    soon, after = lax.fori_loop(0, count, pair_step, (jnp.int32(0), jnp.int32(0)))
+        return soon + soon % 2, after + after % 2, last + last % 2
+
+    soon, after, last = lax.fori_loop(0, count, pair_step, (jnp.int32(0),) * 3)
     early[0] = soon // 2
     late[0] = after // 2
+    later[0] = last // 2
 
     @pl.loop(0, 6 * UNIT)
     def _(k):
         early[1 + soon + k] = count * 65536 + 2 * count
-        late[1 + after + k] = count * 65536 + count
+        late[1 + after + k] = count * 65536 + part
+        later[1 + last + k] = count * 65536 + part
 
     found = collect(count, lambda p: table[SRC + p] < orbitals, slots)
 
@@ -258,10 +282,9 @@
             jax.ShapeDtypeStruct((count, width, width), jnp.float32),
             jax.ShapeDtypeStruct((count, width, width), jnp.bfloat16),
             jax.ShapeDtypeStruct((count, width, width), jnp.float32),
-            jax.ShapeDtypeStruct((entries,), jnp.int32),
-            jax.ShapeDtypeStruct((entries,), jnp.int32),
-        ),
-        (VMEM, VMEM, VMEM, SMEM, SMEM),
+        )
+        + (jax.ShapeDtypeStruct((entries,), jnp.int32),) * 3,
+        (VMEM, VMEM, VMEM, SMEM, SMEM, SMEM),
         [SMEM, SMEM, SMEM, SMEM, VMEM, VMEM, VMEM, VMEM],
         [pltpu.SMEM((count + 1,), jnp.int32)],
         flops=count * depth * depth * width,
@@ -335,9 +358,9 @@
 
 
 def across_body(scale, orbitals, table, *refs):
-    n = len(refs) - 8
+    n = len(refs) - 10
     halves = refs[:n]
-    left, inverse, integ_in, start_in, integ, start, joined, slots = refs[n:]
+    left, inverse, integ_in, start_in, integ, start, one, two, joined, slots = refs[n:]
     carry_over(integ_in, start_in, integ, start)
     low = 0
     for half in halves:
@@ -354,18 +377,32 @@
         start[pair] = (value * inverse[pair]).astype(jnp.bfloat16)
 
     by_twos(found, work, store)
+    split(start, one, two)
+
+
+def split(amps, one, two):
+    part = one.shape[0]
+
+    @pl.loop(0, part)
+    def _(p):
+        one[p] = amps[p]
+        two[p] = amps[part + p]
+
+
+def amps_shapes(start, halved=True):
+    parts = (start.shape[0] // 2,) + start.shape[1:]
+    shapes = (start.shape,) + ((parts, parts) if halved else ())
+    return tuple(jax.ShapeDtypeStruct(shape, jnp.bfloat16) for shape in shapes)
 
 
 def integrals_part(body, table, operands, left, inverse, integ, start, scratch, limit, name):
     count, width, depth = left.shape
     n = len(operands)
+    outs = (jax.ShapeDtypeStruct(integ.shape, integ.dtype),) + amps_shapes(start, name == "across")
     return call(
         body,
-        (
-            jax.ShapeDtypeStruct(integ.shape, integ.dtype),
-            jax.ShapeDtypeStruct(start.shape, start.dtype),
-        ),
-        (VMEM, VMEM),
+        outs,
+        (VMEM,) * len(outs),
         [SMEM] + [VMEM] * (n + 4),
         scratch + [pltpu.SMEM((count + 1,), jnp.int32)],
         flops=count * depth * depth * width,
@@ -461,20 +498,23 @@
         out[p] = integ[p] + COUPLING * total[p]
 
 
-def early_body(listed, inter, here, near_by, integ, out, total, *scratch):
-    couple(listed, inter, (here, near_by), total, *scratch)
+def early_body(tables, listed, inter, *refs):
+    integ, out, total = refs[tables : tables + 3]
+    couple(listed, inter, refs[:tables], total, *refs[tables + 3 :])
 
     @pl.loop(0, integ.shape[0])
     def _(p):
         out[p] = integ[p] + COUPLING * total[p]
 
 
-def late_body(listed, inter, other, so_far, inverse, out, total, *scratch):
+def late_body(listed, inter, other, so_far, inverse, out, one, two, total, *scratch):
     couple(listed, inter, (other,), total, *scratch)
 
     @pl.loop(0, so_far.shape[0])
     def _(p):
         out[p] = ((so_far[p] + COUPLING * total[p]) * inverse[p]).astype(out.dtype)
+
+    split(out, one, two)
 
 
 def last_body(listed, inter, other, so_far, inverse, integ, out, energy, rows, kept, sem, total, *scratch):
@@ -503,10 +543,10 @@
     pl.loop(0, count)(lambda p: result(p).wait())
 
 
-def coupling_scratch(count, width, tables):
+def coupling_scratch(count, width, slots):
     return [
         pltpu.VMEM((count + 1, width, width), jnp.float32),
-        pltpu.VMEM((tables * count + 1, width, width), jnp.bfloat16),
+        pltpu.VMEM((slots + 1, width, width), jnp.bfloat16),
         pltpu.VMEM((UNIT, width, 2 * width), jnp.bfloat16),
         pltpu.VMEM((UNIT, width, 2 * width), jnp.bfloat16),
     ]
@@ -518,8 +558,8 @@
         opening_body,
         tuple(jax.ShapeDtypeStruct(x.shape, x.dtype) for x in (integ, inter, integ, inverse)),
         (VMEM,) * 4,
-        [SMEM, ANY, VMEM, VMEM, ANY, ANY],
-        coupling_scratch(count, width, 2)
+        [SMEM, HBM, VMEM, VMEM, HBM, HBM],
+        coupling_scratch(count, width, 2 * count)
         + [pltpu.SemaphoreType.DMA((CHUNKS,)), pltpu.SemaphoreType.DMA((2,))],
         flops=2 * inter.shape[0] * width**3,
         moved=inter.size * 2,
@@ -528,33 +568,34 @@
     )(listed, inter, here, other, integ, inverse)
 
 
-def early_part(listed, inter, here, other, integ):
+def early_part(listed, inter, tables, integ, name):
     count, width, _ = integ.shape
-    return call(
-        early_body,
+    slots = sum(table.shape[0] for table in tables)
+    return call(
+        functools.partial(early_body, len(tables)),
         jax.ShapeDtypeStruct(integ.shape, jnp.float32),
         VMEM,
-        [SMEM, VMEM, VMEM, VMEM, VMEM],
-        coupling_scratch(count, width, 2),
-        flops=2 * inter.shape[0] * width**3,
-        moved=inter.size * 2,
-        limit=24,
-        name="early",
-    )(listed, inter, here, other, integ)
-
-
-def late_part(listed, inter, other, so_far, inverse):
-    count, width, _ = so_far.shape
-    return call(
-        late_body,
-        jax.ShapeDtypeStruct(so_far.shape, jnp.bfloat16),
-        VMEM,
-        [SMEM, VMEM, VMEM, VMEM, VMEM],
-        coupling_scratch(count, width, 1),
+        [SMEM, VMEM, VMEM] + [VMEM] * len(tables),
+        coupling_scratch(count, width, slots),
         flops=inter.shape[0] * width**3,
         moved=inter.size * 2,
         limit=24,
-        name="late",
+        name=name,
+    )(listed, inter, *tables, integ)
+
+
+def late_part(listed, inter, other, so_far, inverse):
+    count, width, _ = so_far.shape
+    return call(
+        late_body,
+        amps_shapes(so_far),
+        (VMEM,) * 3,
+        [SMEM, VMEM, VMEM, VMEM, VMEM],
+        coupling_scratch(count, width, count // 2),
+        flops=inter.shape[0] * width**3,
+        moved=inter.size * 2,
+        limit=24,
+        name="later",
     )(listed, inter, other, so_far, inverse)
 
 
@@ -573,7 +614,7 @@
             pltpu.VMEM((count, width, width), jnp.float32),
             pltpu.SemaphoreType.DMA((count,)),
         ]
-        + coupling_scratch(count, width, 1),
+        + coupling_scratch(count, width, count // 2),
         flops=inter.shape[0] * width**3,
         moved=inter.size * 2,
         limit=24,
@@ -605,7 +646,11 @@
     swap_across = lambda x: lax.ppermute(x, "pairs", across_perm)
 
     inter = intersections.reshape(count * near, width, width)
-    table, branch = plan(pair_orbitals, block_sizes, orbitals)
+    table, branch = plan(
+        pair_orbitals,
+        block_sizes,
+        orbitals,
+    )
 
     def after(value, *before):
         return lax.optimization_barrier((value,) + before)[0]
@@ -618,10 +663,10 @@
             left = left_part(table, blocks, maps)
             half_one = serve(after(table, left), blocks, got[0], 0, count)
             back_one = swap_across(half_one)
-            integ, start, inverse, early, late = own_part(
+            integ, start, inverse, *lists = own_part(
                 after(table, half_one), sizes, shift, near_pairs, blocks, maps, energy, left, scale
             )
-            half_two = serve(after(table, early), blocks, got[1], got[0].shape[0], count)
+            half_two = serve(after(table, lists[0]), blocks, got[1], got[0].shape[0], count)
             back_two = swap_across(half_two)
             integ, start = integrals_part(
                 functools.partial(beside_body, scale),
@@ -635,7 +680,7 @@
                 24,
                 "beside",
             )
-            integ, start = integrals_part(
+            integ, *start = integrals_part(
                 functools.partial(across_body, scale, orbitals),
                 table,
                 (back_one, back_two),
@@ -647,11 +692,11 @@
                 24,
                 "across",
             )
-            return integ, start, inverse, early, late
+            return integ, start, inverse, lists
 
         return run
 
-    integ, amps, inverse, early, late = lax.switch(
+    integ, amps, inverse, lists = lax.switch(
         branch[0],
         [integrals_with(s) for s in SLOTS],
         table,
@@ -662,17 +707,22 @@
         pno_sizes,
         neighbours.T,
     )
+    early, late, later = lists
     for iteration in range(ITERS):
-        far = swap_across(amps)
-        close = swap_beside(amps)
+        whole, one, two = amps
+        far = swap_across(one)
+        farther = swap_across(two)
+        close = swap_beside(whole)
         if iteration == 0:
-            so_far, inter, integ, inverse = opening_part(early, inter, amps, close, integ, inverse)
+            stay = pltpu.with_memory_space_constraint(inter, pltpu.HBM)
+            so_far, inter, integ, inverse = opening_part(early, stay, whole, close, integ, inverse)
         else:
-            so_far = early_part(early, inter, amps, close, integ)
+            so_far = early_part(early, inter, (whole, close), integ, "early")
+        so_far = early_part(late, inter, (far,), so_far, "late")
         if iteration < ITERS - 1:
-            amps = late_part(late, inter, far, so_far, inverse)
+            amps = late_part(later, inter, farther, so_far, inverse)
         else:
-            amps, energies = last_part(late, inter, far, so_far, inverse, integ)
+            amps, energies = last_part(later, inter, farther, so_far, inverse, integ)
     return (amps, energies.reshape(count))
 
 

time: 137 us -> 144 us (1.051)
  the two profiles are of different devices: /device:TPU:4 before, /device:TPU:6 now
where the time goes in v5:
time: 144 us; the launch traced here: 142 us
  Pallas kernels  83.8 us (58%)
  starting transfers between devices  40.5 us (28%)
  waiting for transfers between devices  16.1 us (11%)
  between operations  1.59 us (1%)
    ppermute x8, starting transfers between devices, shards(): swap_across = lambda x: lax.ppermute(x, 'pairs', across_perm)  40.3 us
    pallas_call x3, Pallas kernels, early_part(): call(functools.partial(early_body, len(tables)), jax.ShapeDtypeStruct(int...  16.9 us
    ppermute x8, waiting for transfers between devices, shards(): swap_across = lambda x: lax.ppermute(x, 'pairs', across_perm)  16.1 us
    pallas_call x1, Pallas kernels, own_part(): call(functools.partial(own_body, scale, orbitals), (jax.ShapeDtypeStruct(...  15.2 us
    pallas_call x2, Pallas kernels, integrals_part(): call(body, outs, (VMEM,) * len(outs), [SMEM] + [VMEM] * (n + 4), scratch...  11.5 us
    pallas_call x1, Pallas kernels, left_part(): call(left_body, jax.ShapeDtypeStruct((count, width, depth), jnp.bfloat16)...  11.1 us
    pallas_call x1, Pallas kernels, opening_part(): call(opening_body, tuple((jax.ShapeDtypeStruct(x.shape, x.dtype) for x in...  10.3 us
    pallas_call x1, Pallas kernels, last_part(): call(last_body, (jax.ShapeDtypeStruct(so_far.shape, jnp.float32), jax.Sha...  5.57 us
  transfers between devices with their start and end apart: 11, of which 1 were waited for; matrix products, arithmetic and copies ran while one was open for 0% of the time, Pallas kernels for 48%

profile of v5, /device:TPU:6, one launch (start us, length us, event | category | flops | bytes accessed | tf_op | source)
XLA Modules:
  0.0 142.3 jit_solution(11027306178011630018)
XLA Ops:
  0.6 2.2 %plan.1 = (s32[128]{0:T(128)S(1)}, s32[1]{0:T(128)}) custom-call(s32[2,4096]{1,0:T(2,128)} %bitcast.24, s32[2048]{0:T(1024)} %sizes_hbm.1), custom_call_target="tpu_custom_call" | custom-call | bytes 65536 | tf_op jit(solution)/shard_map/plan/pallas_call | solution.py:127
  3.4 82.1 %conditional.1 = (f32[32,128,128]{2,1,0:T(8,128)S(1)}, bf16[32,128,128]{2,1,0:T(8,128)(2,1)}, bf16[16,128,128]{2,1,0:T(8,128)(2,1)S(1)}, bf16[16,128,128]{2,1,0:...) conditional(s32[]{:T(128)} %bitcast.1, (s32[128]{0:T(128)S(1)}, ...), branch_computations={%region_0.0_spmd, %region_1.0_spmd, %region_2.0_spmd, %region_3.0_... | conditional | flops 7516192768 | bytes 167843280 | solution.py:699
  3.5 0.1 collective-permute-start.4
  3.6 0.0 copy-start
  3.6 0.0 slice-start
  3.6 2.8 %pack.6 = (bf16[8,512,128]{2,1,0:T(8,128)(2,1)S(1)}, bf16[9,512,128]{2,1,0:T(8,128)(2,1)S(1)}) custom-call(s32[128]{0:T(128)S(1)} %get-tuple-element.98.table, bf16[32,512,128]{2,1,0:T(8,128)(2,1)} %get-tuple-element.86.maps), custom_call_target="tpu_custom_call" | custom-call | bytes 4456448 | tf_op jit(solution)/shard_map/cond/branch_0_fun/pack/pallas_call | solution.py:172
  6.4 8.8 %collective-permute-start = (bf16[8,512,128]{2,1,0:T(8,128)(2,1)S(1)}, bf16[8,512,128]{2,1,0:T(8,128)(2,1)S(1)}, u32[]{:S(2)}, u32[]{:S(2)}) collective-permute-start(bf16[8,512,128]{2,1,0:T(8,128)(2,1)S(1)} %get-tuple-element.88), channel_id=1, source_target_pairs={{1,2},{2,1},{3,4},{4,3},{5,6},{6,5},{7,8},{8,7},{9,10},{10,9},{11,... | collective-permute-start | bytes 3145736 | tf_op jit(solution)/shard_map/cond/branch_0_fun/ppermute | solution.py:646
  15.2 0.0 slice-start.1
  15.2 2.2 %collective-permute-start.2 = (bf16[9,512,128]{2,1,0:T(8,128)(2,1)S(1)}, bf16[9,512,128]{2,1,0:T(8,128)(2,1)S(1)}, u32[]{:S(2)}, u32[]{:S(2)}) collective-permute-start(bf16[9,512,128]{2,1,0:T(8,128)(2,1)S(1)} %get-tuple-element.96), channel_id=1, source_target_pairs={{1,2},{2,1},{3,4},{4,3},{5,6},{6,5},{7,8},{8,7},{9,10},{10,9},{11,... | collective-permute-start | bytes 3538952 | tf_op jit(solution)/shard_map/cond/branch_0_fun/ppermute | solution.py:646
  17.4 0.0 copy-done
  17.4 11.1 %left.6.refs_2_ = bf16[32,128,512]{2,1,0:T(8,128)(2,1)S(1)} custom-call(s32[128]{0:T(128)S(1)} %get-tuple-element.98.table, bf16[16,512,512]{2,1,0:T(8,128)(2,1)} %get-tuple-element.85.blocks, bf16[32,512,128]{2,1,0:T(8,128)(2,1)S(1)} %copy-done), custom_call_target="tpu_custom_call" | custom-call | flops 2147483648 | bytes 8388608 | tf_op jit(solution)/shard_map/cond/branch_0_fun/left/pallas_call | solution.py:201
  28.5 0.0 copy-start.6
  28.5 0.0 copy-start.12
  28.5 0.0 copy-start.18
  28.6 0.0 copy-start.24
  28.6 0.0 collective-permute-done.maps
  28.6 0.0 slice-done
  28.6 0.0 slice-done.1
  28.6 2.6 %serve.12 = bf16[8,512,128]{2,1,0:T(8,128)(2,1)S(1)} custom-call(s32[128]{0:T(128)S(1)} %get-tuple-element.98.table, bf16[16,512,512]{2,1,0:T(8,128)(2,1)S(1)} %bitcast.6, bf16[8,512,128]{2,1,0:T(8,128)(2,1)S(1)} %collective-permute-done.maps), custom_call_target="tpu_custom_call" | custom-call | flops 536870912 | bytes 6291456 | tf_op jit(solution)/shard_map/cond/branch_0_fun/serve/pallas_call | solution.py:318
  31.2 0.0 copy-done.6
  31.2 0.0 copy-done.12
  31.2 0.0 copy-done.18
  31.2 0.0 copy-done.24
  31.2 15.2 %own.6 = (f32[32,128,128]{2,1,0:T(8,128)S(1)}, bf16[32,128,128]{2,1,0:T(8,128)(2,1)S(1)}, f32[32,128,128]{2,1,0:T(8,128)}, s32[288]{0:T(512)S(1)}, s32[288]{0:T(512)S(1)}, /*index=5*/s32[288]{0:T(512)S(1)}) custom-call(s32[128]{0:T(128)S(1)} %get-tuple-element.98.table, s32[32]{0:T(128)S(1)} %copy-done.18, f32[32]{0:T(128)S(1)} %copy-done.24, ...), custom_call_target="tpu_custom_call" | custom-call | flops 1073741824 | bytes 8388608 | tf_op jit(solution)/shard_map/cond/branch_0_fun/own/pallas_call | solution.py:279
  46.4 0.0 collective-permute-done.2.maps
  46.4 1.7 %serve.13 = bf16[9,512,128]{2,1,0:T(8,128)(2,1)S(1)} custom-call(s32[128]{0:T(128)S(1)} %get-tuple-element.98.table, bf16[16,512,512]{2,1,0:T(8,128)(2,1)S(1)} %bitcast.6, bf16[9,512,128]{2,1,0:T(8,128)(2,1)S(1)} %collective-permute-done.2.maps), custom_call_target="tpu_custom_call" | custom-call | flops 603979776 | bytes 7077888 | tf_op jit(solution)/shard_map/cond/branch_0_fun/serve/pallas_call | solution.py:318
  48.1 6.0 %collective-permute-start.3 = (bf16[9,512,128]{2,1,0:T(8,128)(2,1)S(1)}, bf16[9,512,128]{2,1,0:T(8,128)(2,1)S(1)}, u32[]{:S(2)}, u32[]{:S(2)}) collective-permute-start(bf16[9,512,128]{2,1,0:T(8,128)(2,1)S(1)} %serve.13), channel_id=1, source_target_pairs={{1,2},{2,1},{3,4},{4,3},{5,6},{6,5},{7,8},{8,7},{9,10},{10,9},{11,... | collective-permute-start | bytes 3538952 | tf_op jit(solution)/shard_map/cond/branch_0_fun/ppermute | solution.py:646
  54.1 3.8 %collective-permute-start.1 = (bf16[8,512,128]{2,1,0:T(8,128)(2,1)S(1)}, bf16[8,512,128]{2,1,0:T(8,128)(2,1)S(1)}, u32[]{:S(2)}, u32[]{:S(2)}) collective-permute-start(bf16[8,512,128]{2,1,0:T(8,128)(2,1)S(1)} %serve.12), channel_id=1, source_target_pairs={{1,2},{2,1},{3,4},{4,3},{5,6},{6,5},{7,8},{8,7},{9,10},{10,9},{11,... | collective-permute-start | bytes 3145736 | tf_op jit(solution)/shard_map/cond/branch_0_fun/ppermute | solution.py:646
  57.9 0.0 collective-permute-done.4.blocks
  57.9 7.1 %beside.6 = (f32[32,128,128]{2,1,0:T(8,128)S(1)}, bf16[32,128,128]{2,1,0:T(8,128)(2,1)S(1)}) custom-call(s32[128]{0:T(128)S(1)} %get-tuple-element.98.table, bf16[16,512,512]{2,1,0:T(8,128)(2,1)S(1)} %collective-permute-done.4.blocks, bf16[32,512,128]{2,1,0:T(8,128)(2,1)S(1)} %copy-done, bf16[32,128,512]{2,1,0:T(8,128)(2,1)S(1)} %left.6.refs_2_, ...), custom_call_target="tpu_custom_call" | custom-call | flops 1073741824 | bytes 4194304 | tf_op jit(solution)/shard_map/cond/branch_0_fun/beside/pallas_call | solution.py:402
  65.1 16.0 %collective-permute-done.1.refs_0_ = bf16[8,512,128]{2,1,0:T(8,128)(2,1)S(1)} collective-permute-done((bf16[8,512,128]{2,1,0:T(8,128)(2,1)S(1)}, bf16[8,512,128]{2,1,0:T(8,128)(2,1)S(1)}, u32[]{:S(2)}, u32[]{:S(2)}) %collective-permute-start.1) | collective-permute-done | bytes 1048608 | tf_op jit(solution)/shard_map/cond/branch_0_fun/ppermute | solution.py:646
  81.1 0.0 collective-permute-done.3.refs_1_
  81.1 4.4 %across.6 = (f32[32,128,128]{2,1,0:T(8,128)S(1)}, bf16[32,128,128]{2,1,0:T(8,128)(2,1)}, bf16[16,128,128]{2,1,0:T(8,128)(2,1)S(1)}, bf16[16,128,128]{2,1,0:T(8,128)(2,1)}) custom-call(s32[128]{0:T(128)S(1)} %get-tuple-element.98.table, bf16[8,512,128]{2,1,0:T(8,128)(2,1)S(1)} %collective-permute-done.1.refs_0_, ...), custom_call_target="tpu_custom_call" | custom-call | flops 1073741824 | bytes 4194304 | tf_op jit(solution)/shard_map/cond/branch_0_fun/across/pallas_call | solution.py:402
  85.5 0.0 collective-permute-start.30
  85.5 6.4 %collective-permute-start.32 = (bf16[16,128,128]{2,1,0:T(8,128)(2,1)S(1)}, bf16[16,128,128]{2,1,0:T(8,128)(2,1)S(1)}, u32[]{:S(2)}, u32[]{:S(2)}) collective-permute-start(bf16[16,128,128]{2,1,0:T(8,128)(2,1)S(1)} %get-tuple-element.265), channel_id=1, source_target_pairs={{1,2},{2,1},{3,4},{4,3},{5,6},{6,5},{7,8},{8,7},{9,10},{10,9},{11,... | collective-permute-start | bytes 1572872 | tf_op jit(solution)/shard_map/ppermute | solution.py:646
  91.9 3.4 %collective-permute-start.31 = (bf16[16,128,128]{2,1,0:T(8,128)(2,1)}, bf16[16,128,128]{2,1,0:T(8,128)(2,1)S(1)}, u32[]{:S(2)}, u32[]{:S(2)}) collective-permute-start(bf16[16,128,128]{2,1,0:T(8,128)(2,1)} %get-tuple-element.263), channel_id=1, source_target_pairs={{1,2},{2,1},{3,4},{4,3},{5,6},{6,5},{7,8},{8,7},{9,10},{10,9},{11,... | collective-permute-start | bytes 1572872 | tf_op jit(solution)/shard_map/ppermute | solution.py:646
  95.3 0.0 collective-permute-done.30.near_by
  95.3 10.3 %opening.1 = (f32[32,128,128]{2,1,0:T(8,128)S(1)}, bf16[256,128,128]{2,1,0:T(8,128)(2,1)S(1)}, f32[32,128,128]{2,1,0:T(8,128)S(1)}, f32[32,128,128]{2,1,0:T(8,128)S(1)}) custom-call(s32[288]{0:T(512)S(1)} %get-tuple-element.258.listed, bf16[256,128,128]{2,1,0:T(8,128)(2,1)} %bitcast.17, bf16[32,128,128]{2,1,0:T(8,128)(2,1)} %get-tuple-element.259.here, ...), custom_call_target="tpu_custom_call" | custom-call | flops 1073741824 | bytes 8388608 | tf_op jit(solution)/shard_map/opening/pallas_call | solution.py:557
  105.6 0.0 collective-permute-done.32.refs_0_
  105.6 4.3 %late.2.so_far = f32[32,128,128]{2,1,0:T(8,128)S(1)} custom-call(s32[288]{0:T(512)S(1)} %get-tuple-element.264.listed, bf16[256,128,128]{2,1,0:T(8,128)(2,1)S(1)} %get-tuple-element.262.inter, bf16[16,128,128]{2,1,0:T(8,128)(2,1)S(1)} %collective-permute-done.32.refs_0_, f32[32,128,128]{2,1,0:T(8,128)S(1)} %get-tuple-element.266.refs_1_), custom_call_target="tpu_custom_call" | custom-call | flops 536870912 | bytes 8388608 | tf_op jit(solution)/shard_map/late/pallas_call | solution.py:574
  109.9 0.0 collective-permute-done.31.other
  110.0 4.0 %later.1 = (bf16[32,128,128]{2,1,0:T(8,128)(2,1)S(1)}, bf16[16,128,128]{2,1,0:T(8,128)(2,1)S(1)}, bf16[16,128,128]{2,1,0:T(8,128)(2,1)S(1)}) custom-call(s32[288]{0:T(512)S(1)} %get-tuple-element.257.listed, bf16[256,128,128]{2,1,0:T(8,128)(2,1)S(1)} %get-tuple-element.262.inter, bf16[16,128,128]{2,1,0:T(8,128)(2,1)S(1)} %collective-permute-done.31.other, ...), custom_call_target="tpu_custom_call" | custom-call | flops 536870912 | bytes 8388608 | tf_op jit(solution)/shard_map/later/pallas_call | solution.py:589
  113.9 0.1 collective-permute-start.35
  114.0 5.9 %collective-permute-start.34 = (bf16[16,128,128]{2,1,0:T(8,128)(2,1)S(1)}, bf16[16,128,128]{2,1,0:T(8,128)(2,1)S(1)}, u32[]{:S(2)}, u32[]{:S(2)}) collective-permute-start(bf16[16,128,128]{2,1,0:T(8,128)(2,1)S(1)} %get-tuple-element.269), channel_id=1, source_target_pairs={{1,2},{2,1},{3,4},{4,3},{5,6},{6,5},{7,8},{8,7},{9,10},{10,9},{11,... | collective-permute-start | bytes 1572872 | tf_op jit(solution)/shard_map/ppermute | solution.py:646
  119.9 3.9 %collective-permute-start.33 = (bf16[16,128,128]{2,1,0:T(8,128)(2,1)S(1)}, bf16[16,128,128]{2,1,0:T(8,128)(2,1)S(1)}, u32[]{:S(2)}, u32[]{:S(2)}) collective-permute-start(bf16[16,128,128]{2,1,0:T(8,128)(2,1)S(1)} %get-tuple-element.268), channel_id=1, source_target_pairs={{1,2},{2,1},{3,4},{4,3},{5,6},{6,5},{7,8},{8,7},{9,10},{10,9},{11,... | collective-permute-start | bytes 1572872 | tf_op jit(solution)/shard_map/ppermute | solution.py:646
  123.8 0.0 collective-permute-done.35.refs_1_
  123.8 8.3 %early.1.refs_1_ = f32[32,128,128]{2,1,0:T(8,128)S(1)} custom-call(s32[288]{0:T(512)S(1)} %get-tuple-element.258.listed, bf16[256,128,128]{2,1,0:T(8,128)(2,1)S(1)} %get-tuple-element.262.inter, bf16[32,128,128]{2,1,0:T(8,128)(2,1)S(1)} %get-tuple-element.270.refs_0_, bf16[32,128,128]{2,1,0:T(8,128)(2,1)S(1)} %collective-permute-done.35.refs_1_, ...), custom_call_target="tpu_custom_call" | custom-call | flops 536870912 | bytes 8388608 | tf_op jit(solution)/shard_map/early/pallas_call | solution.py:574
  132.2 0.0 collective-permute-done.34.refs_0_
  132.2 4.3 %late.3.so_far = f32[32,128,128]{2,1,0:T(8,128)S(1)} custom-call(s32[288]{0:T(512)S(1)} %get-tuple-element.264.listed, bf16[256,128,128]{2,1,0:T(8,128)(2,1)S(1)} %get-tuple-element.262.inter, bf16[16,128,128]{2,1,0:T(8,128)(2,1)S(1)} %collective-permute-done.34.refs_0_, f32[32,128,128]{2,1,0:T(8,128)S(1)} %early.1.refs_1_), custom_call_target="tpu_custom_call" | custom-call | flops 536870912 | bytes 8388608 | tf_op jit(solution)/shard_map/late/pallas_call | solution.py:574
  136.5 0.0 collective-permute-done.33.other
  136.5 5.6 %last.1 = (f32[32,128,128]{2,1,0:T(8,128)}, f32[1,32]{1,0:T(1,128)}) custom-call(s32[288]{0:T(512)S(1)} %get-tuple-element.257.listed, bf16[256,128,128]{2,1,0:T(8,128)(2,1)S(1)} %get-tuple-element.262.inter, bf16[16,128,128]{2,1,0:T(8,128)(2,1)S(1)} %collective-permute-done.33.other, f32[32,128,128]{2,1,0:T(8,128)S(1)} %late.3.so_far, ...), custom_call_target="tpu_custom_call" | custom-call | flops 536870912 | bytes 8388608 | tf_op jit(solution)/shard_map/last/pallas_call | solution.py:604
  (1 shorter events, 0.0 us)
Async XLA Ops:
  3.5 54.5 %collective-permute-start.4 = (bf16[16,512,512]{2,1,0:T(8,128)(2,1)}, bf16[16,512,512]{2,1,0:T(8,128)(2,1)S(1)}, u32[]{:S(2)}, u32[]{:S(2)}) collective-permute-start(bf16[16,512,512]{2,1,0:T(8,128)(2,1)} %get-tuple-element.85.blocks), channel_id=1, source_target_pairs={{0,1},{1,0},{2,3},{3,2},{4,5},{5,4},{6,7},{7,6},{8,9},{9,8},{10,11... | collective-permute-start | bytes 25165832 | tf_op jit(solution)/shard_map/cond/branch_0_fun/ppermute | solution.py:645
  3.6 13.9 %copy-start = (bf16[32,512,128]{2,1,0:T(8,128)(2,1)S(1)}, bf16[32,512,128]{2,1,0:T(8,128)(2,1)}, u32[]{:S(2)}) copy-start(bf16[32,512,128]{2,1,0:T(8,128)(2,1)} %get-tuple-element.86.maps) | copy-start | bytes 12582916 | tf_op jit(solution)/shard_map/cond
  3.6 25.0 %slice-start = ((s8[8388608]{0:T(1024)(128)(4,1)}), s8[4194304]{0:T(1024)(128)(4,1)S(1)}, s32[]{:S(2)}) async-start(s8[8388608]{0:T(1024)(128)(4,1)} %bitcast.5), calls=%async_computation | async-start | bytes 8388608 | tf_op jit(solution)/shard_map/cond
  6.4 22.2 %collective-permute-start = (bf16[8,512,128]{2,1,0:T(8,128)(2,1)S(1)}, bf16[8,512,128]{2,1,0:T(8,128)(2,1)S(1)}, u32[]{:S(2)}, u32[]{:S(2)}) collective-permute-start(bf16[8,512,128]{2,1,0:T(8,128)(2,1)S(1)} %get-tuple-element.88), channel_id=1, source_target_pairs={{1,2},{2,1},{3,4},{4,3},{5,6},{6,5},{7,8},{8,7},{9,10},{10,9},{11,... | collective-permute-start | bytes 3145736 | tf_op jit(solution)/shard_map/cond/branch_0_fun/ppermute | solution.py:646
  15.2 13.4 %slice-start.1 = ((s8[8388608]{0:T(1024)(128)(4,1)}), s8[4194304]{0:T(1024)(128)(4,1)S(1)}, s32[]{:S(2)}) async-start(s8[8388608]{0:T(1024)(128)(4,1)} %bitcast.5), calls=%async_computation.1 | async-start | bytes 8388608 | tf_op jit(solution)/shard_map/cond
  15.2 31.2 %collective-permute-start.2 = (bf16[9,512,128]{2,1,0:T(8,128)(2,1)S(1)}, bf16[9,512,128]{2,1,0:T(8,128)(2,1)S(1)}, u32[]{:S(2)}, u32[]{:S(2)}) collective-permute-start(bf16[9,512,128]{2,1,0:T(8,128)(2,1)S(1)} %get-tuple-element.96), channel_id=1, source_target_pairs={{1,2},{2,1},{3,4},{4,3},{5,6},{6,5},{7,8},{8,7},{9,10},{10,9},{11,... | collective-permute-start | bytes 3538952 | tf_op jit(solution)/shard_map/cond/branch_0_fun/ppermute | solution.py:646
  28.5 2.7 %copy-start.6 = (f32[32,128]{1,0:T(8,128)S(1)}, f32[32,128]{1,0:T(8,128)}, u32[]{:S(2)}) copy-start(f32[32,128]{1,0:T(8,128)} %get-tuple-element.93.energy) | copy-start | bytes 49156 | tf_op jit(solution)/shard_map/cond
  28.5 2.7 %copy-start.12 = (s32[8,32]{1,0:T(8,128)S(1)}, s32[8,32]{1,0:T(8,128)}, u32[]{:S(2)}) copy-start(s32[8,32]{1,0:T(8,128)} %get-tuple-element.92.near_pairs) | copy-start | bytes 3076 | tf_op jit(solution)/shard_map/cond
  28.5 2.7 %copy-start.18 = (s32[32]{0:T(128)S(1)}, s32[32]{0:T(128)}, u32[]{:S(2)}) copy-start(s32[32]{0:T(128)} %get-tuple-element.90.sizes) | copy-start | bytes 388 | tf_op jit(solution)/shard_map/cond
  28.6 2.7 %copy-start.24 = (f32[32]{0:T(128)S(1)}, f32[32]{0:T(128)}, u32[]{:S(2)}) copy-start(f32[32]{0:T(128)} %get-tuple-element.91.shift) | copy-start | bytes 388 | tf_op jit(solution)/shard_map/cond
  48.1 33.0 %collective-permute-start.3 = (bf16[9,512,128]{2,1,0:T(8,128)(2,1)S(1)}, bf16[9,512,128]{2,1,0:T(8,128)(2,1)S(1)}, u32[]{:S(2)}, u32[]{:S(2)}) collective-permute-start(bf16[9,512,128]{2,1,0:T(8,128)(2,1)S(1)} %serve.13), channel_id=1, source_target_pairs={{1,2},{2,1},{3,4},{4,3},{5,6},{6,5},{7,8},{8,7},{9,10},{10,9},{11,... | collective-permute-start | bytes 3538952 | tf_op jit(solution)/shard_map/cond/branch_0_fun/ppermute | solution.py:646
  54.1 27.0 %collective-permute-start.1 = (bf16[8,512,128]{2,1,0:T(8,128)(2,1)S(1)}, bf16[8,512,128]{2,1,0:T(8,128)(2,1)S(1)}, u32[]{:S(2)}, u32[]{:S(2)}) collective-permute-start(bf16[8,512,128]{2,1,0:T(8,128)(2,1)S(1)} %serve.12), channel_id=1, source_target_pairs={{1,2},{2,1},{3,4},{4,3},{5,6},{6,5},{7,8},{8,7},{9,10},{10,9},{11,... | collective-permute-start | bytes 3145736 | tf_op jit(solution)/shard_map/cond/branch_0_fun/ppermute | solution.py:646
  85.5 9.8 %collective-permute-start.30 = (bf16[32,128,128]{2,1,0:T(8,128)(2,1)}, bf16[32,128,128]{2,1,0:T(8,128)(2,1)S(1)}, u32[]{:S(2)}, u32[]{:S(2)}) collective-permute-start(bf16[32,128,128]{2,1,0:T(8,128)(2,1)} %get-tuple-element.259.here), channel_id=1, source_target_pairs={{0,1},{1,0},{2,3},{3,2},{4,5},{5,4},{6,7},{7,6},{8,9},{9,8},{10,11... | collective-permute-start | bytes 3145736 | tf_op jit(solution)/shard_map/ppermute | solution.py:645
  85.5 20.1 %collective-permute-start.32 = (bf16[16,128,128]{2,1,0:T(8,128)(2,1)S(1)}, bf16[16,128,128]{2,1,0:T(8,128)(2,1)S(1)}, u32[]{:S(2)}, u32[]{:S(2)}) collective-permute-start(bf16[16,128,128]{2,1,0:T(8,128)(2,1)S(1)} %get-tuple-element.265), channel_id=1, source_target_pairs={{1,2},{2,1},{3,4},{4,3},{5,6},{6,5},{7,8},{8,7},{9,10},{10,9},{11,... | collective-permute-start | bytes 1572872 | tf_op jit(solution)/shard_map/ppermute | solution.py:646
  91.9 18.0 %collective-permute-start.31 = (bf16[16,128,128]{2,1,0:T(8,128)(2,1)}, bf16[16,128,128]{2,1,0:T(8,128)(2,1)S(1)}, u32[]{:S(2)}, u32[]{:S(2)}) collective-permute-start(bf16[16,128,128]{2,1,0:T(8,128)(2,1)} %get-tuple-element.263), channel_id=1, source_target_pairs={{1,2},{2,1},{3,4},{4,3},{5,6},{6,5},{7,8},{8,7},{9,10},{10,9},{11,... | collective-permute-start | bytes 1572872 | tf_op jit(solution)/shard_map/ppermute | solution.py:646
  113.9 9.9 %collective-permute-start.35 = (bf16[32,128,128]{2,1,0:T(8,128)(2,1)S(1)}, bf16[32,128,128]{2,1,0:T(8,128)(2,1)S(1)}, u32[]{:S(2)}, u32[]{:S(2)}) collective-permute-start(bf16[32,128,128]{2,1,0:T(8,128)(2,1)S(1)} %get-tuple-element.270.refs_0_), channel_id=1, source_target_pairs={{0,1},{1,0},{2,3},{3,2},{4,5},{5,4},{6,7},{7,6},{8,9},{9,8},{10,11... | collective-permute-start | bytes 3145736 | tf_op jit(solution)/shard_map/ppermute | solution.py:645
  114.0 18.2 %collective-permute-start.34 = (bf16[16,128,128]{2,1,0:T(8,128)(2,1)S(1)}, bf16[16,128,128]{2,1,0:T(8,128)(2,1)S(1)}, u32[]{:S(2)}, u32[]{:S(2)}) collective-permute-start(bf16[16,128,128]{2,1,0:T(8,128)(2,1)S(1)} %get-tuple-element.269), channel_id=1, source_target_pairs={{1,2},{2,1},{3,4},{4,3},{5,6},{6,5},{7,8},{8,7},{9,10},{10,9},{11,... | collective-permute-start | bytes 1572872 | tf_op jit(solution)/shard_map/ppermute | solution.py:646
  119.9 16.6 %collective-permute-start.33 = (bf16[16,128,128]{2,1,0:T(8,128)(2,1)S(1)}, bf16[16,128,128]{2,1,0:T(8,128)(2,1)S(1)}, u32[]{:S(2)}, u32[]{:S(2)}) collective-permute-start(bf16[16,128,128]{2,1,0:T(8,128)(2,1)S(1)} %get-tuple-element.268), channel_id=1, source_target_pairs={{1,2},{2,1},{3,4},{4,3},{5,6},{6,5},{7,8},{8,7},{9,10},{10,9},{11,... | collective-permute-start | bytes 1572872 | tf_op jit(solution)/shard_map/ppermute | solution.py:646

commit v6 on v4

--- a/solution.py
+++ b/solution.py
@@ -10,9 +10,10 @@
 
 ITERS = 2
 COUPLING = 0.35
-SLOTS = (16, 18, 20, 24, 32)
+SLOTS = (17, 18, 19, 20, 24, 32)
 
 ANY = pl.BlockSpec(memory_space=pl.ANY)
+HBM = pl.BlockSpec(memory_space=pltpu.HBM)
 VMEM = pl.BlockSpec(memory_space=pltpu.VMEM)
 SMEM = pl.BlockSpec(memory_space=pltpu.SMEM)
 
@@ -65,7 +66,7 @@
             store(k, values)
 
 
-def plan_body(orbitals, everyone, pairs_hbm, sizes, table, branch, mine, theirs, sem):
+def plan_body(orbitals, pairs_hbm, sizes_hbm, table, branch, everyone, sizes, mine, theirs, sem):
     count = mine.shape[1] // 4
     lanes = mine.shape[1]
     devices = everyone.shape[1] // count
@@ -79,9 +80,16 @@
         start = pl.multiple_of(who // 4 * lanes, lanes)
         return pltpu.make_async_copy(pairs_hbm.at[:, pl.ds(start, lanes)], place, sem.at[k])
 
-    copies = (fetch(device, mine, 0), fetch(near_by, theirs, 1))
+    copies = (
+        fetch(device, mine, 0),
+        fetch(near_by, theirs, 1),
+        pltpu.make_async_copy(sizes_hbm, sizes, sem.at[3]),
+    )
+    whole = pltpu.make_async_copy(pairs_hbm, everyone, sem.at[2])
+    whole.start()
     for copy in copies:
         copy.start()
+    whole.wait()
 
     groups = devices * count // lanes
     second = jnp.concatenate([everyone[1:2, g * lanes : (g + 1) * lanes] for g in range(groups)], axis=0)
@@ -120,12 +128,21 @@
         functools.partial(plan_body, orbitals),
         (jax.ShapeDtypeStruct((128,), jnp.int32), jax.ShapeDtypeStruct((1,), jnp.int32)),
         (SMEM, SMEM),
-        [VMEM, ANY, SMEM],
-        [pltpu.SMEM((2, 128), jnp.int32), pltpu.SMEM((2, 128), jnp.int32), pltpu.SemaphoreType.DMA((2,))],
+        [HBM, HBM],
+        [
+            pltpu.VMEM(turned.shape, jnp.int32),
+            pltpu.SMEM(block_sizes.shape, jnp.int32),
+            pltpu.SMEM((2, 128), jnp.int32),
+            pltpu.SMEM((2, 128), jnp.int32),
+            pltpu.SemaphoreType.DMA((4,)),
+        ],
         moved=turned.size * 8,
         limit=4,
         name="plan",
-    )(turned, turned, block_sizes)
+    )(
+        pltpu.with_memory_space_constraint(turned, pltpu.HBM),
+        pltpu.with_memory_space_constraint(block_sizes, pltpu.HBM),
+    )
 
 
 def pack_body(orbitals, table, maps, *refs):
@@ -518,7 +535,7 @@
         opening_body,
         tuple(jax.ShapeDtypeStruct(x.shape, x.dtype) for x in (integ, inter, integ, inverse)),
         (VMEM,) * 4,
-        [SMEM, ANY, VMEM, VMEM, ANY, ANY],
+        [SMEM, HBM, VMEM, VMEM, ANY, ANY],
         coupling_scratch(count, width, 2)
         + [pltpu.SemaphoreType.DMA((CHUNKS,)), pltpu.SemaphoreType.DMA((2,))],
         flops=2 * inter.shape[0] * width**3,
@@ -613,7 +630,7 @@
     def integrals_with(slots):
         def run(table, blocks, maps, energy, shift, sizes, near_pairs):
             blocks_beside = swap_beside(blocks)
-            packed = pack(table, maps, (slots // 2, slots - slots // 2), orbitals)
+            packed = pack(table, maps, (slots - slots // 2, slots // 2), orbitals)
             got = [swap_across(x) for x in packed]
             left = left_part(table, blocks, maps)
             half_one = serve(after(table, left), blocks, got[0], 0, count)
@@ -666,7 +683,8 @@
         far = swap_across(amps)
         close = swap_beside(amps)
         if iteration == 0:
-            so_far, inter, integ, inverse = opening_part(early, inter, amps, close, integ, inverse)
+            stay = pltpu.with_memory_space_constraint(inter, pltpu.HBM)
+            so_far, inter, integ, inverse = opening_part(early, stay, amps, close, integ, inverse)
         else:
             so_far = early_part(early, inter, amps, close, integ)
         if iteration < ITERS - 1:

time: 137 us -> 133 us (0.971)
  the two profiles are of different devices: /device:TPU:4 before, /device:TPU:2 now
where the time goes in v6:
time: 133 us; the launch traced here: 132 us
  Pallas kernels  73 us (55%)
  waiting for transfers between devices  31.8 us (24%)
  starting transfers between devices  24.7 us (19%)
  between operations  1.53 us (1%)
    ppermute x6, waiting for transfers between devices, shards(): swap_across = lambda x: lax.ppermute(x, 'pairs', across_perm)  30.4 us
    ppermute x6, starting transfers between devices, shards(): swap_across = lambda x: lax.ppermute(x, 'pairs', across_perm)  24.4 us
    pallas_call x1, Pallas kernels, own_part(): call(functools.partial(own_body, scale, orbitals), (jax.ShapeDtypeStruct(...  12 us
    pallas_call x1, Pallas kernels, left_part(): call(left_body, jax.ShapeDtypeStruct((count, width, depth), jnp.bfloat16)...  11.1 us
    pallas_call x2, Pallas kernels, integrals_part(): call(body, (jax.ShapeDtypeStruct(integ.shape, integ.dtype), jax.ShapeDtyp...  10.7 us
    pallas_call x1, Pallas kernels, opening_part(): call(opening_body, tuple((jax.ShapeDtypeStruct(x.shape, x.dtype) for x in...  9.02 us
    pallas_call x1, Pallas kernels, early_part(): call(early_body, jax.ShapeDtypeStruct(integ.shape, jnp.float32), VMEM, [S...  7.77 us
    pallas_call x1, Pallas kernels, last_part(): call(last_body, (jax.ShapeDtypeStruct(so_far.shape, jnp.float32), jax.Sha...  7.31 us
  transfers between devices with their start and end apart: 9, of which 6 were waited for; matrix products, arithmetic and copies ran while one was open for 0% of the time, Pallas kernels for 41%

profile of v6, /device:TPU:2, one launch (start us, length us, event | category | flops | bytes accessed | tf_op | source)
XLA Modules:
  0.0 131.6 jit_solution(126734682830429263)
XLA Ops:
  0.6 2.2 %plan.1 = (s32[128]{0:T(128)S(1)}, s32[1]{0:T(128)}) custom-call(s32[2,4096]{1,0:T(2,128)} %bitcast.24, s32[2048]{0:T(1024)} %sizes_hbm.1), custom_call_target="tpu_custom_call" | custom-call | bytes 65536 | tf_op jit(solution)/shard_map/plan/pallas_call | solution.py:127
  3.4 74.2 %conditional.1 = (f32[32,128,128]{2,1,0:T(8,128)S(1)}, bf16[32,128,128]{2,1,0:T(8,128)(2,1)S(1)}, f32[32,128,128]{2,1,0:T(8,128)}, s32[288]{0:T(512)S(1)}, s32[288]{0:T(512)S(1)}) conditional(s32[]{:T(128)} %bitcast.1, (s32[128]{0:T(128)S(1)}, bf16[16,512,512]{2,1,0:T(8,128)(2,1)}, bf16[32,512,128]{2,1,0:T(8,128)(2,1)}, ...), branch_computations={%region_0.0_spmd, %region_1.0_spmd, %region_2.0_spmd, %region_3.0_... | conditional | flops 7516192768 | bytes 167843264 | solution.py:671
  3.5 0.1 collective-permute-start.4
  3.6 0.0 copy-start
  3.6 0.0 slice-start
  3.6 2.7 %pack.6 = (bf16[9,512,128]{2,1,0:T(8,128)(2,1)S(1)}, bf16[8,512,128]{2,1,0:T(8,128)(2,1)S(1)}) custom-call(s32[128]{0:T(128)S(1)} %get-tuple-element.98.table, bf16[32,512,128]{2,1,0:T(8,128)(2,1)} %get-tuple-element.86.maps), custom_call_target="tpu_custom_call" | custom-call | bytes 4456448 | tf_op jit(solution)/shard_map/cond/branch_0_fun/pack/pallas_call | solution.py:172
  6.3 8.6 %collective-permute-start = (bf16[9,512,128]{2,1,0:T(8,128)(2,1)S(1)}, bf16[9,512,128]{2,1,0:T(8,128)(2,1)S(1)}, u32[]{:S(2)}, u32[]{:S(2)}) collective-permute-start(bf16[9,512,128]{2,1,0:T(8,128)(2,1)S(1)} %get-tuple-element.88), channel_id=1, source_target_pairs={{1,2},{2,1},{3,4},{4,3},{5,6},{6,5},{7,8},{8,7},{9,10},{10,9},{11,... | collective-permute-start | bytes 3538952 | tf_op jit(solution)/shard_map/cond/branch_0_fun/ppermute | solution.py:622
  14.9 0.0 slice-start.1
  15.0 2.2 %collective-permute-start.2 = (bf16[8,512,128]{2,1,0:T(8,128)(2,1)S(1)}, bf16[8,512,128]{2,1,0:T(8,128)(2,1)S(1)}, u32[]{:S(2)}, u32[]{:S(2)}) collective-permute-start(bf16[8,512,128]{2,1,0:T(8,128)(2,1)S(1)} %get-tuple-element.96), channel_id=1, source_target_pairs={{1,2},{2,1},{3,4},{4,3},{5,6},{6,5},{7,8},{8,7},{9,10},{10,9},{11,... | collective-permute-start | bytes 3145736 | tf_op jit(solution)/shard_map/cond/branch_0_fun/ppermute | solution.py:622
  17.2 0.0 copy-done
  17.2 11.1 %left.6.refs_2_ = bf16[32,128,512]{2,1,0:T(8,128)(2,1)S(1)} custom-call(s32[128]{0:T(128)S(1)} %get-tuple-element.98.table, bf16[16,512,512]{2,1,0:T(8,128)(2,1)} %get-tuple-element.85.blocks, bf16[32,512,128]{2,1,0:T(8,128)(2,1)S(1)} %copy-done), custom_call_target="tpu_custom_call" | custom-call | flops 2147483648 | bytes 8388608 | tf_op jit(solution)/shard_map/cond/branch_0_fun/left/pallas_call | solution.py:201
  28.2 0.0 copy-start.6
  28.3 0.0 copy-start.12
  28.3 0.0 copy-start.18
  28.3 0.0 copy-start.24
  28.3 0.5 collective-permute-done.maps
  28.8 0.0 slice-done
  28.8 0.0 slice-done.1
  28.8 3.0 %serve.12 = bf16[9,512,128]{2,1,0:T(8,128)(2,1)S(1)} custom-call(s32[128]{0:T(128)S(1)} %get-tuple-element.98.table, bf16[16,512,512]{2,1,0:T(8,128)(2,1)S(1)} %bitcast.6, bf16[9,512,128]{2,1,0:T(8,128)(2,1)S(1)} %collective-permute-done.maps), custom_call_target="tpu_custom_call" | custom-call | flops 603979776 | bytes 7077888 | tf_op jit(solution)/shard_map/cond/branch_0_fun/serve/pallas_call | solution.py:312
  31.9 7.9 %collective-permute-start.1 = (bf16[9,512,128]{2,1,0:T(8,128)(2,1)S(1)}, bf16[9,512,128]{2,1,0:T(8,128)(2,1)S(1)}, u32[]{:S(2)}, u32[]{:S(2)}) collective-permute-start(bf16[9,512,128]{2,1,0:T(8,128)(2,1)S(1)} %serve.12), channel_id=1, source_target_pairs={{1,2},{2,1},{3,4},{4,3},{5,6},{6,5},{7,8},{8,7},{9,10},{10,9},{11,... | collective-permute-start | bytes 3538952 | tf_op jit(solution)/shard_map/cond/branch_0_fun/ppermute | solution.py:622
  39.7 0.0 copy-done.6
  39.7 0.0 copy-done.12
  39.7 0.0 copy-done.18
  39.8 0.0 copy-done.24
  39.8 12.0 %own.6 = (f32[32,128,128]{2,1,0:T(8,128)S(1)}, bf16[32,128,128]{2,1,0:T(8,128)(2,1)S(1)}, f32[32,128,128]{2,1,0:T(8,128)}, s32[288]{0:T(512)S(1)}, s32[288]{0:T(512)S(1)}) custom-call(s32[128]{0:T(128)S(1)} %get-tuple-element.98.table, s32[32]{0:T(128)S(1)} %copy-done.18, f32[32]{0:T(128)S(1)} %copy-done.24, s32[8,32]{1,0:T(8,128)S(1)} %copy-done.12, ...), custom_call_target="tpu_custom_call" | custom-call | flops 1073741824 | bytes 8388608 | tf_op jit(solution)/shard_map/cond/branch_0_fun/own/pallas_call | solution.py:272
  51.8 0.0 collective-permute-done.2.maps
  51.8 1.7 %serve.13 = bf16[8,512,128]{2,1,0:T(8,128)(2,1)S(1)} custom-call(s32[128]{0:T(128)S(1)} %get-tuple-element.98.table, bf16[16,512,512]{2,1,0:T(8,128)(2,1)S(1)} %bitcast.6, bf16[8,512,128]{2,1,0:T(8,128)(2,1)S(1)} %collective-permute-done.2.maps), custom_call_target="tpu_custom_call" | custom-call | flops 536870912 | bytes 6291456 | tf_op jit(solution)/shard_map/cond/branch_0_fun/serve/pallas_call | solution.py:312
  53.5 1.9 %collective-permute-start.3 = (bf16[8,512,128]{2,1,0:T(8,128)(2,1)S(1)}, bf16[8,512,128]{2,1,0:T(8,128)(2,1)S(1)}, u32[]{:S(2)}, u32[]{:S(2)}) collective-permute-start(bf16[8,512,128]{2,1,0:T(8,128)(2,1)S(1)} %serve.13), channel_id=1, source_target_pairs={{1,2},{2,1},{3,4},{4,3},{5,6},{6,5},{7,8},{8,7},{9,10},{10,9},{11,... | collective-permute-start | bytes 3145736 | tf_op jit(solution)/shard_map/cond/branch_0_fun/ppermute | solution.py:622
  55.4 0.0 collective-permute-done.4.blocks
  55.4 7.1 %beside.6 = (f32[32,128,128]{2,1,0:T(8,128)S(1)}, bf16[32,128,128]{2,1,0:T(8,128)(2,1)S(1)}) custom-call(s32[128]{0:T(128)S(1)} %get-tuple-element.98.table, bf16[16,512,512]{2,1,0:T(8,128)(2,1)S(1)} %collective-permute-done.4.blocks, bf16[32,512,128]{2,1,0:T(8,128)(2,1)S(1)} %copy-done, bf16[32,128,512]{2,1,0:T(8,128)(2,1)S(1)} %left.6.refs_2_, ...), custom_call_target="tpu_custom_call" | custom-call | flops 1073741824 | bytes 4194304 | tf_op jit(solution)/shard_map/cond/branch_0_fun/beside/pallas_call | solution.py:379
  62.6 11.3 %collective-permute-done.3.refs_1_ = bf16[8,512,128]{2,1,0:T(8,128)(2,1)S(1)} collective-permute-done((bf16[8,512,128]{2,1,0:T(8,128)(2,1)S(1)}, bf16[8,512,128]{2,1,0:T(8,128)(2,1)S(1)}, u32[]{:S(2)}, u32[]{:S(2)}) %collective-permute-start.3) | collective-permute-done | bytes 1048608 | tf_op jit(solution)/shard_map/cond/branch_0_fun/ppermute | solution.py:622
  73.8 0.0 collective-permute-done.1.refs_0_
  73.8 3.6 %across.6 = (f32[32,128,128]{2,1,0:T(8,128)S(1)}, bf16[32,128,128]{2,1,0:T(8,128)(2,1)S(1)}) custom-call(s32[128]{0:T(128)S(1)} %get-tuple-element.98.table, bf16[9,512,128]{2,1,0:T(8,128)(2,1)S(1)} %collective-permute-done.1.refs_0_, bf16[8,512,128]{2,1,0:T(8,128)(2,1)S(1)} %collective-permute-done.3.refs_1_, bf16[32,128,512]{2,1,0:T(8,128)(2,1)S(1)} %left.6.refs_2_, ...), custom_call_target="tpu_custom_call" | custom-call | flops 1073741824 | bytes 4194304 | tf_op jit(solution)/shard_map/cond/branch_0_fun/across/pallas_call | solution.py:379
  77.7 0.1 collective-permute-start.30
  77.8 1.9 %collective-permute-start.31 = (bf16[32,128,128]{2,1,0:T(8,128)(2,1)S(1)}, bf16[32,128,128]{2,1,0:T(8,128)(2,1)S(1)}, u32[]{:S(2)}, u32[]{:S(2)}) collective-permute-start(bf16[32,128,128]{2,1,0:T(8,128)(2,1)S(1)} %get-tuple-element.235.here), channel_id=1, source_target_pairs={{1,2},{2,1},{3,4},{4,3},{5,6},{6,5},{7,8},{8,7},{9,10},{10,9},{11,... | collective-permute-start | bytes 3145736 | tf_op jit(solution)/shard_map/ppermute | solution.py:622
  79.7 0.7 collective-permute-done.30.near_by
  80.4 9.0 %opening.1 = (f32[32,128,128]{2,1,0:T(8,128)S(1)}, bf16[256,128,128]{2,1,0:T(8,128)(2,1)S(1)}, f32[32,128,128]{2,1,0:T(8,128)S(1)}, f32[32,128,128]{2,1,0:T(8,128)S(1)}) custom-call(s32[288]{0:T(512)S(1)} %get-tuple-element.234.listed, bf16[256,128,128]{2,1,0:T(8,128)(2,1)} %bitcast.17, bf16[32,128,128]{2,1,0:T(8,128)(2,1)S(1)} %get-tuple-element.235.here, ...), custom_call_target="tpu_custom_call" | custom-call | flops 1073741824 | bytes 8388608 | tf_op jit(solution)/shard_map/opening/pallas_call | solution.py:534
  89.4 8.7 %collective-permute-done.31.other = bf16[32,128,128]{2,1,0:T(8,128)(2,1)S(1)} collective-permute-done((bf16[32,128,128]{2,1,0:T(8,128)(2,1)S(1)}, bf16[32,128,128]{2,1,0:T(8,128)(2,1)S(1)}, u32[]{:S(2)}, u32[]{:S(2)}) %collective-permute-start.31) | collective-permute-done | bytes 1048608 | tf_op jit(solution)/shard_map/ppermute | solution.py:622
  98.1 5.5 %late.1.here = bf16[32,128,128]{2,1,0:T(8,128)(2,1)S(1)} custom-call(s32[288]{0:T(512)S(1)} %get-tuple-element.233.listed, bf16[256,128,128]{2,1,0:T(8,128)(2,1)S(1)} %get-tuple-element.238.inter, bf16[32,128,128]{2,1,0:T(8,128)(2,1)S(1)} %collective-permute-done.31.other, f32[32,128,128]{2,1,0:T(8,128)S(1)} %get-tuple-element.239.so_far, ...), custom_call_target="tpu_custom_call" | custom-call | flops 536870912 | bytes 8388608 | tf_op jit(solution)/shard_map/late/pallas_call | solution.py:565
  103.6 0.1 collective-permute-start.33
  103.7 1.9 %collective-permute-start.32 = (bf16[32,128,128]{2,1,0:T(8,128)(2,1)S(1)}, bf16[32,128,128]{2,1,0:T(8,128)(2,1)S(1)}, u32[]{:S(2)}, u32[]{:S(2)}) collective-permute-start(bf16[32,128,128]{2,1,0:T(8,128)(2,1)S(1)} %late.1.here), channel_id=1, source_target_pairs={{1,2},{2,1},{3,4},{4,3},{5,6},{6,5},{7,8},{8,7},{9,10},{10,9},{11,... | collective-permute-start | bytes 3145736 | tf_op jit(solution)/shard_map/ppermute | solution.py:622
  105.7 0.7 collective-permute-done.33.near_by
  106.4 7.8 %early.1.so_far = f32[32,128,128]{2,1,0:T(8,128)S(1)} custom-call(s32[288]{0:T(512)S(1)} %get-tuple-element.234.listed, bf16[256,128,128]{2,1,0:T(8,128)(2,1)S(1)} %get-tuple-element.238.inter, bf16[32,128,128]{2,1,0:T(8,128)(2,1)S(1)} %late.1.here, bf16[32,128,128]{2,1,0:T(8,128)(2,1)S(1)} %collective-permute-done.33.near_by, ...), custom_call_target="tpu_custom_call" | custom-call | flops 1073741824 | bytes 8388608 | tf_op jit(solution)/shard_map/early/pallas_call | solution.py:550
  114.2 9.9 %collective-permute-done.32.other = bf16[32,128,128]{2,1,0:T(8,128)(2,1)S(1)} collective-permute-done((bf16[32,128,128]{2,1,0:T(8,128)(2,1)S(1)}, bf16[32,128,128]{2,1,0:T(8,128)(2,1)S(1)}, u32[]{:S(2)}, u32[]{:S(2)}) %collective-permute-start.32) | collective-permute-done | bytes 1048608 | tf_op jit(solution)/shard_map/ppermute | solution.py:622
  124.1 7.3 %last.1 = (f32[32,128,128]{2,1,0:T(8,128)}, f32[1,32]{1,0:T(1,128)}) custom-call(s32[288]{0:T(512)S(1)} %get-tuple-element.233.listed, bf16[256,128,128]{2,1,0:T(8,128)(2,1)S(1)} %get-tuple-element.238.inter, bf16[32,128,128]{2,1,0:T(8,128)(2,1)S(1)} %collective-permute-done.32.other, f32[32,128,128]{2,1,0:T(8,128)S(1)} %early.1.so_far, ...), custom_call_target="tpu_custom_call" | custom-call | flops 536870912 | bytes 8388608 | tf_op jit(solution)/shard_map/last/pallas_call | solution.py:580
  (1 shorter events, 0.0 us)
Async XLA Ops:
  3.5 52.0 %collective-permute-start.4 = (bf16[16,512,512]{2,1,0:T(8,128)(2,1)}, bf16[16,512,512]{2,1,0:T(8,128)(2,1)S(1)}, u32[]{:S(2)}, u32[]{:S(2)}) collective-permute-start(bf16[16,512,512]{2,1,0:T(8,128)(2,1)} %get-tuple-element.85.blocks), channel_id=1, source_target_pairs={{0,1},{1,0},{2,3},{3,2},{4,5},{5,4},{6,7},{7,6},{8,9},{9,8},{10,11... | collective-permute-start | bytes 25165832 | tf_op jit(solution)/shard_map/cond/branch_0_fun/ppermute | solution.py:621
  3.6 13.6 %copy-start = (bf16[32,512,128]{2,1,0:T(8,128)(2,1)S(1)}, bf16[32,512,128]{2,1,0:T(8,128)(2,1)}, u32[]{:S(2)}) copy-start(bf16[32,512,128]{2,1,0:T(8,128)(2,1)} %get-tuple-element.86.maps) | copy-start | bytes 12582916 | tf_op jit(solution)/shard_map/cond
  3.6 25.3 %slice-start = ((s8[8388608]{0:T(1024)(128)(4,1)}), s8[4194304]{0:T(1024)(128)(4,1)S(1)}, s32[]{:S(2)}) async-start(s8[8388608]{0:T(1024)(128)(4,1)} %bitcast.5), calls=%async_computation | async-start | bytes 8388608 | tf_op jit(solution)/shard_map/cond
  6.3 22.5 %collective-permute-start = (bf16[9,512,128]{2,1,0:T(8,128)(2,1)S(1)}, bf16[9,512,128]{2,1,0:T(8,128)(2,1)S(1)}, u32[]{:S(2)}, u32[]{:S(2)}) collective-permute-start(bf16[9,512,128]{2,1,0:T(8,128)(2,1)S(1)} %get-tuple-element.88), channel_id=1, source_target_pairs={{1,2},{2,1},{3,4},{4,3},{5,6},{6,5},{7,8},{8,7},{9,10},{10,9},{11,... | collective-permute-start | bytes 3538952 | tf_op jit(solution)/shard_map/cond/branch_0_fun/ppermute | solution.py:622
  14.9 13.9 %slice-start.1 = ((s8[8388608]{0:T(1024)(128)(4,1)}), s8[4194304]{0:T(1024)(128)(4,1)S(1)}, s32[]{:S(2)}) async-start(s8[8388608]{0:T(1024)(128)(4,1)} %bitcast.5), calls=%async_computation.1 | async-start | bytes 8388608 | tf_op jit(solution)/shard_map/cond
  15.0 36.8 %collective-permute-start.2 = (bf16[8,512,128]{2,1,0:T(8,128)(2,1)S(1)}, bf16[8,512,128]{2,1,0:T(8,128)(2,1)S(1)}, u32[]{:S(2)}, u32[]{:S(2)}) collective-permute-start(bf16[8,512,128]{2,1,0:T(8,128)(2,1)S(1)} %get-tuple-element.96), channel_id=1, source_target_pairs={{1,2},{2,1},{3,4},{4,3},{5,6},{6,5},{7,8},{8,7},{9,10},{10,9},{11,... | collective-permute-start | bytes 3145736 | tf_op jit(solution)/shard_map/cond/branch_0_fun/ppermute | solution.py:622
  28.2 11.5 %copy-start.6 = (f32[32,128]{1,0:T(8,128)S(1)}, f32[32,128]{1,0:T(8,128)}, u32[]{:S(2)}) copy-start(f32[32,128]{1,0:T(8,128)} %get-tuple-element.93.energy) | copy-start | bytes 49156 | tf_op jit(solution)/shard_map/cond
  28.3 11.5 %copy-start.12 = (s32[8,32]{1,0:T(8,128)S(1)}, s32[8,32]{1,0:T(8,128)}, u32[]{:S(2)}) copy-start(s32[8,32]{1,0:T(8,128)} %get-tuple-element.92.near_pairs) | copy-start | bytes 3076 | tf_op jit(solution)/shard_map/cond
  28.3 11.5 %copy-start.18 = (s32[32]{0:T(128)S(1)}, s32[32]{0:T(128)}, u32[]{:S(2)}) copy-start(s32[32]{0:T(128)} %get-tuple-element.90.sizes) | copy-start | bytes 388 | tf_op jit(solution)/shard_map/cond
  28.3 11.5 %copy-start.24 = (f32[32]{0:T(128)S(1)}, f32[32]{0:T(128)}, u32[]{:S(2)}) copy-start(f32[32]{0:T(128)} %get-tuple-element.91.shift) | copy-start | bytes 388 | tf_op jit(solution)/shard_map/cond
  31.9 42.0 %collective-permute-start.1 = (bf16[9,512,128]{2,1,0:T(8,128)(2,1)S(1)}, bf16[9,512,128]{2,1,0:T(8,128)(2,1)S(1)}, u32[]{:S(2)}, u32[]{:S(2)}) collective-permute-start(bf16[9,512,128]{2,1,0:T(8,128)(2,1)S(1)} %serve.12), channel_id=1, source_target_pairs={{1,2},{2,1},{3,4},{4,3},{5,6},{6,5},{7,8},{8,7},{9,10},{10,9},{11,... | collective-permute-start | bytes 3538952 | tf_op jit(solution)/shard_map/cond/branch_0_fun/ppermute | solution.py:622
  53.5 20.3 %collective-permute-start.3 = (bf16[8,512,128]{2,1,0:T(8,128)(2,1)S(1)}, bf16[8,512,128]{2,1,0:T(8,128)(2,1)S(1)}, u32[]{:S(2)}, u32[]{:S(2)}) collective-permute-start(bf16[8,512,128]{2,1,0:T(8,128)(2,1)S(1)} %serve.13), channel_id=1, source_target_pairs={{1,2},{2,1},{3,4},{4,3},{5,6},{6,5},{7,8},{8,7},{9,10},{10,9},{11,... | collective-permute-start | bytes 3145736 | tf_op jit(solution)/shard_map/cond/branch_0_fun/ppermute | solution.py:622
  77.7 2.7 %collective-permute-start.30 = (bf16[32,128,128]{2,1,0:T(8,128)(2,1)S(1)}, bf16[32,128,128]{2,1,0:T(8,128)(2,1)S(1)}, u32[]{:S(2)}, u32[]{:S(2)}) collective-permute-start(bf16[32,128,128]{2,1,0:T(8,128)(2,1)S(1)} %get-tuple-element.235.here), channel_id=1, source_target_pairs={{0,1},{1,0},{2,3},{3,2},{4,5},{5,4},{6,7},{7,6},{8,9},{9,8},{10,11... | collective-permute-start | bytes 3145736 | tf_op jit(solution)/shard_map/ppermute | solution.py:621
  77.8 20.3 %collective-permute-start.31 = (bf16[32,128,128]{2,1,0:T(8,128)(2,1)S(1)}, bf16[32,128,128]{2,1,0:T(8,128)(2,1)S(1)}, u32[]{:S(2)}, u32[]{:S(2)}) collective-permute-start(bf16[32,128,128]{2,1,0:T(8,128)(2,1)S(1)} %get-tuple-element.235.here), channel_id=1, source_target_pairs={{1,2},{2,1},{3,4},{4,3},{5,6},{6,5},{7,8},{8,7},{9,10},{10,9},{11,... | collective-permute-start | bytes 3145736 | tf_op jit(solution)/shard_map/ppermute | solution.py:622
  103.6 2.7 %collective-permute-start.33 = (bf16[32,128,128]{2,1,0:T(8,128)(2,1)S(1)}, bf16[32,128,128]{2,1,0:T(8,128)(2,1)S(1)}, u32[]{:S(2)}, u32[]{:S(2)}) collective-permute-start(bf16[32,128,128]{2,1,0:T(8,128)(2,1)S(1)} %late.1.here), channel_id=1, source_target_pairs={{0,1},{1,0},{2,3},{3,2},{4,5},{5,4},{6,7},{7,6},{8,9},{9,8},{10,11... | collective-permute-start | bytes 3145736 | tf_op jit(solution)/shard_map/ppermute | solution.py:621
  103.7 20.3 %collective-permute-start.32 = (bf16[32,128,128]{2,1,0:T(8,128)(2,1)S(1)}, bf16[32,128,128]{2,1,0:T(8,128)(2,1)S(1)}, u32[]{:S(2)}, u32[]{:S(2)}) collective-permute-start(bf16[32,128,128]{2,1,0:T(8,128)(2,1)S(1)} %late.1.here), channel_id=1, source_target_pairs={{1,2},{2,1},{3,4},{4,3},{5,6},{6,5},{7,8},{8,7},{9,10},{10,9},{11,... | collective-permute-start | bytes 3145736 | tf_op jit(solution)/shard_map/ppermute | solution.py:622

commit v7 on v6

--- a/solution.py
+++ b/solution.py
@@ -211,9 +211,8 @@
     )(table, blocks, maps)
 
 
-def own_body(scale, orbitals, table, sizes, shift, near_pairs, blocks, maps, energy, left,
-             integ, start, inverse, early, late, slots):
-    count, width, _ = left.shape
+def prepare_body(table, sizes, shift, near_pairs, energy, inverse, early, late):
+    count, width, _ = inverse.shape
     near = near_pairs.shape[0]
     device = lax.axis_index("pairs")
     side = 2 * (device % 2) - 1
@@ -250,6 +249,29 @@
         early[1 + soon + k] = count * 65536 + 2 * count
         late[1 + after + k] = count * 65536 + count
 
+
+def prepare(table, sizes, shift, near_pairs, energy):
+    count, width = energy.shape
+    entries = near_pairs.size + 6 * UNIT + 8
+    return call(
+        prepare_body,
+        (
+            jax.ShapeDtypeStruct((count, width, width), jnp.float32),
+            jax.ShapeDtypeStruct((entries,), jnp.int32),
+            jax.ShapeDtypeStruct((entries,), jnp.int32),
+        ),
+        (VMEM, SMEM, SMEM),
+        [SMEM, SMEM, SMEM, SMEM, VMEM],
+        [],
+        flops=count * width * width * 10,
+        moved=count * width * width * 4,
+        limit=8,
+        name="prepare",
+    )(table, sizes, shift, near_pairs, energy)
+
+
+def own_body(scale, orbitals, table, blocks, maps, left, inverse, integ, start, slots):
+    count = left.shape[0]
     found = collect(count, lambda p: table[SRC + p] < orbitals, slots)
 
     def work(slot):
@@ -265,27 +287,23 @@
     by_twos(found, work, store)
 
 
-def own_part(table, sizes, shift, near_pairs, blocks, maps, energy, left, scale):
+def own_part(table, blocks, maps, left, inverse, scale):
     orbitals = blocks.shape[0]
     count, width, depth = left.shape
-    entries = near_pairs.size + 6 * UNIT + 8
     return call(
         functools.partial(own_body, scale, orbitals),
         (
             jax.ShapeDtypeStruct((count, width, width), jnp.float32),
             jax.ShapeDtypeStruct((count, width, width), jnp.bfloat16),
-            jax.ShapeDtypeStruct((count, width, width), jnp.float32),
-            jax.ShapeDtypeStruct((entries,), jnp.int32),
-            jax.ShapeDtypeStruct((entries,), jnp.int32),
         ),
-        (VMEM, VMEM, VMEM, SMEM, SMEM),
-        [SMEM, SMEM, SMEM, SMEM, VMEM, VMEM, VMEM, VMEM],
+        (VMEM, VMEM),
+        [SMEM, VMEM, VMEM, VMEM, VMEM],
         [pltpu.SMEM((count + 1,), jnp.int32)],
         flops=count * depth * depth * width,
         moved=blocks.size * 2,
-        limit=28,
+        limit=24,
         name="own",
-    )(table, sizes, shift, near_pairs, blocks, maps, energy, left)
+    )(table, blocks, maps, left, inverse)
 
 
 def serve_body(low, table, blocks, maps, out, slots):
@@ -352,25 +370,24 @@
 
 
 def across_body(scale, orbitals, table, *refs):
-    n = len(refs) - 8
+    n = len(refs) - 7
     halves = refs[:n]
-    left, inverse, integ_in, start_in, integ, start, joined, slots = refs[n:]
+    left, inverse, integ_in, start_in, integ, start, slots = refs[n:]
     carry_over(integ_in, start_in, integ, start)
+    found = collect(left.shape[0], lambda p: table[SRC + p] >= 2 * orbitals, slots)
     low = 0
     for half in halves:
-        joined[pl.ds(low, half.shape[0])] = half[...]
+
+        def work(slot, half=half, low=low):
+            return dot(left[slots[low + slot]], half[slot]) * scale
+
+        def store(slot, value, low=low):
+            pair = slots[low + slot]
+            integ[pair] = value
+            start[pair] = (value * inverse[pair]).astype(jnp.bfloat16)
+
+        by_twos(jnp.clip(found - low, 0, half.shape[0]), work, store)
         low += half.shape[0]
-    found = collect(left.shape[0], lambda p: table[SRC + p] >= 2 * orbitals, slots)
-
-    def work(slot):
-        return dot(left[slots[slot]], joined[slot]) * scale
-
-    def store(slot, value):
-        pair = slots[slot]
-        integ[pair] = value
-        start[pair] = (value * inverse[pair]).astype(jnp.bfloat16)
-
-    by_twos(found, work, store)
 
 
 def integrals_part(body, table, operands, left, inverse, integ, start, scratch, limit, name):
@@ -635,14 +652,13 @@
             left = left_part(table, blocks, maps)
             half_one = serve(after(table, left), blocks, got[0], 0, count)
             back_one = swap_across(half_one)
-            integ, start, inverse, early, late = own_part(
-                after(table, half_one), sizes, shift, near_pairs, blocks, maps, energy, left, scale
-            )
+            inverse, early, late = prepare(after(table, half_one), sizes, shift, near_pairs, energy)
             half_two = serve(after(table, early), blocks, got[1], got[0].shape[0], count)
             back_two = swap_across(half_two)
+            integ, start = own_part(after(table, half_two), blocks, maps, left, inverse, scale)
             integ, start = integrals_part(
                 functools.partial(beside_body, scale),
-                after(table, half_two),
+                after(table, start),
                 (blocks_beside, maps),
                 left,
                 inverse,
@@ -660,7 +676,7 @@
                 inverse,
                 integ,
                 start,
-                [pltpu.VMEM((slots, depth, width), jnp.bfloat16)],
+                [],
                 24,
                 "across",
             )

time: 133 us -> 127 us (0.955)
  the two profiles are of different devices: /device:TPU:2 before, /device:TPU:6 now
where the time goes in v7:
time: 127 us
  Pallas kernels  76.2 us (60%)
  starting transfers between devices  31.6 us (25%)
  waiting for transfers between devices  17.1 us (13%)
  between operations  1.53 us (1%)
    ppermute x6, starting transfers between devices, shards(): swap_across = lambda x: lax.ppermute(x, 'pairs', across_perm)  31.5 us
    ppermute x6, waiting for transfers between devices, shards(): swap_across = lambda x: lax.ppermute(x, 'pairs', across_perm)  17.1 us
    pallas_call x1, Pallas kernels, left_part(): call(left_body, jax.ShapeDtypeStruct((count, width, depth), jnp.bfloat16)...  11.1 us
    pallas_call x2, Pallas kernels, integrals_part(): call(body, (jax.ShapeDtypeStruct(integ.shape, integ.dtype), jax.ShapeDtyp...  10.1 us
    pallas_call x1, Pallas kernels, opening_part(): call(opening_body, tuple((jax.ShapeDtypeStruct(x.shape, x.dtype) for x in...  9.65 us
    pallas_call x1, Pallas kernels, own_part(): call(functools.partial(own_body, scale, orbitals), (jax.ShapeDtypeStruct(...  8.82 us
    pallas_call x1, Pallas kernels, early_part(): call(early_body, jax.ShapeDtypeStruct(integ.shape, jnp.float32), VMEM, [S...  8.33 us
    pallas_call x1, Pallas kernels, last_part(): call(last_body, (jax.ShapeDtypeStruct(so_far.shape, jnp.float32), jax.Sha...  7.31 us
  transfers between devices with their start and end apart: 9, of which 4 were waited for; matrix products, arithmetic and copies ran while one was open for 0% of the time, Pallas kernels for 44%

profile of v7, /device:TPU:6, one launch (start us, length us, event | category | flops | bytes accessed | tf_op | source)
XLA Modules:
  0.0 126.7 jit_solution(836853683337136986)
XLA Ops:
  0.6 2.2 %plan.1 = (s32[128]{0:T(128)S(1)}, s32[1]{0:T(128)}) custom-call(s32[2,4096]{1,0:T(2,128)} %bitcast.24, s32[2048]{0:T(1024)} %sizes_hbm.1), custom_call_target="tpu_custom_call" | custom-call | bytes 65536 | tf_op jit(solution)/shard_map/plan/pallas_call | solution.py:127
  3.4 69.4 %conditional.1 = (f32[32,128,128]{2,1,0:T(8,128)}, bf16[32,128,128]{2,1,0:T(8,128)(2,1)S(1)}, f32[32,128,128]{2,1,0:T(8,128)}, s32[288]{0:T(512)S(1)}, s32[288]{0:T(512)S(1)}) conditional(s32[]{:T(128)} %bitcast.1, (s32[128]{0:T(128)S(1)}, bf16[16,512,512]{2,1,0:T(8,128)(2,1)}, bf16[32,512,128]{2,1,0:T(8,128)(2,1)}, ...), branch_computations={%region_0.0_spmd, %region_1.0_spmd, %region_2.0_spmd, %region_3.0_... | conditional | flops 7521435648 | bytes 169940416 | solution.py:687
  3.5 0.1 collective-permute-start.4
  3.6 0.0 copy-start
  3.6 0.0 slice-start
  3.6 2.7 %pack.6 = (bf16[9,512,128]{2,1,0:T(8,128)(2,1)S(1)}, bf16[8,512,128]{2,1,0:T(8,128)(2,1)S(1)}) custom-call(s32[128]{0:T(128)S(1)} %get-tuple-element.100.table, bf16[32,512,128]{2,1,0:T(8,128)(2,1)} %get-tuple-element.86.maps), custom_call_target="tpu_custom_call" | custom-call | bytes 4456448 | tf_op jit(solution)/shard_map/cond/branch_0_fun/pack/pallas_call | solution.py:172
  6.3 8.9 %collective-permute-start = (bf16[9,512,128]{2,1,0:T(8,128)(2,1)S(1)}, bf16[9,512,128]{2,1,0:T(8,128)(2,1)S(1)}, u32[]{:S(2)}, u32[]{:S(2)}) collective-permute-start(bf16[9,512,128]{2,1,0:T(8,128)(2,1)S(1)} %get-tuple-element.88), channel_id=1, source_target_pairs={{1,2},{2,1},{3,4},{4,3},{5,6},{6,5},{7,8},{8,7},{9,10},{10,9},{11,... | collective-permute-start | bytes 3538952 | tf_op jit(solution)/shard_map/cond/branch_0_fun/ppermute | solution.py:639
  15.2 0.0 slice-start.1
  15.2 2.2 %collective-permute-start.2 = (bf16[8,512,128]{2,1,0:T(8,128)(2,1)S(1)}, bf16[8,512,128]{2,1,0:T(8,128)(2,1)S(1)}, u32[]{:S(2)}, u32[]{:S(2)}) collective-permute-start(bf16[8,512,128]{2,1,0:T(8,128)(2,1)S(1)} %get-tuple-element.96), channel_id=1, source_target_pairs={{1,2},{2,1},{3,4},{4,3},{5,6},{6,5},{7,8},{8,7},{9,10},{10,9},{11,... | collective-permute-start | bytes 3145736 | tf_op jit(solution)/shard_map/cond/branch_0_fun/ppermute | solution.py:639
  17.4 0.0 copy-done
  17.5 11.1 %left.6.refs_2_ = bf16[32,128,512]{2,1,0:T(8,128)(2,1)S(1)} custom-call(s32[128]{0:T(128)S(1)} %get-tuple-element.100.table, bf16[16,512,512]{2,1,0:T(8,128)(2,1)} %get-tuple-element.85.blocks, bf16[32,512,128]{2,1,0:T(8,128)(2,1)S(1)} %copy-done), custom_call_target="tpu_custom_call" | custom-call | flops 2147483648 | bytes 8388608 | tf_op jit(solution)/shard_map/cond/branch_0_fun/left/pallas_call | solution.py:201
  28.5 0.0 copy-start.6
  28.5 0.0 copy-start.12
  28.6 0.0 copy-start.18
  28.6 0.0 copy-start.24
  28.6 0.5 collective-permute-done.maps
  29.1 0.0 slice-done
  29.1 0.0 slice-done.1
  29.1 3.0 %serve.12 = bf16[9,512,128]{2,1,0:T(8,128)(2,1)S(1)} custom-call(s32[128]{0:T(128)S(1)} %get-tuple-element.100.table, bf16[16,512,512]{2,1,0:T(8,128)(2,1)S(1)} %bitcast.6, bf16[9,512,128]{2,1,0:T(8,128)(2,1)S(1)} %collective-permute-done.maps), custom_call_target="tpu_custom_call" | custom-call | flops 603979776 | bytes 7077888 | tf_op jit(solution)/shard_map/cond/branch_0_fun/serve/pallas_call | solution.py:330
  32.1 7.9 %collective-permute-start.1 = (bf16[9,512,128]{2,1,0:T(8,128)(2,1)S(1)}, bf16[9,512,128]{2,1,0:T(8,128)(2,1)S(1)}, u32[]{:S(2)}, u32[]{:S(2)}) collective-permute-start(bf16[9,512,128]{2,1,0:T(8,128)(2,1)S(1)} %serve.12), channel_id=1, source_target_pairs={{1,2},{2,1},{3,4},{4,3},{5,6},{6,5},{7,8},{8,7},{9,10},{10,9},{11,... | collective-permute-start | bytes 3538952 | tf_op jit(solution)/shard_map/cond/branch_0_fun/ppermute | solution.py:639
  40.0 0.0 copy-done.6
  40.0 0.0 copy-done.12
  40.0 0.0 copy-done.18
  40.0 0.0 copy-done.24
  40.1 5.8 %prepare.6 = (f32[32,128,128]{2,1,0:T(8,128)}, s32[288]{0:T(512)S(1)}, s32[288]{0:T(512)S(1)}) custom-call(s32[128]{0:T(128)S(1)} %get-tuple-element.100.table, s32[32]{0:T(128)S(1)} %copy-done.18, f32[32]{0:T(128)S(1)} %copy-done.24, s32[8,32]{1,0:T(8,128)S(1)} %copy-done.12, f32[32,128]{1,0:T(8,128)S(1)} %copy-done.6), custom_call_target="tpu_custom_call" | custom-call | flops 5242880 | bytes 2097152 | tf_op jit(solution)/shard_map/cond/branch_0_fun/prepare/pallas_call | solution.py:256
  45.8 0.0 collective-permute-done.2.maps
  45.9 1.7 %serve.13 = bf16[8,512,128]{2,1,0:T(8,128)(2,1)S(1)} custom-call(s32[128]{0:T(128)S(1)} %get-tuple-element.100.table, bf16[16,512,512]{2,1,0:T(8,128)(2,1)S(1)} %bitcast.6, bf16[8,512,128]{2,1,0:T(8,128)(2,1)S(1)} %collective-permute-done.2.maps), custom_call_target="tpu_custom_call" | custom-call | flops 536870912 | bytes 6291456 | tf_op jit(solution)/shard_map/cond/branch_0_fun/serve/pallas_call | solution.py:330
  47.6 2.3 %collective-permute-start.3 = (bf16[8,512,128]{2,1,0:T(8,128)(2,1)S(1)}, bf16[8,512,128]{2,1,0:T(8,128)(2,1)S(1)}, u32[]{:S(2)}, u32[]{:S(2)}) collective-permute-start(bf16[8,512,128]{2,1,0:T(8,128)(2,1)S(1)} %serve.13), channel_id=1, source_target_pairs={{1,2},{2,1},{3,4},{4,3},{5,6},{6,5},{7,8},{8,7},{9,10},{10,9},{11,... | collective-permute-start | bytes 3145736 | tf_op jit(solution)/shard_map/cond/branch_0_fun/ppermute | solution.py:639
  49.9 8.8 %own.6 = (f32[32,128,128]{2,1,0:T(8,128)S(1)}, bf16[32,128,128]{2,1,0:T(8,128)(2,1)S(1)}) custom-call(s32[128]{0:T(128)S(1)} %get-tuple-element.100.table, bf16[16,512,512]{2,1,0:T(8,128)(2,1)S(1)} %bitcast.6, bf16[32,512,128]{2,1,0:T(8,128)(2,1)S(1)} %copy-done, bf16[32,128,512]{2,1,0:T(8,128)(2,1)S(1)} %left.6.refs_2_, ...), custom_call_target="tpu_custom_call" | custom-call | flops 1073741824 | bytes 8388608 | tf_op jit(solution)/shard_map/cond/branch_0_fun/own/pallas_call | solution.py:293
  58.7 0.0 collective-permute-done.4.blocks
  58.7 5.1 %beside.6 = (f32[32,128,128]{2,1,0:T(8,128)S(1)}, bf16[32,128,128]{2,1,0:T(8,128)(2,1)S(1)}) custom-call(s32[128]{0:T(128)S(1)} %get-tuple-element.100.table, bf16[16,512,512]{2,1,0:T(8,128)(2,1)S(1)} %collective-permute-done.4.blocks, bf16[32,512,128]{2,1,0:T(8,128)(2,1)S(1)} %copy-done, bf16[32,128,512]{2,1,0:T(8,128)(2,1)S(1)} %left.6.refs_2_, ...), custom_call_target="tpu_custom_call" | custom-call | flops 1073741824 | bytes 4194304 | tf_op jit(solution)/shard_map/cond/branch_0_fun/beside/pallas_call | solution.py:396
  63.9 4.0 %collective-permute-done.3.refs_1_ = bf16[8,512,128]{2,1,0:T(8,128)(2,1)S(1)} collective-permute-done((bf16[8,512,128]{2,1,0:T(8,128)(2,1)S(1)}, bf16[8,512,128]{2,1,0:T(8,128)(2,1)S(1)}, u32[]{:S(2)}, u32[]{:S(2)}) %collective-permute-start.3) | collective-permute-done | bytes 1048608 | tf_op jit(solution)/shard_map/cond/branch_0_fun/ppermute | solution.py:639
  67.9 0.0 collective-permute-done.1.refs_0_
  67.9 5.0 %across.6 = (f32[32,128,128]{2,1,0:T(8,128)}, bf16[32,128,128]{2,1,0:T(8,128)(2,1)S(1)}) custom-call(s32[128]{0:T(128)S(1)} %get-tuple-element.100.table, bf16[9,512,128]{2,1,0:T(8,128)(2,1)S(1)} %collective-permute-done.1.refs_0_, bf16[8,512,128]{2,1,0:T(8,128)(2,1)S(1)} %collective-permute-done.3.refs_1_, bf16[32,128,512]{2,1,0:T(8,128)(2,1)S(1)} %left.6.refs_2_, ...), custom_call_target="tpu_custom_call" | custom-call | flops 1073741824 | bytes 4194304 | tf_op jit(solution)/shard_map/cond/branch_0_fun/across/pallas_call | solution.py:396
  72.9 0.0 collective-permute-start.30
  72.9 5.1 %collective-permute-start.31 = (bf16[32,128,128]{2,1,0:T(8,128)(2,1)S(1)}, bf16[32,128,128]{2,1,0:T(8,128)(2,1)S(1)}, u32[]{:S(2)}, u32[]{:S(2)}) collective-permute-start(bf16[32,128,128]{2,1,0:T(8,128)(2,1)S(1)} %get-tuple-element.241.here), channel_id=1, source_target_pairs={{1,2},{2,1},{3,4},{4,3},{5,6},{6,5},{7,8},{8,7},{9,10},{10,9},{11,... | collective-permute-start | bytes 3145736 | tf_op jit(solution)/shard_map/ppermute | solution.py:639
  78.0 0.0 collective-permute-done.30.near_by
  78.0 9.6 %opening.1 = (f32[32,128,128]{2,1,0:T(8,128)S(1)}, bf16[256,128,128]{2,1,0:T(8,128)(2,1)S(1)}, f32[32,128,128]{2,1,0:T(8,128)S(1)}, f32[32,128,128]{2,1,0:T(8,128)S(1)}) custom-call(s32[288]{0:T(512)S(1)} %get-tuple-element.240.listed, bf16[256,128,128]{2,1,0:T(8,128)(2,1)} %bitcast.17, bf16[32,128,128]{2,1,0:T(8,128)(2,1)S(1)} %get-tuple-element.241.here, ...), custom_call_target="tpu_custom_call" | custom-call | flops 1073741824 | bytes 8388608 | tf_op jit(solution)/shard_map/opening/pallas_call | solution.py:551
  87.6 5.6 %collective-permute-done.31.other = bf16[32,128,128]{2,1,0:T(8,128)(2,1)S(1)} collective-permute-done((bf16[32,128,128]{2,1,0:T(8,128)(2,1)S(1)}, bf16[32,128,128]{2,1,0:T(8,128)(2,1)S(1)}, u32[]{:S(2)}, u32[]{:S(2)}) %collective-permute-start.31) | collective-permute-done | bytes 1048608 | tf_op jit(solution)/shard_map/ppermute | solution.py:639
  93.2 5.6 %late.1.here = bf16[32,128,128]{2,1,0:T(8,128)(2,1)S(1)} custom-call(s32[288]{0:T(512)S(1)} %get-tuple-element.239.listed, bf16[256,128,128]{2,1,0:T(8,128)(2,1)S(1)} %get-tuple-element.244.inter, bf16[32,128,128]{2,1,0:T(8,128)(2,1)S(1)} %collective-permute-done.31.other, f32[32,128,128]{2,1,0:T(8,128)S(1)} %get-tuple-element.245.so_far, ...), custom_call_target="tpu_custom_call" | custom-call | flops 536870912 | bytes 8388608 | tf_op jit(solution)/shard_map/late/pallas_call | solution.py:582
  98.8 0.1 collective-permute-start.33
  98.9 5.1 %collective-permute-start.32 = (bf16[32,128,128]{2,1,0:T(8,128)(2,1)S(1)}, bf16[32,128,128]{2,1,0:T(8,128)(2,1)S(1)}, u32[]{:S(2)}, u32[]{:S(2)}) collective-permute-start(bf16[32,128,128]{2,1,0:T(8,128)(2,1)S(1)} %late.1.here), channel_id=1, source_target_pairs={{1,2},{2,1},{3,4},{4,3},{5,6},{6,5},{7,8},{8,7},{9,10},{10,9},{11,... | collective-permute-start | bytes 3145736 | tf_op jit(solution)/shard_map/ppermute | solution.py:639
  103.9 0.0 collective-permute-done.33.near_by
  103.9 8.3 %early.1.so_far = f32[32,128,128]{2,1,0:T(8,128)S(1)} custom-call(s32[288]{0:T(512)S(1)} %get-tuple-element.240.listed, bf16[256,128,128]{2,1,0:T(8,128)(2,1)S(1)} %get-tuple-element.244.inter, bf16[32,128,128]{2,1,0:T(8,128)(2,1)S(1)} %late.1.here, bf16[32,128,128]{2,1,0:T(8,128)(2,1)S(1)} %collective-permute-done.33.near_by, ...), custom_call_target="tpu_custom_call" | custom-call | flops 1073741824 | bytes 8388608 | tf_op jit(solution)/shard_map/early/pallas_call | solution.py:567
  112.3 6.9 %collective-permute-done.32.other = bf16[32,128,128]{2,1,0:T(8,128)(2,1)S(1)} collective-permute-done((bf16[32,128,128]{2,1,0:T(8,128)(2,1)S(1)}, bf16[32,128,128]{2,1,0:T(8,128)(2,1)S(1)}, u32[]{:S(2)}, u32[]{:S(2)}) %collective-permute-start.32) | collective-permute-done | bytes 1048608 | tf_op jit(solution)/shard_map/ppermute | solution.py:639
  119.2 7.3 %last.1 = (f32[32,128,128]{2,1,0:T(8,128)}, f32[1,32]{1,0:T(1,128)}) custom-call(s32[288]{0:T(512)S(1)} %get-tuple-element.239.listed, bf16[256,128,128]{2,1,0:T(8,128)(2,1)S(1)} %get-tuple-element.244.inter, bf16[32,128,128]{2,1,0:T(8,128)(2,1)S(1)} %collective-permute-done.32.other, f32[32,128,128]{2,1,0:T(8,128)S(1)} %early.1.so_far, ...), custom_call_target="tpu_custom_call" | custom-call | flops 536870912 | bytes 8388608 | tf_op jit(solution)/shard_map/last/pallas_call | solution.py:597
  (1 shorter events, 0.0 us)
Async XLA Ops:
  3.5 55.3 %collective-permute-start.4 = (bf16[16,512,512]{2,1,0:T(8,128)(2,1)}, bf16[16,512,512]{2,1,0:T(8,128)(2,1)S(1)}, u32[]{:S(2)}, u32[]{:S(2)}) collective-permute-start(bf16[16,512,512]{2,1,0:T(8,128)(2,1)} %get-tuple-element.85.blocks), channel_id=1, source_target_pairs={{0,1},{1,0},{2,3},{3,2},{4,5},{5,4},{6,7},{7,6},{8,9},{9,8},{10,11... | collective-permute-start | bytes 25165832 | tf_op jit(solution)/shard_map/cond/branch_0_fun/ppermute | solution.py:638
  3.6 13.9 %copy-start = (bf16[32,512,128]{2,1,0:T(8,128)(2,1)S(1)}, bf16[32,512,128]{2,1,0:T(8,128)(2,1)}, u32[]{:S(2)}) copy-start(bf16[32,512,128]{2,1,0:T(8,128)(2,1)} %get-tuple-element.86.maps) | copy-start | bytes 12582916 | tf_op jit(solution)/shard_map/cond
  3.6 25.5 %slice-start = ((s8[8388608]{0:T(1024)(128)(4,1)}), s8[4194304]{0:T(1024)(128)(4,1)S(1)}, s32[]{:S(2)}) async-start(s8[8388608]{0:T(1024)(128)(4,1)} %bitcast.5), calls=%async_computation | async-start | bytes 8388608 | tf_op jit(solution)/shard_map/cond
  6.3 22.8 %collective-permute-start = (bf16[9,512,128]{2,1,0:T(8,128)(2,1)S(1)}, bf16[9,512,128]{2,1,0:T(8,128)(2,1)S(1)}, u32[]{:S(2)}, u32[]{:S(2)}) collective-permute-start(bf16[9,512,128]{2,1,0:T(8,128)(2,1)S(1)} %get-tuple-element.88), channel_id=1, source_target_pairs={{1,2},{2,1},{3,4},{4,3},{5,6},{6,5},{7,8},{8,7},{9,10},{10,9},{11,... | collective-permute-start | bytes 3538952 | tf_op jit(solution)/shard_map/cond/branch_0_fun/ppermute | solution.py:639
  15.2 13.9 %slice-start.1 = ((s8[8388608]{0:T(1024)(128)(4,1)}), s8[4194304]{0:T(1024)(128)(4,1)S(1)}, s32[]{:S(2)}) async-start(s8[8388608]{0:T(1024)(128)(4,1)} %bitcast.5), calls=%async_computation.1 | async-start | bytes 8388608 | tf_op jit(solution)/shard_map/cond
  15.2 30.6 %collective-permute-start.2 = (bf16[8,512,128]{2,1,0:T(8,128)(2,1)S(1)}, bf16[8,512,128]{2,1,0:T(8,128)(2,1)S(1)}, u32[]{:S(2)}, u32[]{:S(2)}) collective-permute-start(bf16[8,512,128]{2,1,0:T(8,128)(2,1)S(1)} %get-tuple-element.96), channel_id=1, source_target_pairs={{1,2},{2,1},{3,4},{4,3},{5,6},{6,5},{7,8},{8,7},{9,10},{10,9},{11,... | collective-permute-start | bytes 3145736 | tf_op jit(solution)/shard_map/cond/branch_0_fun/ppermute | solution.py:639
  28.5 11.5 %copy-start.6 = (f32[32,128]{1,0:T(8,128)S(1)}, f32[32,128]{1,0:T(8,128)}, u32[]{:S(2)}) copy-start(f32[32,128]{1,0:T(8,128)} %get-tuple-element.93.energy) | copy-start | bytes 49156 | tf_op jit(solution)/shard_map/cond
  28.5 11.5 %copy-start.12 = (s32[8,32]{1,0:T(8,128)S(1)}, s32[8,32]{1,0:T(8,128)}, u32[]{:S(2)}) copy-start(s32[8,32]{1,0:T(8,128)} %get-tuple-element.92.near_pairs) | copy-start | bytes 3076 | tf_op jit(solution)/shard_map/cond
  28.6 11.5 %copy-start.18 = (s32[32]{0:T(128)S(1)}, s32[32]{0:T(128)}, u32[]{:S(2)}) copy-start(s32[32]{0:T(128)} %get-tuple-element.90.sizes) | copy-start | bytes 388 | tf_op jit(solution)/shard_map/cond
  28.6 11.5 %copy-start.24 = (f32[32]{0:T(128)S(1)}, f32[32]{0:T(128)}, u32[]{:S(2)}) copy-start(f32[32]{0:T(128)} %get-tuple-element.91.shift) | copy-start | bytes 388 | tf_op jit(solution)/shard_map/cond
  32.1 35.8 %collective-permute-start.1 = (bf16[9,512,128]{2,1,0:T(8,128)(2,1)S(1)}, bf16[9,512,128]{2,1,0:T(8,128)(2,1)S(1)}, u32[]{:S(2)}, u32[]{:S(2)}) collective-permute-start(bf16[9,512,128]{2,1,0:T(8,128)(2,1)S(1)} %serve.12), channel_id=1, source_target_pairs={{1,2},{2,1},{3,4},{4,3},{5,6},{6,5},{7,8},{8,7},{9,10},{10,9},{11,... | collective-permute-start | bytes 3538952 | tf_op jit(solution)/shard_map/cond/branch_0_fun/ppermute | solution.py:639
  47.6 20.3 %collective-permute-start.3 = (bf16[8,512,128]{2,1,0:T(8,128)(2,1)S(1)}, bf16[8,512,128]{2,1,0:T(8,128)(2,1)S(1)}, u32[]{:S(2)}, u32[]{:S(2)}) collective-permute-start(bf16[8,512,128]{2,1,0:T(8,128)(2,1)S(1)} %serve.13), channel_id=1, source_target_pairs={{1,2},{2,1},{3,4},{4,3},{5,6},{6,5},{7,8},{8,7},{9,10},{10,9},{11,... | collective-permute-start | bytes 3145736 | tf_op jit(solution)/shard_map/cond/branch_0_fun/ppermute | solution.py:639
  72.9 5.1 %collective-permute-start.30 = (bf16[32,128,128]{2,1,0:T(8,128)(2,1)S(1)}, bf16[32,128,128]{2,1,0:T(8,128)(2,1)S(1)}, u32[]{:S(2)}, u32[]{:S(2)}) collective-permute-start(bf16[32,128,128]{2,1,0:T(8,128)(2,1)S(1)} %get-tuple-element.241.here), channel_id=1, source_target_pairs={{0,1},{1,0},{2,3},{3,2},{4,5},{5,4},{6,7},{7,6},{8,9},{9,8},{10,11... | collective-permute-start | bytes 3145736 | tf_op jit(solution)/shard_map/ppermute | solution.py:638
  72.9 20.3 %collective-permute-start.31 = (bf16[32,128,128]{2,1,0:T(8,128)(2,1)S(1)}, bf16[32,128,128]{2,1,0:T(8,128)(2,1)S(1)}, u32[]{:S(2)}, u32[]{:S(2)}) collective-permute-start(bf16[32,128,128]{2,1,0:T(8,128)(2,1)S(1)} %get-tuple-element.241.here), channel_id=1, source_target_pairs={{1,2},{2,1},{3,4},{4,3},{5,6},{6,5},{7,8},{8,7},{9,10},{10,9},{11,... | collective-permute-start | bytes 3145736 | tf_op jit(solution)/shard_map/ppermute | solution.py:639
  98.8 5.2 %collective-permute-start.33 = (bf16[32,128,128]{2,1,0:T(8,128)(2,1)S(1)}, bf16[32,128,128]{2,1,0:T(8,128)(2,1)S(1)}, u32[]{:S(2)}, u32[]{:S(2)}) collective-permute-start(bf16[32,128,128]{2,1,0:T(8,128)(2,1)S(1)} %late.1.here), channel_id=1, source_target_pairs={{0,1},{1,0},{2,3},{3,2},{4,5},{5,4},{6,7},{7,6},{8,9},{9,8},{10,11... | collective-permute-start | bytes 3145736 | tf_op jit(solution)/shard_map/ppermute | solution.py:638
  98.9 20.3 %collective-permute-start.32 = (bf16[32,128,128]{2,1,0:T(8,128)(2,1)S(1)}, bf16[32,128,128]{2,1,0:T(8,128)(2,1)S(1)}, u32[]{:S(2)}, u32[]{:S(2)}) collective-permute-start(bf16[32,128,128]{2,1,0:T(8,128)(2,1)S(1)} %late.1.here), channel_id=1, source_target_pairs={{1,2},{2,1},{3,4},{4,3},{5,6},{6,5},{7,8},{8,7},{9,10},{10,9},{11,... | collective-permute-start | bytes 3145736 | tf_op jit(solution)/shard_map/ppermute | solution.py:639

commit v8 on v7

--- a/solution.py
+++ b/solution.py
@@ -370,24 +370,25 @@
 
 
 def across_body(scale, orbitals, table, *refs):
-    n = len(refs) - 7
+    n = len(refs) - 8
     halves = refs[:n]
-    left, inverse, integ_in, start_in, integ, start, slots = refs[n:]
+    left, inverse, integ_in, start_in, integ, start, joined, slots = refs[n:]
     carry_over(integ_in, start_in, integ, start)
-    found = collect(left.shape[0], lambda p: table[SRC + p] >= 2 * orbitals, slots)
     low = 0
     for half in halves:
-
-        def work(slot, half=half, low=low):
-            return dot(left[slots[low + slot]], half[slot]) * scale
-
-        def store(slot, value, low=low):
-            pair = slots[low + slot]
-            integ[pair] = value
-            start[pair] = (value * inverse[pair]).astype(jnp.bfloat16)
-
-        by_twos(jnp.clip(found - low, 0, half.shape[0]), work, store)
+        joined[pl.ds(low, half.shape[0])] = half[...]
         low += half.shape[0]
+    found = collect(left.shape[0], lambda p: table[SRC + p] >= 2 * orbitals, slots)
+
+    def work(slot):
+        return dot(left[slots[slot]], joined[slot]) * scale
+
+    def store(slot, value):
+        pair = slots[slot]
+        integ[pair] = value
+        start[pair] = (value * inverse[pair]).astype(jnp.bfloat16)
+
+    by_twos(found, work, store)
 
 
 def integrals_part(body, table, operands, left, inverse, integ, start, scratch, limit, name):
@@ -676,7 +677,7 @@
                 inverse,
                 integ,
                 start,
-                [],
+                [pltpu.VMEM((slots, depth, width), jnp.bfloat16)],
                 24,
                 "across",
             )

time: 127 us -> 128 us (level); the launches traced: 127 us -> 126 us
  waiting for transfers between devices: 17.1 us -> 14.5 us
  Pallas kernels: 76.2 us -> 78.2 us
    pallas_call x2, Pallas kernels: 10.1 us -> 13.5 us  [integrals_part(): call(body, (jax.ShapeDtypeStruct(integ.shape, integ.dtype), jax.ShapeDtyp...]
    ppermute x6, waiting for transfers between devices: 17.1 us -> 14.5 us  [shards(): swap_across = lambda x: lax.ppermute(x, 'pairs', across_perm)]
    pallas_call x1, Pallas kernels: 8.82 us -> 6.83 us  [own_part(): call(functools.partial(own_body, scale, orbitals), (jax.ShapeDtypeStruct(...]
  transfers between devices with their start and end apart: 9 -> 9, of which waited for: 4 -> 4; matrix products, arithmetic and copies ran while one was open for 0% -> 0% of each run, Pallas kernels for 44% -> 47%
where the time goes in v8:
time: 128 us; the launch traced here: 126 us
  Pallas kernels  78.2 us (61%)
  starting transfers between devices  31.6 us (25%)
  waiting for transfers between devices  14.5 us (11%)
  between operations  1.53 us (1%)
    ppermute x6, starting transfers between devices, shards(): swap_across = lambda x: lax.ppermute(x, 'pairs', across_perm)  31.5 us
    ppermute x6, waiting for transfers between devices, shards(): swap_across = lambda x: lax.ppermute(x, 'pairs', across_perm)  14.5 us
    pallas_call x2, Pallas kernels, integrals_part(): call(body, (jax.ShapeDtypeStruct(integ.shape, integ.dtype), jax.ShapeDtyp...  13.5 us
    pallas_call x1, Pallas kernels, left_part(): call(left_body, jax.ShapeDtypeStruct((count, width, depth), jnp.bfloat16)...  11.1 us
    pallas_call x1, Pallas kernels, opening_part(): call(opening_body, tuple((jax.ShapeDtypeStruct(x.shape, x.dtype) for x in...  9.61 us
    pallas_call x1, Pallas kernels, early_part(): call(early_body, jax.ShapeDtypeStruct(integ.shape, jnp.float32), VMEM, [S...  8.4 us
    pallas_call x1, Pallas kernels, last_part(): call(last_body, (jax.ShapeDtypeStruct(so_far.shape, jnp.float32), jax.Sha...  7.32 us
    pallas_call x1, Pallas kernels, own_part(): call(functools.partial(own_body, scale, orbitals), (jax.ShapeDtypeStruct(...  6.83 us
  transfers between devices with their start and end apart: 9, of which 4 were waited for; matrix products, arithmetic and copies ran while one was open for 0% of the time, Pallas kernels for 47%

profile of v8, /device:TPU:6, one launch (start us, length us, event | category | flops | bytes accessed | tf_op | source)
XLA Modules:
  0.0 126.1 jit_solution(6771115464266659124)
XLA Ops:
  0.6 2.2 %plan.1 = (s32[128]{0:T(128)S(1)}, s32[1]{0:T(128)}) custom-call(s32[2,4096]{1,0:T(2,128)} %bitcast.24, s32[2048]{0:T(1024)} %sizes_hbm.1), custom_call_target="tpu_custom_call" | custom-call | bytes 65536 | tf_op jit(solution)/shard_map/plan/pallas_call | solution.py:127
  3.4 68.9 %conditional.1 = (f32[32,128,128]{2,1,0:T(8,128)}, bf16[32,128,128]{2,1,0:T(8,128)(2,1)S(1)}, f32[32,128,128]{2,1,0:T(8,128)}, s32[288]{0:T(512)S(1)}, s32[288]{0:T(512)S(1)}) conditional(s32[]{:T(128)} %bitcast.1, (s32[128]{0:T(128)S(1)}, bf16[16,512,512]{2,1,0:T(8,128)(2,1)}, bf16[32,512,128]{2,1,0:T(8,128)(2,1)}, ...), branch_computations={%region_0.0_spmd, %region_1.0_spmd, %region_2.0_spmd, %region_3.0_... | conditional | flops 7521435648 | bytes 169940416 | solution.py:688
  3.5 0.1 collective-permute-start.4
  3.6 0.0 copy-start
  3.6 0.0 slice-start
  3.6 2.8 %pack.6 = (bf16[9,512,128]{2,1,0:T(8,128)(2,1)S(1)}, bf16[8,512,128]{2,1,0:T(8,128)(2,1)S(1)}) custom-call(s32[128]{0:T(128)S(1)} %get-tuple-element.100.table, bf16[32,512,128]{2,1,0:T(8,128)(2,1)} %get-tuple-element.86.maps), custom_call_target="tpu_custom_call" | custom-call | bytes 4456448 | tf_op jit(solution)/shard_map/cond/branch_0_fun/pack/pallas_call | solution.py:172
  6.4 8.9 %collective-permute-start = (bf16[9,512,128]{2,1,0:T(8,128)(2,1)S(1)}, bf16[9,512,128]{2,1,0:T(8,128)(2,1)S(1)}, u32[]{:S(2)}, u32[]{:S(2)}) collective-permute-start(bf16[9,512,128]{2,1,0:T(8,128)(2,1)S(1)} %get-tuple-element.88), channel_id=1, source_target_pairs={{1,2},{2,1},{3,4},{4,3},{5,6},{6,5},{7,8},{8,7},{9,10},{10,9},{11,... | collective-permute-start | bytes 3538952 | tf_op jit(solution)/shard_map/cond/branch_0_fun/ppermute | solution.py:640
  15.3 0.0 slice-start.1
  15.3 2.2 %collective-permute-start.2 = (bf16[8,512,128]{2,1,0:T(8,128)(2,1)S(1)}, bf16[8,512,128]{2,1,0:T(8,128)(2,1)S(1)}, u32[]{:S(2)}, u32[]{:S(2)}) collective-permute-start(bf16[8,512,128]{2,1,0:T(8,128)(2,1)S(1)} %get-tuple-element.96), channel_id=1, source_target_pairs={{1,2},{2,1},{3,4},{4,3},{5,6},{6,5},{7,8},{8,7},{9,10},{10,9},{11,... | collective-permute-start | bytes 3145736 | tf_op jit(solution)/shard_map/cond/branch_0_fun/ppermute | solution.py:640
  17.5 0.0 copy-done
  17.5 11.1 %left.6.refs_2_ = bf16[32,128,512]{2,1,0:T(8,128)(2,1)S(1)} custom-call(s32[128]{0:T(128)S(1)} %get-tuple-element.100.table, bf16[16,512,512]{2,1,0:T(8,128)(2,1)} %get-tuple-element.85.blocks, bf16[32,512,128]{2,1,0:T(8,128)(2,1)S(1)} %copy-done), custom_call_target="tpu_custom_call" | custom-call | flops 2147483648 | bytes 8388608 | tf_op jit(solution)/shard_map/cond/branch_0_fun/left/pallas_call | solution.py:201
  28.5 0.0 copy-start.6
  28.6 0.0 copy-start.12
  28.6 0.0 copy-start.18
  28.6 0.0 copy-start.24
  28.6 0.5 collective-permute-done.maps
  29.1 0.0 slice-done
  29.1 0.0 slice-done.1
  29.1 3.0 %serve.12 = bf16[9,512,128]{2,1,0:T(8,128)(2,1)S(1)} custom-call(s32[128]{0:T(128)S(1)} %get-tuple-element.100.table, bf16[16,512,512]{2,1,0:T(8,128)(2,1)S(1)} %bitcast.6, bf16[9,512,128]{2,1,0:T(8,128)(2,1)S(1)} %collective-permute-done.maps), custom_call_target="tpu_custom_call" | custom-call | flops 603979776 | bytes 7077888 | tf_op jit(solution)/shard_map/cond/branch_0_fun/serve/pallas_call | solution.py:330
  32.2 7.4 %collective-permute-start.1 = (bf16[9,512,128]{2,1,0:T(8,128)(2,1)S(1)}, bf16[9,512,128]{2,1,0:T(8,128)(2,1)S(1)}, u32[]{:S(2)}, u32[]{:S(2)}) collective-permute-start(bf16[9,512,128]{2,1,0:T(8,128)(2,1)S(1)} %serve.12), channel_id=1, source_target_pairs={{1,2},{2,1},{3,4},{4,3},{5,6},{6,5},{7,8},{8,7},{9,10},{10,9},{11,... | collective-permute-start | bytes 3538952 | tf_op jit(solution)/shard_map/cond/branch_0_fun/ppermute | solution.py:640
  39.6 0.0 copy-done.6
  39.6 0.0 copy-done.12
  39.6 0.0 copy-done.18
  39.6 0.0 copy-done.24
  39.6 5.8 %prepare.6 = (f32[32,128,128]{2,1,0:T(8,128)}, s32[288]{0:T(512)S(1)}, s32[288]{0:T(512)S(1)}) custom-call(s32[128]{0:T(128)S(1)} %get-tuple-element.100.table, s32[32]{0:T(128)S(1)} %copy-done.18, f32[32]{0:T(128)S(1)} %copy-done.24, s32[8,32]{1,0:T(8,128)S(1)} %copy-done.12, f32[32,128]{1,0:T(8,128)S(1)} %copy-done.6), custom_call_target="tpu_custom_call" | custom-call | flops 5242880 | bytes 2097152 | tf_op jit(solution)/shard_map/cond/branch_0_fun/prepare/pallas_call | solution.py:256
  45.4 0.0 collective-permute-done.2.maps
  45.4 2.1 %serve.13 = bf16[8,512,128]{2,1,0:T(8,128)(2,1)S(1)} custom-call(s32[128]{0:T(128)S(1)} %get-tuple-element.100.table, bf16[16,512,512]{2,1,0:T(8,128)(2,1)S(1)} %bitcast.6, bf16[8,512,128]{2,1,0:T(8,128)(2,1)S(1)} %collective-permute-done.2.maps), custom_call_target="tpu_custom_call" | custom-call | flops 536870912 | bytes 6291456 | tf_op jit(solution)/shard_map/cond/branch_0_fun/serve/pallas_call | solution.py:330
  47.6 1.9 %collective-permute-start.3 = (bf16[8,512,128]{2,1,0:T(8,128)(2,1)S(1)}, bf16[8,512,128]{2,1,0:T(8,128)(2,1)S(1)}, u32[]{:S(2)}, u32[]{:S(2)}) collective-permute-start(bf16[8,512,128]{2,1,0:T(8,128)(2,1)S(1)} %serve.13), channel_id=1, source_target_pairs={{1,2},{2,1},{3,4},{4,3},{5,6},{6,5},{7,8},{8,7},{9,10},{10,9},{11,... | collective-permute-start | bytes 3145736 | tf_op jit(solution)/shard_map/cond/branch_0_fun/ppermute | solution.py:640
  49.5 6.8 %own.6 = (f32[32,128,128]{2,1,0:T(8,128)S(1)}, bf16[32,128,128]{2,1,0:T(8,128)(2,1)S(1)}) custom-call(s32[128]{0:T(128)S(1)} %get-tuple-element.100.table, bf16[16,512,512]{2,1,0:T(8,128)(2,1)S(1)} %bitcast.6, bf16[32,512,128]{2,1,0:T(8,128)(2,1)S(1)} %copy-done, bf16[32,128,512]{2,1,0:T(8,128)(2,1)S(1)} %left.6.refs_2_, ...), custom_call_target="tpu_custom_call" | custom-call | flops 1073741824 | bytes 8388608 | tf_op jit(solution)/shard_map/cond/branch_0_fun/own/pallas_call | solution.py:293
  56.3 0.0 collective-permute-done.4.blocks
  56.4 9.1 %beside.6 = (f32[32,128,128]{2,1,0:T(8,128)S(1)}, bf16[32,128,128]{2,1,0:T(8,128)(2,1)S(1)}) custom-call(s32[128]{0:T(128)S(1)} %get-tuple-element.100.table, bf16[16,512,512]{2,1,0:T(8,128)(2,1)S(1)} %collective-permute-done.4.blocks, bf16[32,512,128]{2,1,0:T(8,128)(2,1)S(1)} %copy-done, bf16[32,128,512]{2,1,0:T(8,128)(2,1)S(1)} %left.6.refs_2_, ...), custom_call_target="tpu_custom_call" | custom-call | flops 1073741824 | bytes 4194304 | tf_op jit(solution)/shard_map/cond/branch_0_fun/beside/pallas_call | solution.py:397
  65.5 2.4 %collective-permute-done.3.refs_1_ = bf16[8,512,128]{2,1,0:T(8,128)(2,1)S(1)} collective-permute-done((bf16[8,512,128]{2,1,0:T(8,128)(2,1)S(1)}, bf16[8,512,128]{2,1,0:T(8,128)(2,1)S(1)}, u32[]{:S(2)}, u32[]{:S(2)}) %collective-permute-start.3) | collective-permute-done | bytes 1048608 | tf_op jit(solution)/shard_map/cond/branch_0_fun/ppermute | solution.py:640
  67.9 0.0 collective-permute-done.1.refs_0_
  67.9 4.4 %across.6 = (f32[32,128,128]{2,1,0:T(8,128)}, bf16[32,128,128]{2,1,0:T(8,128)(2,1)S(1)}) custom-call(s32[128]{0:T(128)S(1)} %get-tuple-element.100.table, bf16[9,512,128]{2,1,0:T(8,128)(2,1)S(1)} %collective-permute-done.1.refs_0_, bf16[8,512,128]{2,1,0:T(8,128)(2,1)S(1)} %collective-permute-done.3.refs_1_, bf16[32,128,512]{2,1,0:T(8,128)(2,1)S(1)} %left.6.refs_2_, ...), custom_call_target="tpu_custom_call" | custom-call | flops 1073741824 | bytes 4194304 | tf_op jit(solution)/shard_map/cond/branch_0_fun/across/pallas_call | solution.py:397
  72.4 0.0 collective-permute-start.30
  72.4 5.5 %collective-permute-start.31 = (bf16[32,128,128]{2,1,0:T(8,128)(2,1)S(1)}, bf16[32,128,128]{2,1,0:T(8,128)(2,1)S(1)}, u32[]{:S(2)}, u32[]{:S(2)}) collective-permute-start(bf16[32,128,128]{2,1,0:T(8,128)(2,1)S(1)} %get-tuple-element.241.here), channel_id=1, source_target_pairs={{1,2},{2,1},{3,4},{4,3},{5,6},{6,5},{7,8},{8,7},{9,10},{10,9},{11,... | collective-permute-start | bytes 3145736 | tf_op jit(solution)/shard_map/ppermute | solution.py:640
  77.9 0.0 collective-permute-done.30.near_by
  77.9 9.6 %opening.1 = (f32[32,128,128]{2,1,0:T(8,128)S(1)}, bf16[256,128,128]{2,1,0:T(8,128)(2,1)S(1)}, f32[32,128,128]{2,1,0:T(8,128)S(1)}, f32[32,128,128]{2,1,0:T(8,128)S(1)}) custom-call(s32[288]{0:T(512)S(1)} %get-tuple-element.240.listed, bf16[256,128,128]{2,1,0:T(8,128)(2,1)} %bitcast.17, bf16[32,128,128]{2,1,0:T(8,128)(2,1)S(1)} %get-tuple-element.241.here, ...), custom_call_target="tpu_custom_call" | custom-call | flops 1073741824 | bytes 8388608 | tf_op jit(solution)/shard_map/opening/pallas_call | solution.py:552
  87.5 5.2 %collective-permute-done.31.other = bf16[32,128,128]{2,1,0:T(8,128)(2,1)S(1)} collective-permute-done((bf16[32,128,128]{2,1,0:T(8,128)(2,1)S(1)}, bf16[32,128,128]{2,1,0:T(8,128)(2,1)S(1)}, u32[]{:S(2)}, u32[]{:S(2)}) %collective-permute-start.31) | collective-permute-done | bytes 1048608 | tf_op jit(solution)/shard_map/ppermute | solution.py:640
  92.7 5.5 %late.1.here = bf16[32,128,128]{2,1,0:T(8,128)(2,1)S(1)} custom-call(s32[288]{0:T(512)S(1)} %get-tuple-element.239.listed, bf16[256,128,128]{2,1,0:T(8,128)(2,1)S(1)} %get-tuple-element.244.inter, bf16[32,128,128]{2,1,0:T(8,128)(2,1)S(1)} %collective-permute-done.31.other, f32[32,128,128]{2,1,0:T(8,128)S(1)} %get-tuple-element.245.so_far, ...), custom_call_target="tpu_custom_call" | custom-call | flops 536870912 | bytes 8388608 | tf_op jit(solution)/shard_map/late/pallas_call | solution.py:583
  98.2 0.1 collective-permute-start.33
  98.3 5.5 %collective-permute-start.32 = (bf16[32,128,128]{2,1,0:T(8,128)(2,1)S(1)}, bf16[32,128,128]{2,1,0:T(8,128)(2,1)S(1)}, u32[]{:S(2)}, u32[]{:S(2)}) collective-permute-start(bf16[32,128,128]{2,1,0:T(8,128)(2,1)S(1)} %late.1.here), channel_id=1, source_target_pairs={{1,2},{2,1},{3,4},{4,3},{5,6},{6,5},{7,8},{8,7},{9,10},{10,9},{11,... | collective-permute-start | bytes 3145736 | tf_op jit(solution)/shard_map/ppermute | solution.py:640
  103.9 0.0 collective-permute-done.33.near_by
  103.9 8.4 %early.1.so_far = f32[32,128,128]{2,1,0:T(8,128)S(1)} custom-call(s32[288]{0:T(512)S(1)} %get-tuple-element.240.listed, bf16[256,128,128]{2,1,0:T(8,128)(2,1)S(1)} %get-tuple-element.244.inter, bf16[32,128,128]{2,1,0:T(8,128)(2,1)S(1)} %late.1.here, bf16[32,128,128]{2,1,0:T(8,128)(2,1)S(1)} %collective-permute-done.33.near_by, ...), custom_call_target="tpu_custom_call" | custom-call | flops 1073741824 | bytes 8388608 | tf_op jit(solution)/shard_map/early/pallas_call | solution.py:568
  112.3 6.4 %collective-permute-done.32.other = bf16[32,128,128]{2,1,0:T(8,128)(2,1)S(1)} collective-permute-done((bf16[32,128,128]{2,1,0:T(8,128)(2,1)S(1)}, bf16[32,128,128]{2,1,0:T(8,128)(2,1)S(1)}, u32[]{:S(2)}, u32[]{:S(2)}) %collective-permute-start.32) | collective-permute-done | bytes 1048608 | tf_op jit(solution)/shard_map/ppermute | solution.py:640
  118.6 7.3 %last.1 = (f32[32,128,128]{2,1,0:T(8,128)}, f32[1,32]{1,0:T(1,128)}) custom-call(s32[288]{0:T(512)S(1)} %get-tuple-element.239.listed, bf16[256,128,128]{2,1,0:T(8,128)(2,1)S(1)} %get-tuple-element.244.inter, bf16[32,128,128]{2,1,0:T(8,128)(2,1)S(1)} %collective-permute-done.32.other, f32[32,128,128]{2,1,0:T(8,128)S(1)} %early.1.so_far, ...), custom_call_target="tpu_custom_call" | custom-call | flops 536870912 | bytes 8388608 | tf_op jit(solution)/shard_map/last/pallas_call | solution.py:598
  (1 shorter events, 0.0 us)
Async XLA Ops:
  3.5 52.9 %collective-permute-start.4 = (bf16[16,512,512]{2,1,0:T(8,128)(2,1)}, bf16[16,512,512]{2,1,0:T(8,128)(2,1)S(1)}, u32[]{:S(2)}, u32[]{:S(2)}) collective-permute-start(bf16[16,512,512]{2,1,0:T(8,128)(2,1)} %get-tuple-element.85.blocks), channel_id=1, source_target_pairs={{0,1},{1,0},{2,3},{3,2},{4,5},{5,4},{6,7},{7,6},{8,9},{9,8},{10,11... | collective-permute-start | bytes 25165832 | tf_op jit(solution)/shard_map/cond/branch_0_fun/ppermute | solution.py:639
  3.6 13.9 %copy-start = (bf16[32,512,128]{2,1,0:T(8,128)(2,1)S(1)}, bf16[32,512,128]{2,1,0:T(8,128)(2,1)}, u32[]{:S(2)}) copy-start(bf16[32,512,128]{2,1,0:T(8,128)(2,1)} %get-tuple-element.86.maps) | copy-start | bytes 12582916 | tf_op jit(solution)/shard_map/cond
  3.6 25.6 %slice-start = ((s8[8388608]{0:T(1024)(128)(4,1)}), s8[4194304]{0:T(1024)(128)(4,1)S(1)}, s32[]{:S(2)}) async-start(s8[8388608]{0:T(1024)(128)(4,1)} %bitcast.5), calls=%async_computation | async-start | bytes 8388608 | tf_op jit(solution)/shard_map/cond
  6.4 22.8 %collective-permute-start = (bf16[9,512,128]{2,1,0:T(8,128)(2,1)S(1)}, bf16[9,512,128]{2,1,0:T(8,128)(2,1)S(1)}, u32[]{:S(2)}, u32[]{:S(2)}) collective-permute-start(bf16[9,512,128]{2,1,0:T(8,128)(2,1)S(1)} %get-tuple-element.88), channel_id=1, source_target_pairs={{1,2},{2,1},{3,4},{4,3},{5,6},{6,5},{7,8},{8,7},{9,10},{10,9},{11,... | collective-permute-start | bytes 3538952 | tf_op jit(solution)/shard_map/cond/branch_0_fun/ppermute | solution.py:640
  15.3 13.9 %slice-start.1 = ((s8[8388608]{0:T(1024)(128)(4,1)}), s8[4194304]{0:T(1024)(128)(4,1)S(1)}, s32[]{:S(2)}) async-start(s8[8388608]{0:T(1024)(128)(4,1)} %bitcast.5), calls=%async_computation.1 | async-start | bytes 8388608 | tf_op jit(solution)/shard_map/cond
  15.3 30.2 %collective-permute-start.2 = (bf16[8,512,128]{2,1,0:T(8,128)(2,1)S(1)}, bf16[8,512,128]{2,1,0:T(8,128)(2,1)S(1)}, u32[]{:S(2)}, u32[]{:S(2)}) collective-permute-start(bf16[8,512,128]{2,1,0:T(8,128)(2,1)S(1)} %get-tuple-element.96), channel_id=1, source_target_pairs={{1,2},{2,1},{3,4},{4,3},{5,6},{6,5},{7,8},{8,7},{9,10},{10,9},{11,... | collective-permute-start | bytes 3145736 | tf_op jit(solution)/shard_map/cond/branch_0_fun/ppermute | solution.py:640
  28.5 11.0 %copy-start.6 = (f32[32,128]{1,0:T(8,128)S(1)}, f32[32,128]{1,0:T(8,128)}, u32[]{:S(2)}) copy-start(f32[32,128]{1,0:T(8,128)} %get-tuple-element.93.energy) | copy-start | bytes 49156 | tf_op jit(solution)/shard_map/cond
  28.6 11.0 %copy-start.12 = (s32[8,32]{1,0:T(8,128)S(1)}, s32[8,32]{1,0:T(8,128)}, u32[]{:S(2)}) copy-start(s32[8,32]{1,0:T(8,128)} %get-tuple-element.92.near_pairs) | copy-start | bytes 3076 | tf_op jit(solution)/shard_map/cond
  28.6 11.0 %copy-start.18 = (s32[32]{0:T(128)S(1)}, s32[32]{0:T(128)}, u32[]{:S(2)}) copy-start(s32[32]{0:T(128)} %get-tuple-element.90.sizes) | copy-start | bytes 388 | tf_op jit(solution)/shard_map/cond
  28.6 11.0 %copy-start.24 = (f32[32]{0:T(128)S(1)}, f32[32]{0:T(128)}, u32[]{:S(2)}) copy-start(f32[32]{0:T(128)} %get-tuple-element.91.shift) | copy-start | bytes 388 | tf_op jit(solution)/shard_map/cond
  32.2 35.8 %collective-permute-start.1 = (bf16[9,512,128]{2,1,0:T(8,128)(2,1)S(1)}, bf16[9,512,128]{2,1,0:T(8,128)(2,1)S(1)}, u32[]{:S(2)}, u32[]{:S(2)}) collective-permute-start(bf16[9,512,128]{2,1,0:T(8,128)(2,1)S(1)} %serve.12), channel_id=1, source_target_pairs={{1,2},{2,1},{3,4},{4,3},{5,6},{6,5},{7,8},{8,7},{9,10},{10,9},{11,... | collective-permute-start | bytes 3538952 | tf_op jit(solution)/shard_map/cond/branch_0_fun/ppermute | solution.py:640
  47.6 20.3 %collective-permute-start.3 = (bf16[8,512,128]{2,1,0:T(8,128)(2,1)S(1)}, bf16[8,512,128]{2,1,0:T(8,128)(2,1)S(1)}, u32[]{:S(2)}, u32[]{:S(2)}) collective-permute-start(bf16[8,512,128]{2,1,0:T(8,128)(2,1)S(1)} %serve.13), channel_id=1, source_target_pairs={{1,2},{2,1},{3,4},{4,3},{5,6},{6,5},{7,8},{8,7},{9,10},{10,9},{11,... | collective-permute-start | bytes 3145736 | tf_op jit(solution)/shard_map/cond/branch_0_fun/ppermute | solution.py:640
  72.4 5.5 %collective-permute-start.30 = (bf16[32,128,128]{2,1,0:T(8,128)(2,1)S(1)}, bf16[32,128,128]{2,1,0:T(8,128)(2,1)S(1)}, u32[]{:S(2)}, u32[]{:S(2)}) collective-permute-start(bf16[32,128,128]{2,1,0:T(8,128)(2,1)S(1)} %get-tuple-element.241.here), channel_id=1, source_target_pairs={{0,1},{1,0},{2,3},{3,2},{4,5},{5,4},{6,7},{7,6},{8,9},{9,8},{10,11... | collective-permute-start | bytes 3145736 | tf_op jit(solution)/shard_map/ppermute | solution.py:639
  72.4 20.3 %collective-permute-start.31 = (bf16[32,128,128]{2,1,0:T(8,128)(2,1)S(1)}, bf16[32,128,128]{2,1,0:T(8,128)(2,1)S(1)}, u32[]{:S(2)}, u32[]{:S(2)}) collective-permute-start(bf16[32,128,128]{2,1,0:T(8,128)(2,1)S(1)} %get-tuple-element.241.here), channel_id=1, source_target_pairs={{1,2},{2,1},{3,4},{4,3},{5,6},{6,5},{7,8},{8,7},{9,10},{10,9},{11,... | collective-permute-start | bytes 3145736 | tf_op jit(solution)/shard_map/ppermute | solution.py:640
  98.2 5.6 %collective-permute-start.33 = (bf16[32,128,128]{2,1,0:T(8,128)(2,1)S(1)}, bf16[32,128,128]{2,1,0:T(8,128)(2,1)S(1)}, u32[]{:S(2)}, u32[]{:S(2)}) collective-permute-start(bf16[32,128,128]{2,1,0:T(8,128)(2,1)S(1)} %late.1.here), channel_id=1, source_target_pairs={{0,1},{1,0},{2,3},{3,2},{4,5},{5,4},{6,7},{7,6},{8,9},{9,8},{10,11... | collective-permute-start | bytes 3145736 | tf_op jit(solution)/shard_map/ppermute | solution.py:639
  98.3 20.3 %collective-permute-start.32 = (bf16[32,128,128]{2,1,0:T(8,128)(2,1)S(1)}, bf16[32,128,128]{2,1,0:T(8,128)(2,1)S(1)}, u32[]{:S(2)}, u32[]{:S(2)}) collective-permute-start(bf16[32,128,128]{2,1,0:T(8,128)(2,1)S(1)} %late.1.here), channel_id=1, source_target_pairs={{1,2},{2,1},{3,4},{4,3},{5,6},{6,5},{7,8},{8,7},{9,10},{10,9},{11,... | collective-permute-start | bytes 3145736 | tf_op jit(solution)/shard_map/ppermute | solution.py:640
